TPU v7x, 256 devices: a whole 4x4x8 slice. The times are simulated.
256 devices in a mesh: col: 32 (over z, x), bin: 8 (over y, core).
Axes of the slice: x: 4, y: 4, z: 8, core: 2. Of those that a mesh axis runs over, the one named last changes fastest.
Arguments:
- slope: float32 [262144], P('bin'), may hold values from -6 to 6
- curvature: float32 [262144], P('bin'), may hold values from -6 to 0
- target_mean: float32 [262144], P('bin'), may hold values from 0.15 to 0.85
- target_var: float32 [262144], P('bin'), may hold values from 0.06 to 0.12
- table: float32 [64, 512], P(None, 'col'), may hold values from -6 to 6
Outputs:
- species_mean: float32 [64, 262144], P('col')
- final_slope: float32 [262144], replicated
All inputs are finite; a program needn't handle non-finite values.
Results may differ from a plain program's by a relative error of at most 0.0001.
Values sent between devices are 32-bit elements; how exact they have to be, the bound alone decides.
No kernel may reach another device: no remote copies, remote signals or barrier semaphores. Data moves between devices by JAX's collectives and lax.ppermute only.
A program may use at most 64 MiB of HBM per device.

v0:
```python
import jax
import jax.numpy as jnp
from jax import lax
from jax.sharding import PartitionSpec as P

ITERS = 3


def in_order(blocks, dim):
    blocks = jnp.moveaxis(blocks, 0, dim)
    shape = blocks.shape
    return blocks.reshape(*shape[:dim], shape[dim] * shape[dim + 1], *shape[dim + 2 :])


def copy_for_each(array, axis):
    copies = jnp.broadcast_to(array, (lax.axis_size(axis), *array.shape))
    return lax.all_to_all(copies, axis, split_axis=0, concat_axis=0, tiled=True)


def gather_directly(array, axis, dim):
    return in_order(copy_for_each(array, axis), dim)


def exponent(lam, curvature, points):
    return jnp.exp(lam[None, :] * points + curvature[None, :] * points * points)


def per_device(slope, curvature, target_mean, target_var, table):
    columns = lax.axis_size("col")
    width = slope.shape[0] // columns
    offset = lax.axis_index("col") * width
    own_slope = lax.dynamic_slice_in_dim(slope, offset, width, 0)
    own_curve = lax.dynamic_slice_in_dim(curvature, offset, width, 0)
    own_mean = lax.dynamic_slice_in_dim(target_mean, offset, width, 0)
    own_var = lax.dynamic_slice_in_dim(target_var, offset, width, 0)
    full_table = gather_directly(table, "col", 1)
    total_pts = full_table.shape[1]
    points = ((lax.iota(jnp.int32, total_pts).astype(jnp.float32) + 0.5) / total_pts)[:, None]
    own_lam = own_slope
    for step in range(ITERS):
        expo = exponent(own_lam, own_curve, points)
        partition = jnp.sum(expo, axis=0)
        moment = jnp.sum(points * expo, axis=0)
        own_lam = own_lam + (own_mean - moment / partition) / own_var
    expo = exponent(own_lam, own_curve, points)
    weights = expo / jnp.sum(expo, axis=0)[None, :]
    terms = jnp.dot(
        full_table, weights, precision=lax.Precision.HIGHEST, preferred_element_type=jnp.float32
    )
    species = lax.all_to_all(terms, "col", split_axis=0, concat_axis=1, tiled=True)
    lam = gather_directly(own_lam, "col", 0)
    species_mean, final_slope = (
        lax.all_gather(species, "bin", axis=1, tiled=True),
        lax.all_gather(lam, "bin", axis=0, tiled=True),
    )
    return (species_mean, final_slope)


def solution(mesh):
    placed = (P("bin"), P("bin"), P("bin"), P("bin"), P(None, "col"))
    return jax.shard_map(
        per_device, mesh=mesh, in_specs=placed, out_specs=(P("col", None), P()), check_vma=False
    )
```

profile of v0, /device:TPU:1, one launch (start us, length us, event | category | flops | bytes accessed | tf_op | source)
XLA Modules:
  0.0 104.1 jit_solution(18431287290563344208)
XLA Ops:
  7.2 0.0 copy-start
  7.2 0.0 all-gather.5.cloned.1.call-start
  7.2 0.7 dynamic_slice.14
  7.9 0.7 dynamic_slice.12
  8.6 0.7 fusion.4
  9.3 0.7 divide_add_fusion.2
  10.1 0.7 fusion
  10.8 0.7 divide_add_fusion.1
  11.5 0.7 fusion.1
  12.2 0.7 divide_add_fusion
  12.9 0.1 broadcast_in_dim.5
  13.0 21.1 %all_to_all.30 = f32[32,1,1024]{2,1,0:T(1,128)} all-to-all(f32[32,1,1024]{2,1,0:T(1,128)S(1)} %broadcast_in_dim.5), channel_id=1, replica_groups=mesh['col'=32,'bin'=8] {'col'}, dimensions={0} | all-to-all | bytes 262144 | tf_op jit(solution)/shard_map/all_to_all | solution.py:17
  34.1 0.0 all-gather.5.cloned.1.call-update
  34.1 0.0 copy-done
  34.2 0.8 reshape.32
  35.0 3.9 %all-to-all-start = ((f32[32,1,1024]{2,1,0:T(1,128)}), f32[32,1,1024]{2,1,0:T(1,128)S(1)}, u32[]{:S(2)}, u32[]{:S(2)}) async-start(f32[32,1,1024]{2,1,0:T(1,128)} %reshape.32), calls=%async_computation | async-start | bytes 262144 | tf_op jit(solution)/shard_map/all_to_all | solution.py:17
  38.9 0.0 all-gather.3.cloned.1.call-start
  38.9 0.6 fusion.3
  39.5 8.8 %all-to-all-done = f32[32,1,1024]{2,1,0:T(1,128)S(1)} async-done(((f32[32,1,1024]{2,1,0:T(1,128)}), f32[32,1,1024]{2,1,0:T(1,128)S(1)}, u32[]{:S(2)}, u32[]{:S(2)}) %all-to-all-start) | async-done | bytes 131104 | tf_op jit(solution)/shard_map/all_to_all | solution.py:17
  48.3 0.5 broadcast.18
  48.8 1.0 reduce
  49.8 0.1 reshape.33
  49.9 2.0 %fusion.7 = f32[64,1024]{1,0:T(8,128)S(1)} fusion(f32[64,512]{0,1:T(8,128)S(1)} %bitcast.15, f32[1024]{0:T(1024)S(1)} %fusion.3, f32[1024]{0:T(1024)S(1)} %divide_add_fusion, f32[1024]{0:T(1024)S(1)} %dynamic_slice.14, f32[512]{0:T(512)S(1)} %add_multiply_fusion), kind=kOutput, calls=%fused_computation.14 | convolution fusion | flops 405274624 | bytes 407552 | tf_op jit(solution)/shard_map/dot_general | solution.py:47
  51.9 0.1 all_to_all.22
  52.0 14.2 %all_to_all.31 = f32[32,2,1024]{2,1,0:T(2,128)} all-to-all(f32[32,2,1024]{2,1,0:T(2,128)S(1)} %all_to_all.22), channel_id=1, replica_groups=mesh['col'=32,'bin'=8] {'col'}, dimensions={0} | all-to-all | bytes 524288 | tf_op jit(solution)/shard_map/all_to_all | solution.py:50
  66.3 0.0 all-gather.3.cloned.1.call-update
  66.3 0.0 all-gather.5.cloned.1.call-done
  66.3 0.0 copy-start.1
  66.3 27.3 %all-gather.3.cloned.1.call-done = f32[2,262144]{1,0:T(2,128)} async-done(((f32[2,32768]{1,0:T(2,128)}), f32[2,262144]{1,0:T(2,128)}) %all-gather.3.cloned.1.call-update) | async-done | bytes 2097168 | tf_op jit(solution)/shard_map/all_gather | solution.py:53
  93.6 2.6 %copy.14 = f32[2,262144]{1,0:T(2,128)} copy(f32[2,262144]{1,0:T(2,128)} %all-gather.3.cloned.1.call-done) | data formatting | bytes 4194304
  96.2 0.0 copy-done.1
  96.2 1.0 copy.15
  (2 shorter events, 0.0 us)
Async XLA Ops:
  7.2 27.0 %copy-start = (f32[64,16]{0,1:T(8,128)S(1)}, f32[64,16]{0,1:T(8,128)}, u32[]{:S(2)}) copy-start(f32[64,16]{0,1:T(8,128)} %param.9) | copy-start | bytes 12292
  7.2 59.1 %all-gather.5.cloned.1.call-start = ((), (), s32[]{:S(2)}) async-start(), calls=%async_computation.4 | async-start | bytes 1179648 | tf_op jit(solution)/shard_map/all_gather | solution.py:54
  35.0 13.3 %all-to-all-start = ((f32[32,1,1024]{2,1,0:T(1,128)}), f32[32,1,1024]{2,1,0:T(1,128)S(1)}, u32[]{:S(2)}, u32[]{:S(2)}) async-start(f32[32,1,1024]{2,1,0:T(1,128)} %reshape.32), calls=%async_computation | async-start | bytes 262144 | tf_op jit(solution)/shard_map/all_to_all | solution.py:17
  38.9 54.7 %all-gather.3.cloned.1.call-start = ((), (), s32[]{:S(2)}) async-start(), calls=%async_computation.3 | async-start | bytes 2359296 | tf_op jit(solution)/shard_map/all_gather | solution.py:53
  66.3 29.9 %copy-start.1 = (f32[262144]{0:T(1024)S(1)}, f32[262144]{0:T(1024)}, u32[]{:S(2)}) copy-start(f32[262144]{0:T(1024)} %all-gather.5.cloned.1.call-done) | copy-start | bytes 3145732
Sparse Core Ops, SparseCore 0:
  34.3 22.9 all-gather.4
  66.4 27.1 all-gather.2
where the time goes:
time: 105 us; the launch traced here: 104 us
  waiting for transfers between devices  36.1 us (34%)
  blocking collectives  35.4 us (34%)
  between operations  14.1 us (13%)
  local copies, waits for them, and re-layouts  6.73 us (6%)
  other arithmetic  5.81 us (6%)
  starting transfers between devices  3.94 us (4%)
  matrix products  2.01 us (2%)
    all_gather x1, waiting for transfers between devices, per_device(): lax.all_gather(species, 'bin', axis=1, tiled=True)  27.3 us
    all_to_all x1, blocking collectives, copy_for_each(): return lax.all_to_all(copies, axis, split_axis=0, concat_axis=0, tiled=True)  21.1 us
    all_to_all x1, blocking collectives, per_device(): lax.all_to_all(terms, 'col', split_axis=0, concat_axis=1, tiled=True)  14.2 us
    all_to_all x1, waiting for transfers between devices, copy_for_each(): return lax.all_to_all(copies, axis, split_axis=0, concat_axis=0, tiled=True)  8.78 us
    unnamed x9, local copies, waits for them, and re-layouts  4.62 us
    all_to_all x1, starting transfers between devices, copy_for_each(): return lax.all_to_all(copies, axis, split_axis=0, concat_axis=0, tiled=True)  3.86 us
    add x3, other arithmetic, per_device(): own_lam = own_lam + (own_mean - moment / partition) / own_var  2.17 us
    reduce_sum x3, other arithmetic, per_device(): partition = jnp.sum(expo, axis=0)  2.11 us
  transfers between devices with their start and end apart: 3, of which 2 were waited for; matrix products, arithmetic and copies ran while one was open for 5% of the time, Pallas kernels for 0%

commit v1 on v0

v1 whole, which is shorter than its diff:
```python
import functools

import jax
import jax.numpy as jnp
from jax import lax
from jax.experimental import pallas as pl
from jax.experimental.pallas import tpu as pltpu
from jax.sharding import PartitionSpec as P

ITERS = 3
CHUNKS = 2
LANES = 128
COARSE = 8
FINE = 16


def newton_kernel(x_ref, slope_ref, curve_ref, mean_ref, var_ref, lam_ref, ch_ref, sh_ref, g_ref):
    per_chunk = lam_ref.shape[1] // 8

    def body(v, _):
        chunk = v // per_chunk
        rows = pl.ds(pl.multiple_of((v % per_chunk) * 8, 8), 8)
        curve = curve_ref[chunk, 0, rows, :]
        mean = mean_ref[chunk, 0, rows, :]
        inverse = 1.0 / var_ref[chunk, 0, rows, :]
        for j in range(FINE):
            angle = curve * ((2 * j + 1) / 16384.0)
            up, down = jnp.exp(angle), jnp.exp(-angle)
            up2, down2 = up * up, down * down
            for i in range(COARSE):
                ch_ref[i * FINE + j] = 0.5 * (up + down)
                sh_ref[i * FINE + j] = 0.5 * (up - down)
                if i < COARSE - 1:
                    up, down = up * up2, down * down2
            g_ref[j] = jnp.exp(curve * (((2 * j + 1) / 1024.0) ** 2))
        for i in range(COARSE):
            g_ref[FINE + i] = jnp.exp(curve * (((2 * i + 1) / 32.0) ** 2))

        def newton(_, lam):
            mu = lam + curve
            up, down = jnp.exp(mu * (1 / 1024.0)), jnp.exp(mu * (-1 / 1024.0))
            up2, down2 = up * up, down * down
            sums = [[None] * 4 for _ in range(COARSE)]
            for j in range(FINE):
                g = g_ref[j]
                even, odd = g * (up + down), g * (up - down)
                d = (2 * j + 1) / 1024.0
                d_even, d_odd = even * d, odd * d
                for i in range(COARSE):
                    ch, sh = ch_ref[i * FINE + j], sh_ref[i * FINE + j]
                    terms = (ch * even, sh * odd, ch * d_odd, sh * d_even)
                    sums[i] = [t if s is None else s + t for s, t in zip(sums[i], terms)]
                if j < FINE - 1:
                    up, down = up * up2, down * down2
            up, down = jnp.exp(mu * (1 / 32.0)), jnp.exp(mu * (-1 / 32.0))
            up2, down2 = up * up, down * down
            partition, moment = 0.0, 0.0
            for i in range(COARSE):
                g = g_ref[FINE + i]
                even, odd = g * (up + down), g * (up - down)
                a = (2 * i + 1) / 32.0
                e0, o0, o1, e1 = sums[i]
                partition = partition + (even * e0 + odd * o0)
                moment = moment + (a * (odd * e0 + even * o0) + (even * o1 + odd * e1))
                if i < COARSE - 1:
                    up, down = up * up2, down * down2
            return lam + (mean - (0.5 + moment / partition)) * inverse

        lam_ref[chunk, rows, :] = lax.fori_loop(0, ITERS, newton, slope_ref[chunk, 0, rows, :])
        return 0

    lax.fori_loop(0, CHUNKS * per_chunk, body, 0)


def newton(x, slope, curve, mean, var):
    rows = slope.shape[2]
    mine = pl.BlockSpec((CHUNKS, 1, rows, LANES), lambda g, x: (0, x[0], 0, 0))
    return pl.pallas_call(
        newton_kernel,
        out_shape=jax.ShapeDtypeStruct((CHUNKS, rows, LANES), jnp.float32),
        grid_spec=pltpu.PrefetchScalarGridSpec(
            num_scalar_prefetch=1,
            grid=(1,),
            in_specs=[mine] * 4,
            out_specs=pl.BlockSpec((CHUNKS, rows, LANES), lambda g, x: (0, 0, 0)),
            scratch_shapes=[
                pltpu.VMEM((COARSE * FINE, 8, LANES), jnp.float32),
                pltpu.VMEM((COARSE * FINE, 8, LANES), jnp.float32),
                pltpu.VMEM((COARSE + FINE, 8, LANES), jnp.float32),
            ],
        ),
        cost_estimate=pl.CostEstimate(flops=8192 * 512 * 12, bytes_accessed=1 << 18, transcendentals=0),
        name="newton",
    )(x, slope, curve, mean, var)


def species_kernel(x_ref, lam_ref, curve_ref, table_ref, *refs):
    outs, (turned_ref,) = refs[:-1], refs[-1:]
    turned_ref[...] = jnp.transpose(table_ref[...])
    table = jnp.concatenate([turned_ref[pl.ds(p, 8, stride=16), :] for p in range(16)], axis=1)
    high = table.astype(jnp.bfloat16)
    low = (table - high.astype(jnp.float32)).astype(jnp.bfloat16)
    row = lax.broadcasted_iota(jnp.int32, (8, 8), 0)
    column = lax.broadcasted_iota(jnp.int32, (8, 8), 1)
    order = jnp.where(column == 2 * ((row // 2) ^ x_ref[0]) + row % 2, 1.0, 0.0).astype(jnp.bfloat16)
    parts = [jnp.dot(order, part, preferred_element_type=jnp.float32) for part in (high, low)]
    ones = jnp.ones((16, table.shape[1]), jnp.float32)
    left = jnp.concatenate([*parts, ones], axis=0).astype(jnp.bfloat16)
    sub = lax.broadcasted_iota(jnp.int32, (8, LANES), 0).astype(jnp.float32)

    def tile(row):
        lam = jnp.broadcast_to(lam_ref[0, pl.ds(row, 1), :], (8, LANES))
        curve = jnp.broadcast_to(curve_ref[0, 0, pl.ds(row, 1), :], (8, LANES))
        mu = lam + curve
        ratio2 = jnp.exp(curve * (2.0 / (512.0 * 512.0)))
        columns = []
        for g in range(4):
            s = ((sub + 8.0 * g) * 16.0 + 0.5) * (1 / 512.0) - 0.5
            e = jnp.exp(mu * s + curve * (s * s))
            ratio = jnp.exp(mu * (1 / 512.0) + curve * ((2.0 * s + 1 / 512.0) * (1 / 512.0)))
            column = []
            for p in range(16):
                column.append(e)
                if p < 15:
                    e = e * ratio
                    ratio = ratio * ratio2
            columns.append(column)
        return jnp.concatenate([columns[g][p] for p in range(16) for g in range(4)], axis=0)

    def body(t, _):
        e = jnp.concatenate([tile(2 * t), tile(2 * t + 1)], axis=1)
        e_high = e.astype(jnp.bfloat16)
        e_low = (e - e_high.astype(jnp.float32)).astype(jnp.bfloat16)
        sums = jnp.dot(left, e_high, preferred_element_type=jnp.float32)
        sums = sums + jnp.dot(left, e_low, preferred_element_type=jnp.float32)
        values = (sums[0:8] + sums[8:16]) / sums[16:24]
        lanes = pl.ds(pl.multiple_of(t * 2 * LANES, 2 * LANES), 2 * LANES)
        for d, out in enumerate(outs):
            out[:, lanes] = values[2 * d : 2 * d + 2]
        return 0

    lax.fori_loop(0, lam_ref.shape[1] // 2, body, 0)


def species(x, lam, curve, table, chunk):
    rows = lam.shape[1]
    bins = rows * LANES
    return pl.pallas_call(
        species_kernel,
        out_shape=[jax.ShapeDtypeStruct((2, bins), jnp.float32)] * 4,
        grid_spec=pltpu.PrefetchScalarGridSpec(
            num_scalar_prefetch=1,
            grid=(1,),
            in_specs=[
                pl.BlockSpec((1, rows, LANES), lambda g, x: (chunk, 0, 0)),
                pl.BlockSpec((1, 1, rows, LANES), lambda g, x: (chunk, x[0], 0, 0)),
                pl.BlockSpec((32, LANES), lambda g, x: (0, 0)),
            ],
            out_specs=[pl.BlockSpec((2, bins), lambda g, x: (0, 0))] * 4,
            scratch_shapes=[pltpu.VMEM((LANES, 32), jnp.float32)],
        ),
        cost_estimate=pl.CostEstimate(flops=bins * 512 * 80, bytes_accessed=bins * 40, transcendentals=0),
        name="species",
    )(x, lam, curve, table)


def join_kernel(x_ref, *refs):
    pieces, out = refs[:4], refs[4]
    width = pieces[0].shape[1]
    for d in range(4):
        out[:, pl.ds(pl.multiple_of((x_ref[0] ^ d) * width, LANES), width)] = pieces[d][...]


def join(x, pieces):
    height, width = pieces[0].shape
    return pl.pallas_call(
        join_kernel,
        out_shape=jax.ShapeDtypeStruct((height, 4 * width), jnp.float32),
        in_specs=[pl.BlockSpec(memory_space=pltpu.SMEM)] + [pl.BlockSpec(memory_space=pltpu.VMEM)] * 4,
        out_specs=pl.BlockSpec(memory_space=pltpu.VMEM),
        name="join",
    )(x, *pieces)


def lay_kernel(place_ref, *refs):
    n = 8 * CHUNKS
    species_in, lam_in = refs[:n], refs[n : n + 8]
    species_out, lam_out, sems = refs[n + 8 :]
    copies = []
    width = species_in[0].shape[1]
    for k in range(8):
        group = place_ref[0] ^ k
        length = lam_in[k].shape[0]
        copies.append((lam_in[k], lam_out.at[pl.ds(pl.multiple_of(group * length, 8), length), :]))
        for chunk in range(CHUNKS):
            start = pl.multiple_of((group * CHUNKS + chunk) * width, LANES)
            copies.append((species_in[chunk * 8 + k], species_out.at[:, pl.ds(start, width)]))
    started = [pltpu.make_async_copy(a, b, sems.at[i]) for i, (a, b) in enumerate(copies)]
    for copy in started:
        copy.start()
    for copy in started:
        copy.wait()


def lay(place, species_blocks, lam_blocks):
    anywhere = pl.BlockSpec(memory_space=pl.ANY)
    n = 8 * CHUNKS
    height, width = species_blocks[0].shape
    rows = lam_blocks[0].shape[0]
    return pl.pallas_call(
        lay_kernel,
        out_shape=[
            jax.ShapeDtypeStruct((height, n * width), jnp.float32),
            jax.ShapeDtypeStruct((8 * rows, LANES), jnp.float32),
        ],
        in_specs=[pl.BlockSpec(memory_space=pltpu.SMEM)] + [anywhere] * (n + 8),
        out_specs=[anywhere] * 2,
        scratch_shapes=[pltpu.SemaphoreType.DMA((n + 8,))],
        name="lay",
    )(place, *species_blocks, *lam_blocks)


def swap(array, axis, bit):
    size = lax.axis_size(axis)
    return lax.ppermute(array, axis, [(i, i ^ bit) for i in range(size)])


def spread(block):
    own = [block] + [swap(block, "bin", 2 * e) for e in (1, 3, 2)]
    other = [swap(b, "bin", 1) for b in own]
    order = {0: 0, 2: 1, 6: 2, 4: 3}
    return [(other if k % 2 else own)[order[k - k % 2]] for k in range(8)]


def per_device(slope, curvature, target_mean, target_var, table):
    column = lax.axis_index("col")
    x = jnp.reshape(column % 4, (1,)).astype(jnp.int32)
    place = jnp.reshape(lax.axis_index("bin"), (1,)).astype(jnp.int32)
    columns = lax.axis_size("col")
    sent = jnp.broadcast_to(table.reshape(8, 1, 8 * 16), (8, 4, 8 * 16)).reshape(columns, 8 * 16)
    points = lax.all_to_all(sent, "col", split_axis=0, concat_axis=0, tiled=True)

    bins = slope.shape[0]
    rows = bins // (CHUNKS * 4 * LANES)
    args = [a.reshape(CHUNKS, 4, rows, LANES) for a in (slope, curvature, target_mean, target_var)]
    lam = newton(x, *args)
    lam_pieces = [lam.reshape(1, -1)] + [swap(lam, "col", d).reshape(1, -1) for d in (1, 2, 3)]
    flat = [p.reshape(CHUNKS, rows * LANES) for p in lam_pieces]
    lam_block = join(x, flat)
    lam_block = lam_block.reshape(bins // LANES, LANES)
    lam_blocks = spread(lam_block)

    blocks = []
    for chunk in range(CHUNKS):
        pieces = species(x, lam, args[1], points, chunk)
        pieces = [pieces[0]] + [swap(pieces[d], "col", d) for d in (1, 2, 3)]
        blocks += spread(join(x, pieces))
    species_mean, final_slope = lay(place, blocks, lam_blocks)
    return species_mean, final_slope.reshape(-1)


def solution(mesh):
    placed = (P("bin"), P("bin"), P("bin"), P("bin"), P(None, "col"))
    return jax.shard_map(
        per_device, mesh=mesh, in_specs=placed, out_specs=(P("col", None), P()), check_vma=False
    )
```

time: 105 us -> 188 us (1.79)
  Pallas kernels: 0 us -> 119 us
  starting transfers between devices: 3.94 us -> 39.7 us
  waiting for transfers between devices: 36.1 us -> 3.99 us
  blocking collectives: 35.4 us -> 17.8 us
  between operations: 14.1 us -> 1.04 us
  other arithmetic: 5.81 us -> 0 us
  matrix products: 2.01 us -> 0 us
    pallas_call x0 -> x7, Pallas kernels: none -> 119 us  [the longest x1 96.6 us: lay(): pl.pallas_call(lay_kernel, out_shape=[jax.ShapeDtypeStruct((height, n * w...]
    ppermute x0 -> x30, starting transfers between devices: none -> 39.7 us  [swap(): return lax.ppermute(array, axis, [(i, i ^ bit) for i in range(size)])]
    all_gather x2 -> x0, waiting for transfers between devices: 27.3 us -> none  [the longest x1 27.3 us: per_device(): lax.all_gather(species, 'bin', axis=1, tiled=True)]
    all_to_all x2 -> x1, blocking collectives: 35.4 us -> 17.8 us  [per_device(): lax.all_to_all(sent, 'col', split_axis=0, concat_axis=0, tiled=True)]
    all_to_all x1 -> x0, waiting for transfers between devices: 8.78 us -> none  [copy_for_each(): return lax.all_to_all(copies, axis, split_axis=0, concat_axis=0, tiled=True)]
    ppermute x0 -> x30, waiting for transfers between devices: none -> 3.99 us  [swap(): return lax.ppermute(array, axis, [(i, i ^ bit) for i in range(size)])]
    all_to_all x1 -> x0, starting transfers between devices: 3.86 us -> none  [copy_for_each(): return lax.all_to_all(copies, axis, split_axis=0, concat_axis=0, tiled=True)]
    reduce_sum x4 -> x0, other arithmetic: 2.69 us -> none  [the longest x3 2.11 us: per_device(): partition = jnp.sum(expo, axis=0)]
  transfers between devices with their start and end apart: 3 -> 30, of which waited for: 2 -> 7; matrix products, arithmetic and copies ran while one was open for 5% -> 2% of each run, Pallas kernels for 0% -> 7%
where the time goes in v1:
time: 188 us
  Pallas kernels  119 us (63%)
  starting transfers between devices  39.7 us (21%)
  blocking collectives  17.8 us (9%)
  local copies, waits for them, and re-layouts  6.08 us (3%)
  waiting for transfers between devices  3.99 us (2%)
    pallas_call x1, Pallas kernels, lay(): pl.pallas_call(lay_kernel, out_shape=[jax.ShapeDtypeStruct((height, n * w...  96.6 us
    ppermute x30, starting transfers between devices, swap(): return lax.ppermute(array, axis, [(i, i ^ bit) for i in range(size)])  39.7 us
    all_to_all x1, blocking collectives, per_device(): lax.all_to_all(sent, 'col', split_axis=0, concat_axis=0, tiled=True)  17.8 us
    pallas_call x2, Pallas kernels, species(): pl.pallas_call(species_kernel, out_shape=[jax.ShapeDtypeStruct((2, bins),...  10.9 us
    pallas_call x1, Pallas kernels, newton(): pl.pallas_call(newton_kernel, out_shape=jax.ShapeDtypeStruct((CHUNKS, row...  7.18 us
    unnamed x61, local copies, waits for them, and re-layouts  4.97 us
    pallas_call x3, Pallas kernels, join(): pl.pallas_call(join_kernel, out_shape=jax.ShapeDtypeStruct((height, 4 * w...  4.4 us
    ppermute x30, waiting for transfers between devices, swap(): return lax.ppermute(array, axis, [(i, i ^ bit) for i in range(size)])  3.99 us
  transfers between devices with their start and end apart: 30, of which 7 were waited for; matrix products, arithmetic and copies ran while one was open for 2% of the time, Pallas kernels for 7%

profile of v1, /device:TPU:1, one launch (start us, length us, event | category | flops | bytes accessed | tf_op | source)
XLA Modules:
  0.0 187.6 jit_solution(3511661663649674785)
XLA Ops:
  0.6 7.2 %newton.1.lam_ref = f32[2,32,128]{2,1,0:T(8,128)} custom-call(s32[1]{0:T(128)} %bitcast.1.x_ref, f32[2,4,32,128]{3,2,1,0:T(8,128)} %bitcast.25, f32[2,4,32,128]{3,2,1,0:T(8,128)} %bitcast.28, f32[2,4,32,128]{3,2,1,0:T(8,128)} %bitcast.26, f32[2,4,32,128]{3,2,1,0:T(8,128)} %bitcast.27), custom_call_target="tpu_custom_call" | custom-call | flops 50331648 | bytes 262144 | tf_op jit(solution)/shard_map/newton/pallas_call | solution.py:78
  7.8 3.3 %collective-permute-start.22 = (f32[2,32,128]{2,1,0:T(8,128)}, f32[2,32,128]{2,1,0:T(8,128)S(1)}, u32[]{:S(2)}, u32[]{:S(2)}) collective-permute-start(f32[2,32,128]{2,1,0:T(8,128)} %newton.1.lam_ref), channel_id=1, source_target_pairs={{0,24},{8,16},{16,8},{24,0},{32,56},{40,48},{48,40},{56,32},{64,88... | collective-permute-start | bytes 98312 | tf_op jit(solution)/shard_map/ppermute | solution.py:225
  11.1 0.5 collective-permute-start.21
  11.7 0.1 collective-permute-start.20
  11.7 1.4 copy.20
  13.2 0.6 copy.17
  13.8 1.8 collective-permute-done.21
  15.6 0.6 copy.18
  16.3 0.6 copy.19
  16.9 1.5 join.5
  18.4 1.0 reshape.40.refs_16_
  19.4 2.8 %collective-permute-start.28 = (f32[256,128]{1,0:T(8,128)S(1)}, f32[256,128]{1,0:T(8,128)S(1)}, u32[]{:S(2)}, u32[]{:S(2)}) collective-permute-start(f32[256,128]{1,0:T(8,128)S(1)} %reshape.40.refs_16_), channel_id=1, source_target_pairs={{0,6},{1,7},{2,4},{3,5},{4,2},{5,3},{6,0},{7,1},{8,14},{9,15},{10,... | collective-permute-start | bytes 393224 | tf_op jit(solution)/shard_map/ppermute | solution.py:225
  22.2 0.8 copy.8
  23.0 0.1 broadcast_in_dim.7
  23.1 17.8 %all_to_all.11 = f32[32,1,128]{2,1,0:T(1,128)} all-to-all(f32[32,1,128]{2,1,0:T(1,128)S(1)} %bitcast.36), channel_id=1, replica_groups=mesh['col'=32,'bin'=8] {'col'}, dimensions={0} | all-to-all | bytes 32768 | tf_op jit(solution)/shard_map/all_to_all | solution.py:241
  40.8 5.4 %species.2 = (f32[2,4096]{1,0:T(2,128)}, f32[2,4096]{1,0:T(2,128)}, f32[2,4096]{1,0:T(2,128)}, f32[2,4096]{1,0:T(2,128)}) custom-call(s32[1]{0:T(128)} %bitcast.1.x_ref, f32[2,32,128]{2,1,0:T(8,128)} %newton.1.lam_ref, f32[2,4,32,128]{3,2,1,0:T(8,128)} %bitcast.29, f32[32,128]{1,0:T(8,128)} %bitcast.40), custom_call_target="tpu_custom_call" | custom-call | flops 167772160 | bytes 163840 | tf_op jit(solution)/shard_map/species/pallas_call | solution.py:148
  46.3 0.5 collective-permute-start
  46.7 1.7 collective-permute-start.1
  48.4 5.4 %species.3 = (f32[2,4096]{1,0:T(2,128)}, f32[2,4096]{1,0:T(2,128)}, f32[2,4096]{1,0:T(2,128)}, f32[2,4096]{1,0:T(2,128)}) custom-call(s32[1]{0:T(128)} %bitcast.1.x_ref, f32[2,32,128]{2,1,0:T(8,128)} %newton.1.lam_ref, f32[2,4,32,128]{3,2,1,0:T(8,128)} %bitcast.30, f32[32,128]{1,0:T(8,128)} %bitcast.41), custom_call_target="tpu_custom_call" | custom-call | flops 167772160 | bytes 163840 | tf_op jit(solution)/shard_map/species/pallas_call | solution.py:148
  53.9 1.7 collective-permute-start.2
  55.6 0.0 collective-permute-start.10
  55.6 2.2 %collective-permute-start.11 = (f32[2,4096]{1,0:T(2,128)}, f32[2,4096]{1,0:T(2,128)S(1)}, u32[]{:S(2)}, u32[]{:S(2)}) collective-permute-start(f32[2,4096]{1,0:T(2,128)} %get-tuple-element.18), channel_id=1, source_target_pairs={{0,16},{8,24},{16,0},{24,8},{32,48},{40,56},{48,32},{56,40},{64,80... | collective-permute-start | bytes 98312 | tf_op jit(solution)/shard_map/ppermute | solution.py:225
  57.7 0.0 collective-permute-done.1.refs_2_
  57.8 1.7 collective-permute-start.12
  59.4 0.3 collective-permute-start.26
  59.8 0.3 copy-done.27
  60.1 1.5 join.3.refs_0_
  61.5 0.0 collective-permute-start.24
  61.5 0.0 collective-permute-done.11.refs_2_
  61.5 0.0 copy-start.23
  61.6 6.1 %collective-permute-start.23 = (f32[256,128]{1,0:T(8,128)S(1)}, f32[256,128]{1,0:T(8,128)S(1)}, u32[]{:S(2)}, u32[]{:S(2)}) collective-permute-start(f32[256,128]{1,0:T(8,128)S(1)} %reshape.40.refs_16_), channel_id=1, source_target_pairs={{0,1},{1,0},{2,3},{3,2},{4,5},{5,4},{6,7},{7,6},{8,9},{9,8},{10,11... | collective-permute-start | bytes 393224 | tf_op jit(solution)/shard_map/ppermute | solution.py:225
  67.6 0.0 collective-permute-done.12.refs_3_
  67.6 2.8 %collective-permute-start.8 = (f32[2,16384]{1,0:T(2,128)}, f32[2,16384]{1,0:T(2,128)S(1)}, u32[]{:S(2)}, u32[]{:S(2)}) collective-permute-start(f32[2,16384]{1,0:T(2,128)} %join.3.refs_0_), channel_id=1, source_target_pairs={{0,6},{1,7},{2,4},{3,5},{4,2},{5,3},{6,0},{7,1},{8,14},{9,15},{10,... | collective-permute-start | bytes 393224 | tf_op jit(solution)/shard_map/ppermute | solution.py:225
  70.4 0.0 collective-permute-done.28.refs_22_
  70.4 0.3 collective-permute-start.6
  70.8 1.5 join.4.refs_8_
  72.3 0.0 collective-permute-done.26.refs_20_
  72.3 0.3 collective-permute-start.4
  72.6 0.0 collective-permute-done.24.refs_18_
  72.6 1.4 collective-permute-start.3
  74.0 0.0 collective-permute-done.23.refs_17_
  74.0 2.1 %collective-permute-start.18 = (f32[2,16384]{1,0:T(2,128)}, f32[2,16384]{1,0:T(2,128)S(1)}, u32[]{:S(2)}, u32[]{:S(2)}) collective-permute-start(f32[2,16384]{1,0:T(2,128)} %join.4.refs_8_), channel_id=1, source_target_pairs={{0,6},{1,7},{2,4},{3,5},{4,2},{5,3},{6,0},{7,1},{8,14},{9,15},{10,... | collective-permute-start | bytes 393224 | tf_op jit(solution)/shard_map/ppermute | solution.py:225
  76.1 0.3 collective-permute-done.8.refs_6_
  76.5 2.0 %collective-permute-start.16 = (f32[2,16384]{1,0:T(2,128)}, f32[2,16384]{1,0:T(2,128)S(1)}, u32[]{:S(2)}, u32[]{:S(2)}) collective-permute-start(f32[2,16384]{1,0:T(2,128)} %join.4.refs_8_), channel_id=1, source_target_pairs={{0,4},{1,5},{2,6},{3,7},{4,0},{5,1},{6,2},{7,3},{8,12},{9,13},{10,... | collective-permute-start | bytes 393224 | tf_op jit(solution)/shard_map/ppermute | solution.py:225
  78.5 1.9 collective-permute-start.14
  80.4 1.4 collective-permute-start.13
  81.7 0.1 collective-permute-start.29
  81.8 1.4 collective-permute-start.27
  83.3 2.1 %collective-permute-start.25 = (f32[256,128]{1,0:T(8,128)S(1)}, f32[256,128]{1,0:T(8,128)S(1)}, u32[]{:S(2)}, u32[]{:S(2)}) collective-permute-start(f32[256,128]{1,0:T(8,128)S(1)} %collective-permute-done.24.refs_18_), channel_id=1, source_target_pairs={{0,1},{1,0},{2,3},{3,2},{4,5},{5,4},{6,7},{7,6},{8,9},{9,8},{10,11... | collective-permute-start | bytes 393224 | tf_op jit(solution)/shard_map/ppermute | solution.py:225
  85.4 0.7 collective-permute-done.14.refs_10_
  86.1 1.7 collective-permute-start.9
  87.8 0.1 collective-permute-start.7
  87.9 0.4 collective-permute-start.5
  88.3 0.1 collective-permute-start.19
  88.5 0.4 collective-permute-start.17
  88.9 0.3 collective-permute-start.15
  89.2 0.0 collective-permute-done.7.refs_5_
  89.2 0.2 collective-permute-done.5.refs_3_
  89.4 0.3 collective-permute-done.19.refs_15_
  89.7 0.2 collective-permute-done.17.refs_13_
  89.9 0.3 collective-permute-done.15.refs_11_
  90.4 0.1 copy-done.20
  90.5 0.3 copy-done.21
  90.9 96.6 %lay.1 = (f32[2,262144]{1,0:T(2,128)}, f32[2048,128]{1,0:T(8,128)}) custom-call(s32[1]{0:T(128)} %bitcast.place_ref, f32[2,16384]{1,0:T(2,128)} %join.3.refs_0_, f32[2,16384]{1,0:T(2,128)} %copy-done.8, f32[2,16384]{1,0:T(2,128)} %copy-done.7, f32[2,16384]{1,0:T(2,128)} %copy-done.18, f32[2,16384]{1,0:T(2,128)} %copy-done.6, f32[2,16384]{1,0:T(2,128)} %copy-done.17, ...), custom_call_target="tpu_custom_call" | custom-call | tf_op jit(solution)/shard_map/lay/pallas_call | solution.py:210
  (68 shorter events, 0.1 us)
Async XLA Ops:
  7.8 5.3 %collective-permute-start.22 = (f32[2,32,128]{2,1,0:T(8,128)}, f32[2,32,128]{2,1,0:T(8,128)S(1)}, u32[]{:S(2)}, u32[]{:S(2)}) collective-permute-start(f32[2,32,128]{2,1,0:T(8,128)} %newton.1.lam_ref), channel_id=1, source_target_pairs={{0,24},{8,16},{16,8},{24,0},{32,56},{40,48},{48,40},{56,32},{64,88... | collective-permute-start | bytes 98312 | tf_op jit(solution)/shard_map/ppermute | solution.py:225
  11.1 4.5 %collective-permute-start.21 = (f32[2,32,128]{2,1,0:T(8,128)}, f32[2,32,128]{2,1,0:T(8,128)S(1)}, u32[]{:S(2)}, u32[]{:S(2)}) collective-permute-start(f32[2,32,128]{2,1,0:T(8,128)} %newton.1.lam_ref), channel_id=1, source_target_pairs={{0,16},{8,24},{16,0},{24,8},{32,48},{40,56},{48,32},{56,40},{64,80... | collective-permute-start | bytes 98312 | tf_op jit(solution)/shard_map/ppermute | solution.py:225
  11.7 4.6 %collective-permute-start.20 = (f32[2,32,128]{2,1,0:T(8,128)}, f32[2,32,128]{2,1,0:T(8,128)S(1)}, u32[]{:S(2)}, u32[]{:S(2)}) collective-permute-start(f32[2,32,128]{2,1,0:T(8,128)} %newton.1.lam_ref), channel_id=1, source_target_pairs={{0,8},{8,0},{16,24},{24,16},{32,40},{40,32},{48,56},{56,48},{64,72... | collective-permute-start | bytes 98312 | tf_op jit(solution)/shard_map/ppermute | solution.py:225
  19.4 70.8 %copy-start = (f32[256,128]{1,0:T(8,128)}, f32[256,128]{1,0:T(8,128)S(1)}, u32[]{:S(2)}) copy-start(f32[256,128]{1,0:T(8,128)S(1)} %reshape.40.refs_16_) | copy-start | bytes 393220
  19.4 51.0 %collective-permute-start.28 = (f32[256,128]{1,0:T(8,128)S(1)}, f32[256,128]{1,0:T(8,128)S(1)}, u32[]{:S(2)}, u32[]{:S(2)}) collective-permute-start(f32[256,128]{1,0:T(8,128)S(1)} %reshape.40.refs_16_), channel_id=1, source_target_pairs={{0,6},{1,7},{2,4},{3,5},{4,2},{5,3},{6,0},{7,1},{8,14},{9,15},{10,... | collective-permute-start | bytes 393224 | tf_op jit(solution)/shard_map/ppermute | solution.py:225
  46.3 9.3 %collective-permute-start = (f32[2,4096]{1,0:T(2,128)}, f32[2,4096]{1,0:T(2,128)S(1)}, u32[]{:S(2)}, u32[]{:S(2)}) collective-permute-start(f32[2,4096]{1,0:T(2,128)} %get-tuple-element.13), channel_id=1, source_target_pairs={{0,8},{8,0},{16,24},{24,16},{32,40},{40,32},{48,56},{56,48},{64,72... | collective-permute-start | bytes 98312 | tf_op jit(solution)/shard_map/ppermute | solution.py:225
  46.7 11.0 %collective-permute-start.1 = (f32[2,4096]{1,0:T(2,128)}, f32[2,4096]{1,0:T(2,128)S(1)}, u32[]{:S(2)}, u32[]{:S(2)}) collective-permute-start(f32[2,4096]{1,0:T(2,128)} %get-tuple-element.14), channel_id=1, source_target_pairs={{0,16},{8,24},{16,0},{24,8},{32,48},{40,56},{48,32},{56,40},{64,80... | collective-permute-start | bytes 98312 | tf_op jit(solution)/shard_map/ppermute | solution.py:225
  53.9 5.6 %collective-permute-start.2 = (f32[2,4096]{1,0:T(2,128)}, f32[2,4096]{1,0:T(2,128)S(1)}, u32[]{:S(2)}, u32[]{:S(2)}) collective-permute-start(f32[2,4096]{1,0:T(2,128)} %get-tuple-element.15), channel_id=1, source_target_pairs={{0,24},{8,16},{16,8},{24,0},{32,56},{40,48},{48,40},{56,32},{64,88... | collective-permute-start | bytes 98312 | tf_op jit(solution)/shard_map/ppermute | solution.py:225
  55.6 6.0 %collective-permute-start.10 = (f32[2,4096]{1,0:T(2,128)}, f32[2,4096]{1,0:T(2,128)S(1)}, u32[]{:S(2)}, u32[]{:S(2)}) collective-permute-start(f32[2,4096]{1,0:T(2,128)} %get-tuple-element.17), channel_id=1, source_target_pairs={{0,8},{8,0},{16,24},{24,16},{32,40},{40,32},{48,56},{56,48},{64,72... | collective-permute-start | bytes 98312 | tf_op jit(solution)/shard_map/ppermute | solution.py:225
  55.6 4.2 %copy-start.25 = (f32[2,4096]{1,0:T(2,128)}, f32[2,4096]{1,0:T(2,128)S(1)}, u32[]{:S(2)}) copy-start(f32[2,4096]{1,0:T(2,128)S(1)} %collective-permute-done.refs_1_) | copy-start | bytes 98308
  55.6 6.0 %collective-permute-start.11 = (f32[2,4096]{1,0:T(2,128)}, f32[2,4096]{1,0:T(2,128)S(1)}, u32[]{:S(2)}, u32[]{:S(2)}) collective-permute-start(f32[2,4096]{1,0:T(2,128)} %get-tuple-element.18), channel_id=1, source_target_pairs={{0,16},{8,24},{16,0},{24,8},{32,48},{40,56},{48,32},{56,40},{64,80... | collective-permute-start | bytes 98312 | tf_op jit(solution)/shard_map/ppermute | solution.py:225
  57.8 2.0 %copy-start.26 = (f32[2,4096]{1,0:T(2,128)}, f32[2,4096]{1,0:T(2,128)S(1)}, u32[]{:S(2)}) copy-start(f32[2,4096]{1,0:T(2,128)S(1)} %collective-permute-done.1.refs_2_) | copy-start | bytes 98308
  57.8 9.9 %collective-permute-start.12 = (f32[2,4096]{1,0:T(2,128)}, f32[2,4096]{1,0:T(2,128)S(1)}, u32[]{:S(2)}, u32[]{:S(2)}) collective-permute-start(f32[2,4096]{1,0:T(2,128)} %get-tuple-element.19), channel_id=1, source_target_pairs={{0,24},{8,16},{16,8},{24,0},{32,56},{40,48},{48,40},{56,32},{64,88... | collective-permute-start | bytes 98312 | tf_op jit(solution)/shard_map/ppermute | solution.py:225
  59.4 0.6 copy-start.27
  59.4 12.8 %collective-permute-start.26 = (f32[256,128]{1,0:T(8,128)S(1)}, f32[256,128]{1,0:T(8,128)S(1)}, u32[]{:S(2)}, u32[]{:S(2)}) collective-permute-start(f32[256,128]{1,0:T(8,128)S(1)} %reshape.40.refs_16_), channel_id=1, source_target_pairs={{0,4},{1,5},{2,6},{3,7},{4,0},{5,1},{6,2},{7,3},{8,12},{9,13},{10,... | collective-permute-start | bytes 393224 | tf_op jit(solution)/shard_map/ppermute | solution.py:225
  61.5 9.3 %copy-start.22 = (f32[2,4096]{1,0:T(2,128)}, f32[2,4096]{1,0:T(2,128)S(1)}, u32[]{:S(2)}) copy-start(f32[2,4096]{1,0:T(2,128)S(1)} %collective-permute-done.10.refs_1_) | copy-start | bytes 98308
  61.5 11.1 %collective-permute-start.24 = (f32[256,128]{1,0:T(8,128)S(1)}, f32[256,128]{1,0:T(8,128)S(1)}, u32[]{:S(2)}, u32[]{:S(2)}) collective-permute-start(f32[256,128]{1,0:T(8,128)S(1)} %reshape.40.refs_16_), channel_id=1, source_target_pairs={{0,2},{1,3},{2,0},{3,1},{4,6},{5,7},{6,4},{7,5},{8,10},{9,11},{10,... | collective-permute-start | bytes 393224 | tf_op jit(solution)/shard_map/ppermute | solution.py:225
  61.5 9.2 %copy-start.23 = (f32[2,4096]{1,0:T(2,128)}, f32[2,4096]{1,0:T(2,128)S(1)}, u32[]{:S(2)}) copy-start(f32[2,4096]{1,0:T(2,128)S(1)} %collective-permute-done.11.refs_2_) | copy-start | bytes 98308
  61.6 12.4 %collective-permute-start.23 = (f32[256,128]{1,0:T(8,128)S(1)}, f32[256,128]{1,0:T(8,128)S(1)}, u32[]{:S(2)}, u32[]{:S(2)}) collective-permute-start(f32[256,128]{1,0:T(8,128)S(1)} %reshape.40.refs_16_), channel_id=1, source_target_pairs={{0,1},{1,0},{2,3},{3,2},{4,5},{5,4},{6,7},{7,6},{8,9},{9,8},{10,11... | collective-permute-start | bytes 393224 | tf_op jit(solution)/shard_map/ppermute | solution.py:225
  67.6 3.2 %copy-start.24 = (f32[2,4096]{1,0:T(2,128)}, f32[2,4096]{1,0:T(2,128)S(1)}, u32[]{:S(2)}) copy-start(f32[2,4096]{1,0:T(2,128)S(1)} %collective-permute-done.12.refs_3_) | copy-start | bytes 98308
  67.6 8.8 %collective-permute-start.8 = (f32[2,16384]{1,0:T(2,128)}, f32[2,16384]{1,0:T(2,128)S(1)}, u32[]{:S(2)}, u32[]{:S(2)}) collective-permute-start(f32[2,16384]{1,0:T(2,128)} %join.3.refs_0_), channel_id=1, source_target_pairs={{0,6},{1,7},{2,4},{3,5},{4,2},{5,3},{6,0},{7,1},{8,14},{9,15},{10,... | collective-permute-start | bytes 393224 | tf_op jit(solution)/shard_map/ppermute | solution.py:225
  70.4 19.8 %copy-start.1 = (f32[256,128]{1,0:T(8,128)}, f32[256,128]{1,0:T(8,128)S(1)}, u32[]{:S(2)}) copy-start(f32[256,128]{1,0:T(8,128)S(1)} %collective-permute-done.28.refs_22_) | copy-start | bytes 393220
  70.4 8.0 %collective-permute-start.6 = (f32[2,16384]{1,0:T(2,128)}, f32[2,16384]{1,0:T(2,128)S(1)}, u32[]{:S(2)}, u32[]{:S(2)}) collective-permute-start(f32[2,16384]{1,0:T(2,128)} %join.3.refs_0_), channel_id=1, source_target_pairs={{0,4},{1,5},{2,6},{3,7},{4,0},{5,1},{6,2},{7,3},{8,12},{9,13},{10,... | collective-permute-start | bytes 393224 | tf_op jit(solution)/shard_map/ppermute | solution.py:225
  72.3 18.0 %copy-start.2 = (f32[256,128]{1,0:T(8,128)}, f32[256,128]{1,0:T(8,128)S(1)}, u32[]{:S(2)}) copy-start(f32[256,128]{1,0:T(8,128)S(1)} %collective-permute-done.26.refs_20_) | copy-start | bytes 393220
  72.3 8.1 %collective-permute-start.4 = (f32[2,16384]{1,0:T(2,128)}, f32[2,16384]{1,0:T(2,128)S(1)}, u32[]{:S(2)}, u32[]{:S(2)}) collective-permute-start(f32[2,16384]{1,0:T(2,128)} %join.3.refs_0_), channel_id=1, source_target_pairs={{0,2},{1,3},{2,0},{3,1},{4,6},{5,7},{6,4},{7,5},{8,10},{9,11},{10,... | collective-permute-start | bytes 393224 | tf_op jit(solution)/shard_map/ppermute | solution.py:225
  72.6 17.6 %copy-start.3 = (f32[256,128]{1,0:T(8,128)}, f32[256,128]{1,0:T(8,128)S(1)}, u32[]{:S(2)}) copy-start(f32[256,128]{1,0:T(8,128)S(1)} %collective-permute-done.24.refs_18_) | copy-start | bytes 393220
  72.6 9.1 %collective-permute-start.3 = (f32[2,16384]{1,0:T(2,128)}, f32[2,16384]{1,0:T(2,128)S(1)}, u32[]{:S(2)}, u32[]{:S(2)}) collective-permute-start(f32[2,16384]{1,0:T(2,128)} %join.3.refs_0_), channel_id=1, source_target_pairs={{0,1},{1,0},{2,3},{3,2},{4,5},{5,4},{6,7},{7,6},{8,9},{9,8},{10,11... | collective-permute-start | bytes 393224 | tf_op jit(solution)/shard_map/ppermute | solution.py:225
  74.0 16.2 %copy-start.4 = (f32[256,128]{1,0:T(8,128)}, f32[256,128]{1,0:T(8,128)S(1)}, u32[]{:S(2)}) copy-start(f32[256,128]{1,0:T(8,128)S(1)} %collective-permute-done.23.refs_17_) | copy-start | bytes 393220
  74.0 7.8 %collective-permute-start.18 = (f32[2,16384]{1,0:T(2,128)}, f32[2,16384]{1,0:T(2,128)S(1)}, u32[]{:S(2)}, u32[]{:S(2)}) collective-permute-start(f32[2,16384]{1,0:T(2,128)} %join.4.refs_8_), channel_id=1, source_target_pairs={{0,6},{1,7},{2,4},{3,5},{4,2},{5,3},{6,0},{7,1},{8,14},{9,15},{10,... | collective-permute-start | bytes 393224 | tf_op jit(solution)/shard_map/ppermute | solution.py:225
  76.5 13.8 %copy-start.5 = (f32[2,16384]{1,0:T(2,128)}, f32[2,16384]{1,0:T(2,128)S(1)}, u32[]{:S(2)}) copy-start(f32[2,16384]{1,0:T(2,128)S(1)} %collective-permute-done.8.refs_6_) | copy-start | bytes 393220
  76.5 6.8 %collective-permute-start.16 = (f32[2,16384]{1,0:T(2,128)}, f32[2,16384]{1,0:T(2,128)S(1)}, u32[]{:S(2)}, u32[]{:S(2)}) collective-permute-start(f32[2,16384]{1,0:T(2,128)} %join.4.refs_8_), channel_id=1, source_target_pairs={{0,4},{1,5},{2,6},{3,7},{4,0},{5,1},{6,2},{7,3},{8,12},{9,13},{10,... | collective-permute-start | bytes 393224 | tf_op jit(solution)/shard_map/ppermute | solution.py:225
  78.5 11.8 %copy-start.6 = (f32[2,16384]{1,0:T(2,128)}, f32[2,16384]{1,0:T(2,128)S(1)}, u32[]{:S(2)}) copy-start(f32[2,16384]{1,0:T(2,128)S(1)} %collective-permute-done.6.refs_4_) | copy-start | bytes 393220
  78.5 7.6 %collective-permute-start.14 = (f32[2,16384]{1,0:T(2,128)}, f32[2,16384]{1,0:T(2,128)S(1)}, u32[]{:S(2)}, u32[]{:S(2)}) collective-permute-start(f32[2,16384]{1,0:T(2,128)} %join.4.refs_8_), channel_id=1, source_target_pairs={{0,2},{1,3},{2,0},{3,1},{4,6},{5,7},{6,4},{7,5},{8,10},{9,11},{10,... | collective-permute-start | bytes 393224 | tf_op jit(solution)/shard_map/ppermute | solution.py:225
  80.4 9.9 %copy-start.7 = (f32[2,16384]{1,0:T(2,128)}, f32[2,16384]{1,0:T(2,128)S(1)}, u32[]{:S(2)}) copy-start(f32[2,16384]{1,0:T(2,128)S(1)} %collective-permute-done.4.refs_2_) | copy-start | bytes 393220
  80.4 7.5 %collective-permute-start.13 = (f32[2,16384]{1,0:T(2,128)}, f32[2,16384]{1,0:T(2,128)S(1)}, u32[]{:S(2)}, u32[]{:S(2)}) collective-permute-start(f32[2,16384]{1,0:T(2,128)} %join.4.refs_8_), channel_id=1, source_target_pairs={{0,1},{1,0},{2,3},{3,2},{4,5},{5,4},{6,7},{7,6},{8,9},{9,8},{10,11... | collective-permute-start | bytes 393224 | tf_op jit(solution)/shard_map/ppermute | solution.py:225
  81.7 8.5 %copy-start.8 = (f32[2,16384]{1,0:T(2,128)}, f32[2,16384]{1,0:T(2,128)S(1)}, u32[]{:S(2)}) copy-start(f32[2,16384]{1,0:T(2,128)S(1)} %collective-permute-done.3.refs_1_) | copy-start | bytes 393220
  81.7 6.2 %collective-permute-start.29 = (f32[256,128]{1,0:T(8,128)S(1)}, f32[256,128]{1,0:T(8,128)S(1)}, u32[]{:S(2)}, u32[]{:S(2)}) collective-permute-start(f32[256,128]{1,0:T(8,128)S(1)} %collective-permute-done.28.refs_22_), channel_id=1, source_target_pairs={{0,1},{1,0},{2,3},{3,2},{4,5},{5,4},{6,7},{7,6},{8,9},{9,8},{10,11... | collective-permute-start | bytes 393224 | tf_op jit(solution)/shard_map/ppermute | solution.py:225
  81.8 8.4 %copy-start.9 = (f32[2,16384]{1,0:T(2,128)}, f32[2,16384]{1,0:T(2,128)S(1)}, u32[]{:S(2)}) copy-start(f32[2,16384]{1,0:T(2,128)S(1)} %collective-permute-done.18.refs_14_) | copy-start | bytes 393220
  81.8 6.5 %collective-permute-start.27 = (f32[256,128]{1,0:T(8,128)S(1)}, f32[256,128]{1,0:T(8,128)S(1)}, u32[]{:S(2)}, u32[]{:S(2)}) collective-permute-start(f32[256,128]{1,0:T(8,128)S(1)} %collective-permute-done.26.refs_20_), channel_id=1, source_target_pairs={{0,1},{1,0},{2,3},{3,2},{4,5},{5,4},{6,7},{7,6},{8,9},{9,8},{10,11... | collective-permute-start | bytes 393224 | tf_op jit(solution)/shard_map/ppermute | solution.py:225
  83.3 7.0 %copy-start.10 = (f32[2,16384]{1,0:T(2,128)}, f32[2,16384]{1,0:T(2,128)S(1)}, u32[]{:S(2)}) copy-start(f32[2,16384]{1,0:T(2,128)S(1)} %collective-permute-done.16.refs_12_) | copy-start | bytes 393220
  83.3 5.2 %collective-permute-start.25 = (f32[256,128]{1,0:T(8,128)S(1)}, f32[256,128]{1,0:T(8,128)S(1)}, u32[]{:S(2)}, u32[]{:S(2)}) collective-permute-start(f32[256,128]{1,0:T(8,128)S(1)} %collective-permute-done.24.refs_18_), channel_id=1, source_target_pairs={{0,1},{1,0},{2,3},{3,2},{4,5},{5,4},{6,7},{7,6},{8,9},{9,8},{10,11... | collective-permute-start | bytes 393224 | tf_op jit(solution)/shard_map/ppermute | solution.py:225
  86.1 4.2 %copy-start.11 = (f32[2,16384]{1,0:T(2,128)}, f32[2,16384]{1,0:T(2,128)S(1)}, u32[]{:S(2)}) copy-start(f32[2,16384]{1,0:T(2,128)S(1)} %collective-permute-done.14.refs_10_) | copy-start | bytes 393220
  86.1 2.8 %collective-permute-start.9 = (f32[2,16384]{1,0:T(2,128)S(1)}, f32[2,16384]{1,0:T(2,128)S(1)}, u32[]{:S(2)}, u32[]{:S(2)}) collective-permute-start(f32[2,16384]{1,0:T(2,128)S(1)} %collective-permute-done.8.refs_6_), channel_id=1, source_target_pairs={{0,1},{1,0},{2,3},{3,2},{4,5},{5,4},{6,7},{7,6},{8,9},{9,8},{10,11... | collective-permute-start | bytes 393224 | tf_op jit(solution)/shard_map/ppermute | solution.py:225
  87.8 2.5 %copy-start.12 = (f32[2,16384]{1,0:T(2,128)}, f32[2,16384]{1,0:T(2,128)S(1)}, u32[]{:S(2)}) copy-start(f32[2,16384]{1,0:T(2,128)S(1)} %collective-permute-done.13.refs_9_) | copy-start | bytes 393220
  87.8 1.3 collective-permute-start.7
  87.9 2.4 %copy-start.13 = (f32[256,128]{1,0:T(8,128)}, f32[256,128]{1,0:T(8,128)S(1)}, u32[]{:S(2)}) copy-start(f32[256,128]{1,0:T(8,128)S(1)} %collective-permute-done.29.refs_23_) | copy-start | bytes 393220
  87.9 1.4 collective-permute-start.5
  88.3 2.0 %copy-start.14 = (f32[256,128]{1,0:T(8,128)}, f32[256,128]{1,0:T(8,128)S(1)}, u32[]{:S(2)}) copy-start(f32[256,128]{1,0:T(8,128)S(1)} %collective-permute-done.27.refs_21_) | copy-start | bytes 393220
  88.3 1.3 collective-permute-start.19
  88.5 1.9 %copy-start.15 = (f32[256,128]{1,0:T(8,128)}, f32[256,128]{1,0:T(8,128)S(1)}, u32[]{:S(2)}) copy-start(f32[256,128]{1,0:T(8,128)S(1)} %collective-permute-done.25.refs_19_) | copy-start | bytes 393220
  88.5 1.4 collective-permute-start.17
  88.9 1.5 copy-start.16
  88.9 1.3 collective-permute-start.15
  89.2 1.2 copy-start.17
  89.4 1.0 copy-start.18
  89.7 0.7 copy-start.19
  89.9 0.7 copy-start.20
  90.2 0.7 copy-start.21

commit v2 on v1

v2 whole, which is shorter than its diff:
```python
import jax
import jax.numpy as jnp
import numpy as np
from jax import lax
from jax.experimental import pallas as pl
from jax.experimental.pallas import tpu as pltpu
from jax.sharding import PartitionSpec as P

ITERS = 3
CHUNKS = 1
LANES = 128
COARSE = 8
FINE = 16


def newton_kernel(x_ref, slope_ref, curve_ref, mean_ref, var_ref, lam_ref, ch_ref, sh_ref, g_ref):
    per_chunk = lam_ref.shape[1] // 8

    def body(v, _):
        chunk = v // per_chunk
        rows = pl.ds(pl.multiple_of((v % per_chunk) * 8, 8), 8)
        curve = curve_ref[chunk, 0, rows, :]
        mean = mean_ref[chunk, 0, rows, :]
        inverse = 1.0 / var_ref[chunk, 0, rows, :]
        for j in range(FINE):
            angle = curve * ((2 * j + 1) / 16384.0)
            up, down = jnp.exp(angle), jnp.exp(-angle)
            up2, down2 = up * up, down * down
            for i in range(COARSE):
                ch_ref[i * FINE + j] = 0.5 * (up + down)
                sh_ref[i * FINE + j] = 0.5 * (up - down)
                if i < COARSE - 1:
                    up, down = up * up2, down * down2
            g_ref[j] = jnp.exp(curve * (((2 * j + 1) / 1024.0) ** 2))
        for i in range(COARSE):
            g_ref[FINE + i] = jnp.exp(curve * (((2 * i + 1) / 32.0) ** 2))

        def newton(_, lam):
            mu = lam + curve
            up, down = jnp.exp(mu * (1 / 1024.0)), jnp.exp(mu * (-1 / 1024.0))
            up2, down2 = up * up, down * down
            sums = [[None] * 4 for _ in range(COARSE)]
            for j in range(FINE):
                g = g_ref[j]
                even, odd = g * (up + down), g * (up - down)
                d = (2 * j + 1) / 1024.0
                d_even, d_odd = even * d, odd * d
                for i in range(COARSE):
                    ch, sh = ch_ref[i * FINE + j], sh_ref[i * FINE + j]
                    terms = (ch * even, sh * odd, ch * d_odd, sh * d_even)
                    sums[i] = [t if s is None else s + t for s, t in zip(sums[i], terms)]
                if j < FINE - 1:
                    up, down = up * up2, down * down2
            up, down = jnp.exp(mu * (1 / 32.0)), jnp.exp(mu * (-1 / 32.0))
            up2, down2 = up * up, down * down
            partition, moment = 0.0, 0.0
            for i in range(COARSE):
                g = g_ref[FINE + i]
                even, odd = g * (up + down), g * (up - down)
                a = (2 * i + 1) / 32.0
                e0, o0, o1, e1 = sums[i]
                partition = partition + (even * e0 + odd * o0)
                moment = moment + (a * (odd * e0 + even * o0) + (even * o1 + odd * e1))
                if i < COARSE - 1:
                    up, down = up * up2, down * down2
            return lam + (mean - (0.5 + moment / partition)) * inverse

        lam_ref[chunk, rows, :] = lax.fori_loop(0, ITERS, newton, slope_ref[chunk, 0, rows, :])
        return 0

    lax.fori_loop(0, CHUNKS * per_chunk, body, 0)


def newton(x, slope, curve, mean, var):
    rows = slope.shape[2]
    mine = pl.BlockSpec((CHUNKS, 1, rows, LANES), lambda g, x: (0, x[0], 0, 0))
    return pl.pallas_call(
        newton_kernel,
        out_shape=jax.ShapeDtypeStruct((CHUNKS, rows, LANES), jnp.float32),
        grid_spec=pltpu.PrefetchScalarGridSpec(
            num_scalar_prefetch=1,
            grid=(1,),
            in_specs=[mine] * 4,
            out_specs=pl.BlockSpec((CHUNKS, rows, LANES), lambda g, x: (0, 0, 0)),
            scratch_shapes=[
                pltpu.VMEM((COARSE * FINE, 8, LANES), jnp.float32),
                pltpu.VMEM((COARSE * FINE, 8, LANES), jnp.float32),
                pltpu.VMEM((COARSE + FINE, 8, LANES), jnp.float32),
            ],
        ),
        cost_estimate=pl.CostEstimate(flops=12 * 10**9, bytes_accessed=1 << 18, transcendentals=0),
        name="newton",
    )(x, slope, curve, mean, var)


def species_kernel(x_ref, lam_ref, curve_ref, table_ref, out_ref, turned_ref):
    turned_ref[...] = jnp.transpose(table_ref[...])
    table = jnp.concatenate([turned_ref[pl.ds(p, 8, stride=16), :] for p in range(16)], axis=1)
    high = table.astype(jnp.bfloat16).astype(jnp.float32)
    ones = jnp.ones((16, table.shape[1]), jnp.float32)
    left = jnp.concatenate([high, table - high, ones], axis=0).astype(jnp.bfloat16)
    sub = lax.broadcasted_iota(jnp.int32, (8, LANES), 0).astype(jnp.float32)

    def tile(row):
        lam = jnp.broadcast_to(lam_ref[0, pl.ds(row, 1), :], (8, LANES))
        curve = jnp.broadcast_to(curve_ref[0, 0, pl.ds(row, 1), :], (8, LANES))
        mu = lam + curve
        ratio2 = jnp.exp(curve * (2.0 / (512.0 * 512.0)))
        columns = []
        for g in range(4):
            s = ((sub + 8.0 * g) * 16.0 + 0.5) * (1 / 512.0) - 0.5
            e = jnp.exp(mu * s + curve * (s * s))
            ratio = jnp.exp(mu * (1 / 512.0) + curve * ((2.0 * s + 1 / 512.0) * (1 / 512.0)))
            column = []
            for p in range(16):
                column.append(e)
                if p < 15:
                    e = e * ratio
                    ratio = ratio * ratio2
            columns.append(column)
        return jnp.concatenate([columns[g][p] for p in range(16) for g in range(4)], axis=0)

    def pair(row):
        e = jnp.concatenate([tile(row), tile(row + 1)], axis=1)
        e_high = e.astype(jnp.bfloat16)
        e_low = (e - e_high.astype(jnp.float32)).astype(jnp.bfloat16)
        sums = jnp.dot(left, e_high, preferred_element_type=jnp.float32)
        sums = sums + jnp.dot(left, e_low, preferred_element_type=jnp.float32)
        values = (sums[0:8] + sums[8:16]) / sums[16:24]
        return [values[:, :LANES], values[:, LANES:]]

    def body(t, _):
        values = pair(4 * t) + pair(4 * t + 2)
        rows = pl.ds(pl.multiple_of(8 * t, 8), 8)
        for x in range(4):
            out_ref[x, rows, :] = jnp.concatenate([v[2 * x : 2 * x + 2] for v in values], axis=0)
        return 0

    rows = lam_ref.shape[1]
    lax.fori_loop(0, rows // 4, body, 0)
    for x in range(4):
        out_ref[x, 2 * rows :, :] = lam_ref[0]


def species(x, lam, curve, table):
    rows = lam.shape[1]
    return pl.pallas_call(
        species_kernel,
        out_shape=jax.ShapeDtypeStruct((4, 3 * rows, LANES), jnp.float32),
        grid_spec=pltpu.PrefetchScalarGridSpec(
            num_scalar_prefetch=1,
            grid=(1,),
            in_specs=[
                pl.BlockSpec((1, rows, LANES), lambda g, x: (0, 0, 0)),
                pl.BlockSpec((1, 1, rows, LANES), lambda g, x: (0, x[0], 0, 0)),
                pl.BlockSpec((32, LANES), lambda g, x: (0, 0)),
            ],
            out_specs=pl.BlockSpec((4, 3 * rows, LANES), lambda g, x: (0, 0, 0)),
            scratch_shapes=[pltpu.VMEM((LANES, 32), jnp.float32)],
        ),
        cost_estimate=pl.CostEstimate(flops=6 * 10**9, bytes_accessed=1 << 19, transcendentals=0),
        name="species",
    )(x, lam, curve, table)


def lay_kernel(core_ref, own_ref, other_ref, species_ref, lam_ref, sems):
    rows = lam_ref.shape[3]
    copies = []
    for flip, blocks in ((0, own_ref), (1, other_ref)):
        core = core_ref[0] ^ flip
        for y in range(4):
            copies.append((blocks.at[y, :, pl.ds(0, 2 * rows), :], species_ref.at[y, core]))
            copies.append((blocks.at[y, :, pl.ds(2 * rows, rows), :], lam_ref.at[y, core]))
    started = [pltpu.make_async_copy(a, b, sems.at[i]) for i, (a, b) in enumerate(copies)]
    for copy in started:
        copy.start()
    for copy in started:
        copy.wait()


def lay(core, own, other):
    anywhere = pl.BlockSpec(memory_space=pl.ANY)
    rows = own.shape[2] // 3
    return pl.pallas_call(
        lay_kernel,
        out_shape=[
            jax.ShapeDtypeStruct((4, 2, 4, 2 * rows, LANES), jnp.float32),
            jax.ShapeDtypeStruct((4, 2, 4, rows, LANES), jnp.float32),
        ],
        in_specs=[pl.BlockSpec(memory_space=pltpu.SMEM), anywhere, anywhere],
        out_specs=[anywhere] * 2,
        scratch_shapes=[pltpu.SemaphoreType.DMA((16,))],
        name="lay",
    )(core, own, other)


def exchange(array, axes):
    return lax.all_to_all(array, axes, split_axis=0, concat_axis=0, tiled=True)


def per_device(slope, curvature, target_mean, target_var, table):
    x = jnp.reshape(lax.axis_index("x"), (1,)).astype(jnp.int32)
    core = jnp.reshape(lax.axis_index("core"), (1,)).astype(jnp.int32)
    sent = jnp.broadcast_to(table.reshape(8, 1, 8 * 16), (8, 4, 8 * 16)).reshape(32, 8 * 16)
    points = exchange(sent, ("z", "x"))

    bins = slope.shape[0]
    rows = bins // (4 * LANES)
    args = [a.reshape(1, 4, rows, LANES) for a in (slope, curvature, target_mean, target_var)]
    lam = newton(x, *args)
    sent = species(x, lam, args[1], points)
    ring = exchange(sent, "x")
    own = exchange(jnp.broadcast_to(ring[None], (4, *ring.shape)), "y")
    other = lax.ppermute(own, "core", [(0, 1), (1, 0)])
    values, final_slope = lay(core, own, other)
    values = jnp.transpose(values.reshape(-1, 2, LANES), (1, 0, 2)).reshape(2, -1)
    return values, final_slope.reshape(-1)


def solution(mesh):
    mesh = jax.sharding.Mesh(np.reshape(mesh.devices, (8, 4, 4, 2)), ("z", "x", "y", "core"))
    bins = P(("y", "core"))
    placed = (bins, bins, bins, bins, P(None, ("z", "x")))
    return jax.shard_map(
        per_device, mesh=mesh, in_specs=placed, out_specs=(P(("z", "x"), None), P()), check_vma=False
    )
```

time: 188 us -> 168 us (0.89)
  starting transfers between devices: 39.7 us -> 16.6 us
  blocking collectives: 17.8 us -> 30.6 us
  Pallas kernels: 119 us -> 112 us
  local copies, waits for them, and re-layouts: 6.08 us -> 3.38 us
    ppermute x30 -> x1, starting transfers between devices: 39.7 us -> 4.75 us  [per_device(): other = lax.ppermute(own, 'core', [(0, 1), (1, 0)])]
    all_to_all x1 -> x2, blocking collectives: 17.8 us -> 30.6 us  [exchange(): return lax.all_to_all(array, axes, split_axis=0, concat_axis=0, tiled=True)]
    all_to_all x0 -> x1, starting transfers between devices: none -> 11.9 us  [exchange(): return lax.all_to_all(array, axes, split_axis=0, concat_axis=0, tiled=True)]
    pallas_call x6 -> x2, Pallas kernels: 112 us -> 105 us  [the longest x1 96.5 us: lay(): pl.pallas_call(lay_kernel, out_shape=[jax.ShapeDtypeStruct((4, 2, 4, 2 *...]
    unnamed x61 -> x7, local copies, waits for them, and re-layouts: 4.97 us -> 2.54 us
    ppermute x30 -> x1, waiting for transfers between devices: 3.99 us -> 3.04 us  [per_device(): other = lax.ppermute(own, 'core', [(0, 1), (1, 0)])]
  transfers between devices with their start and end apart: 30 -> 2, of which waited for: 7 -> 2; matrix products, arithmetic and copies ran while one was open for 2% -> 0% of each run, Pallas kernels for 7% -> 4%
where the time goes in v2:
time: 168 us
  Pallas kernels  112 us (67%)
  blocking collectives  30.6 us (18%)
  starting transfers between devices  16.6 us (10%)
  waiting for transfers between devices  4.37 us (3%)
  local copies, waits for them, and re-layouts  3.38 us (2%)
    pallas_call x1, Pallas kernels, lay(): pl.pallas_call(lay_kernel, out_shape=[jax.ShapeDtypeStruct((4, 2, 4, 2 *...  96.5 us
    all_to_all x2, blocking collectives, exchange(): return lax.all_to_all(array, axes, split_axis=0, concat_axis=0, tiled=True)  30.6 us
    all_to_all x1, starting transfers between devices, exchange(): return lax.all_to_all(array, axes, split_axis=0, concat_axis=0, tiled=True)  11.9 us
    pallas_call x1, Pallas kernels, species(): pl.pallas_call(species_kernel, out_shape=jax.ShapeDtypeStruct((4, 3 * row...  8.37 us
    pallas_call x1, Pallas kernels, newton(): pl.pallas_call(newton_kernel, out_shape=jax.ShapeDtypeStruct((CHUNKS, row...  7.17 us
    ppermute x1, starting transfers between devices, per_device(): other = lax.ppermute(own, 'core', [(0, 1), (1, 0)])  4.75 us
  transfers between devices with their start and end apart: 2, of which 2 were waited for; matrix products, arithmetic and copies ran while one was open for 0% of the time, Pallas kernels for 4%

profile of v2, /device:TPU:1, one launch (start us, length us, event | category | flops | bytes accessed | tf_op | source)
XLA Modules:
  0.0 167.7 jit_solution(8320988231432757611)
XLA Ops:
  0.6 0.8 copy.10
  1.4 0.1 broadcast_in_dim.6
  1.5 0.6 broadcast_in_dim.14
  2.1 11.9 %all-to-all-start = ((f32[32,1,128]{2,1,0:T(1,128)}), f32[32,1,128]{2,1,0:T(1,128)S(1)}, u32[]{:S(2)}, u32[]{:S(2)}) async-start(f32[32,1,128]{2,1,0:T(1,128)} %bitcast.6), calls=%async_computation | async-start | bytes 32768 | tf_op jit(solution)/shard_map/all_to_all | solution.py:198
  14.0 7.2 %newton.1.lam_ref = f32[1,64,128]{2,1,0:T(8,128)} custom-call(s32[1]{0:T(128)} %bitcast.1.x_ref, f32[1,4,64,128]{3,2,1,0:T(8,128)} %bitcast.17, f32[1,4,64,128]{3,2,1,0:T(8,128)} %bitcast.20, f32[1,4,64,128]{3,2,1,0:T(8,128)} %bitcast.18, f32[1,4,64,128]{3,2,1,0:T(8,128)} %bitcast.19), custom_call_target="tpu_custom_call" | custom-call | flops 12000000000 | bytes 262144 | tf_op jit(solution)/shard_map/newton/pallas_call | solution.py:77
  21.2 1.3 all-to-all-done
  22.5 0.0 copy-start.2
  22.5 0.6 copy-done.2
  23.1 8.4 %species.1 = f32[4,192,128]{2,1,0:T(8,128)} custom-call(s32[1]{0:T(128)} %bitcast.1.x_ref, f32[1,64,128]{2,1,0:T(8,128)} %newton.1.lam_ref, f32[1,4,64,128]{3,2,1,0:T(8,128)} %bitcast.21, f32[32,128]{1,0:T(8,128)} %bitcast.14), custom_call_target="tpu_custom_call" | custom-call | flops 6000000000 | bytes 524288 | tf_op jit(solution)/shard_map/species/pallas_call | solution.py:147
  31.5 9.7 %all_to_all.21 = f32[4,192,128]{2,1,0:T(8,128)S(1)} all-to-all(f32[4,192,128]{2,1,0:T(8,128)} %species.1), channel_id=1, replica_groups=mesh['z'=8,'x'=4,'y'=4,'core'=2] {'x'}, dimensions={0} | all-to-all | bytes 786432 | tf_op jit(solution)/shard_map/all_to_all | solution.py:198
  41.1 0.2 broadcast_in_dim.15
  41.3 20.9 %all_to_all.22.own_ref = f32[4,4,192,128]{3,2,1,0:T(8,128)S(1)} all-to-all(f32[4,4,192,128]{3,2,1,0:T(8,128)S(1)} %broadcast_in_dim.15), channel_id=1, replica_groups=mesh['z'=8,'x'=4,'y'=4,'core'=2] {'y'}, dimensions={0} | all-to-all | bytes 3145728 | tf_op jit(solution)/shard_map/all_to_all | solution.py:198
  62.2 0.0 copy-start
  62.2 4.8 %collective-permute-start = (f32[4,4,192,128]{3,2,1,0:T(8,128)S(1)}, f32[4,4,192,128]{3,2,1,0:T(8,128)S(1)}, u32[]{:S(2)}, u32[]{:S(2)}) collective-permute-start(f32[4,4,192,128]{3,2,1,0:T(8,128)S(1)} %all_to_all.22.own_ref), channel_id=1, source_target_pairs={{0,1},{1,0},{2,3},{3,2},{4,5},{5,4},{6,7},{7,6},{8,9},{9,8},{10,11... | collective-permute-start | bytes 4718600 | tf_op jit(solution)/shard_map/ppermute | solution.py:214
  66.9 3.0 %collective-permute-done.other_ref = f32[4,4,192,128]{3,2,1,0:T(8,128)S(1)} collective-permute-done((f32[4,4,192,128]{3,2,1,0:T(8,128)S(1)}, f32[4,4,192,128]{3,2,1,0:T(8,128)S(1)}, u32[]{:S(2)}, u32[]{:S(2)}) %collective-permute-start) | collective-permute-done | bytes 1572896 | tf_op jit(solution)/shard_map/ppermute | solution.py:214
  70.0 0.0 copy-start.1
  70.0 0.0 copy-done
  70.0 1.2 copy-done.1
  71.1 96.5 %lay.1 = (f32[4,2,4,128,128]{4,3,2,1,0:T(8,128)}, f32[4,2,4,64,128]{4,3,2,1,0:T(8,128)}) custom-call(s32[1]{0:T(128)} %bitcast.core_ref, f32[4,4,192,128]{3,2,1,0:T(8,128)} %copy-done, f32[4,4,192,128]{3,2,1,0:T(8,128)} %copy-done.1), custom_call_target="tpu_custom_call" | custom-call | tf_op jit(solution)/shard_map/lay/pallas_call | solution.py:184
Async XLA Ops:
  2.1 20.4 %all-to-all-start = ((f32[32,1,128]{2,1,0:T(1,128)}), f32[32,1,128]{2,1,0:T(1,128)S(1)}, u32[]{:S(2)}, u32[]{:S(2)}) async-start(f32[32,1,128]{2,1,0:T(1,128)} %bitcast.6), calls=%async_computation | async-start | bytes 32768 | tf_op jit(solution)/shard_map/all_to_all | solution.py:198
  22.5 0.6 copy-start.2
  62.2 7.8 %copy-start = (f32[4,4,192,128]{3,2,1,0:T(8,128)}, f32[4,4,192,128]{3,2,1,0:T(8,128)S(1)}, u32[]{:S(2)}) copy-start(f32[4,4,192,128]{3,2,1,0:T(8,128)S(1)} %all_to_all.22.own_ref) | copy-start | bytes 4718596
  62.2 7.8 %collective-permute-start = (f32[4,4,192,128]{3,2,1,0:T(8,128)S(1)}, f32[4,4,192,128]{3,2,1,0:T(8,128)S(1)}, u32[]{:S(2)}, u32[]{:S(2)}) collective-permute-start(f32[4,4,192,128]{3,2,1,0:T(8,128)S(1)} %all_to_all.22.own_ref), channel_id=1, source_target_pairs={{0,1},{1,0},{2,3},{3,2},{4,5},{5,4},{6,7},{7,6},{8,9},{9,8},{10,11... | collective-permute-start | bytes 4718600 | tf_op jit(solution)/shard_map/ppermute | solution.py:214
  70.0 1.2 copy-start.1

commit v3 on v2

--- a/solution.py
+++ b/solution.py
@@ -8,6 +8,7 @@
 
 ITERS = 3
 CHUNKS = 1
+PIECES = 2
 LANES = 128
 COARSE = 8
 FINE = 16
@@ -136,66 +137,70 @@
             out_ref[x, rows, :] = jnp.concatenate([v[2 * x : 2 * x + 2] for v in values], axis=0)
         return 0
 
-    rows = lam_ref.shape[1]
-    lax.fori_loop(0, rows // 4, body, 0)
-    for x in range(4):
-        out_ref[x, 2 * rows :, :] = lam_ref[0]
-
-
-def species(x, lam, curve, table):
-    rows = lam.shape[1]
+    lax.fori_loop(0, lam_ref.shape[1] // 4, body, 0)
+
+
+def species(x, lam, curve, table, piece):
+    rows = lam.shape[1] // PIECES
     return pl.pallas_call(
         species_kernel,
-        out_shape=jax.ShapeDtypeStruct((4, 3 * rows, LANES), jnp.float32),
+        out_shape=jax.ShapeDtypeStruct((4, 2 * rows, LANES), jnp.float32),
         grid_spec=pltpu.PrefetchScalarGridSpec(
             num_scalar_prefetch=1,
             grid=(1,),
             in_specs=[
-                pl.BlockSpec((1, rows, LANES), lambda g, x: (0, 0, 0)),
-                pl.BlockSpec((1, 1, rows, LANES), lambda g, x: (0, x[0], 0, 0)),
+                pl.BlockSpec((1, rows, LANES), lambda g, x: (0, piece, 0)),
+                pl.BlockSpec((1, 1, rows, LANES), lambda g, x: (0, x[0], piece, 0)),
                 pl.BlockSpec((32, LANES), lambda g, x: (0, 0)),
             ],
-            out_specs=pl.BlockSpec((4, 3 * rows, LANES), lambda g, x: (0, 0, 0)),
+            out_specs=pl.BlockSpec((4, 2 * rows, LANES), lambda g, x: (0, 0, 0)),
             scratch_shapes=[pltpu.VMEM((LANES, 32), jnp.float32)],
         ),
-        cost_estimate=pl.CostEstimate(flops=6 * 10**9, bytes_accessed=1 << 19, transcendentals=0),
+        cost_estimate=pl.CostEstimate(
+            flops=12 * 10**9 // PIECES, bytes_accessed=1 << 19, transcendentals=0
+        ),
         name="species",
     )(x, lam, curve, table)
 
 
-def lay_kernel(core_ref, own_ref, other_ref, species_ref, lam_ref, sems):
-    rows = lam_ref.shape[3]
-    copies = []
-    for flip, blocks in ((0, own_ref), (1, other_ref)):
-        core = core_ref[0] ^ flip
+def lay_kernel(core_ref, *refs):
+    blocks, (out_ref, sems) = refs[:-2], refs[-2:]
+    started = []
+    for n, block in enumerate(blocks):
+        piece, core = n // 2, core_ref[0] ^ (n % 2)
         for y in range(4):
-            copies.append((blocks.at[y, :, pl.ds(0, 2 * rows), :], species_ref.at[y, core]))
-            copies.append((blocks.at[y, :, pl.ds(2 * rows, rows), :], lam_ref.at[y, core]))
-    started = [pltpu.make_async_copy(a, b, sems.at[i]) for i, (a, b) in enumerate(copies)]
-    for copy in started:
-        copy.start()
+            copy = pltpu.make_async_copy(
+                block.at[:, y], out_ref.at[y, core, :, piece], sems.at[4 * n + y]
+            )
+            copy.start()
+            started.append(copy)
     for copy in started:
         copy.wait()
 
 
-def lay(core, own, other):
-    anywhere = pl.BlockSpec(memory_space=pl.ANY)
-    rows = own.shape[2] // 3
+def lay(core, *blocks):
+    rows = blocks[0].shape[2]
     return pl.pallas_call(
         lay_kernel,
-        out_shape=[
-            jax.ShapeDtypeStruct((4, 2, 4, 2 * rows, LANES), jnp.float32),
-            jax.ShapeDtypeStruct((4, 2, 4, rows, LANES), jnp.float32),
-        ],
-        in_specs=[pl.BlockSpec(memory_space=pltpu.SMEM), anywhere, anywhere],
-        out_specs=[anywhere] * 2,
-        scratch_shapes=[pltpu.SemaphoreType.DMA((16,))],
+        out_shape=jax.ShapeDtypeStruct((4, 2, 4, len(blocks) // 2, rows, LANES), jnp.float32),
+        in_specs=[pl.BlockSpec(memory_space=pltpu.SMEM)]
+        + [pl.BlockSpec(memory_space=pltpu.VMEM)] * len(blocks),
+        out_specs=pl.BlockSpec(memory_space=pl.ANY),
+        scratch_shapes=[pltpu.SemaphoreType.DMA((4 * len(blocks),))],
+        cost_estimate=pl.CostEstimate(flops=2 * 10**9, bytes_accessed=1 << 21, transcendentals=0),
         name="lay",
-    )(core, own, other)
+    )(core, *blocks)
 
 
 def exchange(array, axes):
     return lax.all_to_all(array, axes, split_axis=0, concat_axis=0, tiled=True)
+
+
+def gather(block, per_x=False):
+    block = block[:, None] if per_x else block[None, None]
+    own = exchange(jnp.broadcast_to(block, (4, 4, *block.shape[2:])).reshape(16, *block.shape[2:]), ("x", "y"))
+    own = own.reshape(4, 4, *block.shape[2:])
+    return [own, lax.ppermute(own, "core", [(0, 1), (1, 0)])]
 
 
 def per_device(slope, curvature, target_mean, target_var, table):
@@ -208,11 +213,11 @@
     rows = bins // (4 * LANES)
     args = [a.reshape(1, 4, rows, LANES) for a in (slope, curvature, target_mean, target_var)]
     lam = newton(x, *args)
-    sent = species(x, lam, args[1], points)
-    ring = exchange(sent, "x")
-    own = exchange(jnp.broadcast_to(ring[None], (4, *ring.shape)), "y")
-    other = lax.ppermute(own, "core", [(0, 1), (1, 0)])
-    values, final_slope = lay(core, own, other)
+    lam_blocks = gather(lam[0])
+    pieces = []
+    for piece in range(PIECES):
+        pieces += gather(species(x, lam, args[1], points, piece), per_x=True)
+    values, final_slope = lay(core, *pieces), lay(core, *lam_blocks)
     values = jnp.transpose(values.reshape(-1, 2, LANES), (1, 0, 2)).reshape(2, -1)
     return values, final_slope.reshape(-1)
 

time: 168 us -> 81.5 us (0.49)
  Pallas kernels: 112 us -> 22.2 us
  blocking collectives: 30.6 us -> 0 us
  starting transfers between devices: 16.6 us -> 34.5 us
  waiting for transfers between devices: 4.37 us -> 14 us
  local copies, waits for them, and re-layouts: 3.38 us -> 9.26 us
    pallas_call x2 -> x4, Pallas kernels: 105 us -> 15 us  [the longest x2 9.85 us: species(): pl.pallas_call(species_kernel, out_shape=jax.ShapeDtypeStruct((4, 2 * row...]
    all_to_all x2 -> x0, blocking collectives: 30.6 us -> none  [exchange(): return lax.all_to_all(array, axes, split_axis=0, concat_axis=0, tiled=True)]
    all_to_all x1 -> x4, waiting for transfers between devices: 1.33 us -> 14 us  [exchange(): return lax.all_to_all(array, axes, split_axis=0, concat_axis=0, tiled=True)]
    all_to_all x1 -> x4, starting transfers between devices: 11.9 us -> 24.4 us  [exchange(): return lax.all_to_all(array, axes, split_axis=0, concat_axis=0, tiled=True)]
    ppermute x1 -> x3, starting transfers between devices: 4.75 us -> 10.1 us  [gather(): return [own, lax.ppermute(own, 'core', [(0, 1), (1, 0)])]]
    broadcast_in_dim x1 -> x2, local copies, waits for them, and re-layouts: 0.15 us -> 3.73 us  [gather(): jnp.broadcast_to(block, (4, 4, *block.shape[2:]))]
    ppermute x1 -> x3, waiting for transfers between devices: 3.04 us -> 0.01 us  [gather(): return [own, lax.ppermute(own, 'core', [(0, 1), (1, 0)])]]
  transfers between devices with their start and end apart: 2 -> 7, of which waited for: 2 -> 4; matrix products, arithmetic and copies ran while one was open for 0% -> 0% of each run, Pallas kernels for 4% -> 24%
where the time goes in v3:
time: 81.5 us; the launch traced here: 80.6 us
  starting transfers between devices  34.5 us (42%)
  Pallas kernels  22.2 us (27%)
  waiting for transfers between devices  14 us (17%)
  local copies, waits for them, and re-layouts  9.26 us (11%)
    all_to_all x4, starting transfers between devices, exchange(): return lax.all_to_all(array, axes, split_axis=0, concat_axis=0, tiled=True)  24.4 us
    all_to_all x4, waiting for transfers between devices, exchange(): return lax.all_to_all(array, axes, split_axis=0, concat_axis=0, tiled=True)  14 us
    ppermute x3, starting transfers between devices, gather(): return [own, lax.ppermute(own, 'core', [(0, 1), (1, 0)])]  10.1 us
    pallas_call x2, Pallas kernels, species(): pl.pallas_call(species_kernel, out_shape=jax.ShapeDtypeStruct((4, 2 * row...  9.85 us
    pallas_call x1, Pallas kernels, newton(): pl.pallas_call(newton_kernel, out_shape=jax.ShapeDtypeStruct((CHUNKS, row...  7.16 us
    pallas_call x2, Pallas kernels, lay(): pl.pallas_call(lay_kernel, out_shape=jax.ShapeDtypeStruct((4, 2, 4, len(b...  5.17 us
    broadcast_in_dim x2, local copies, waits for them, and re-layouts, gather(): jnp.broadcast_to(block, (4, 4, *block.shape[2:]))  3.73 us
    unnamed x15, local copies, waits for them, and re-layouts  3.23 us
  transfers between devices with their start and end apart: 7, of which 4 were waited for; matrix products, arithmetic and copies ran while one was open for 0% of the time, Pallas kernels for 24%

profile of v3, /device:TPU:1, one launch (start us, length us, event | category | flops | bytes accessed | tf_op | source)
XLA Modules:
  0.0 80.6 jit_solution(3209575177635206988)
XLA Ops:
  0.6 0.8 copy.10
  1.4 0.1 broadcast_in_dim.10
  1.5 0.6 broadcast_in_dim.11
  2.1 11.9 %all-to-all-start = ((f32[32,1,128]{2,1,0:T(1,128)}), f32[32,1,128]{2,1,0:T(1,128)S(1)}, u32[]{:S(2)}, u32[]{:S(2)}) async-start(f32[32,1,128]{2,1,0:T(1,128)} %bitcast.6), calls=%async_computation | async-start | bytes 32768 | tf_op jit(solution)/shard_map/all_to_all | solution.py:196
  14.0 7.2 %newton.1.lam_ref = f32[1,64,128]{2,1,0:T(8,128)} custom-call(s32[1]{0:T(128)} %bitcast.1.x_ref, f32[1,4,64,128]{3,2,1,0:T(8,128)} %bitcast.29, f32[1,4,64,128]{3,2,1,0:T(8,128)} %bitcast.32, f32[1,4,64,128]{3,2,1,0:T(8,128)} %bitcast.30, f32[1,4,64,128]{3,2,1,0:T(8,128)} %bitcast.31), custom_call_target="tpu_custom_call" | custom-call | flops 12000000000 | bytes 262144 | tf_op jit(solution)/shard_map/newton/pallas_call | solution.py:78
  21.1 1.3 %all-to-all-done = f32[32,1,128]{2,1,0:T(1,128)S(1)} async-done(((f32[32,1,128]{2,1,0:T(1,128)}), f32[32,1,128]{2,1,0:T(1,128)S(1)}, u32[]{:S(2)}, u32[]{:S(2)}) %all-to-all-start) | async-done | bytes 16416 | tf_op jit(solution)/shard_map/all_to_all | solution.py:196
  22.5 0.0 copy-start.3
  22.5 1.6 %reshape.70 = f32[16,64,128]{2,1,0:T(8,128)} broadcast(f32[64,128]{1,0:T(8,128)} %bitcast.26), dimensions={1,2} | broadcast | bytes 557056 | tf_op jit(solution)/shard_map/reshape | solution.py:201
  24.1 5.4 %all-to-all-start.3 = ((f32[16,64,128]{2,1,0:T(8,128)}), f32[16,64,128]{2,1,0:T(8,128)S(1)}, u32[]{:S(2)}, u32[]{:S(2)}) async-start(f32[16,64,128]{2,1,0:T(8,128)} %reshape.70), calls=%async_computation.3 | async-start | bytes 1048576 | tf_op jit(solution)/shard_map/all_to_all | solution.py:196
  29.5 0.0 copy-done.3
  29.5 4.9 %species.3 = f32[4,64,128]{2,1,0:T(8,128)} custom-call(s32[1]{0:T(128)} %bitcast.1.x_ref, f32[1,64,128]{2,1,0:T(8,128)} %newton.1.lam_ref, f32[1,4,64,128]{3,2,1,0:T(8,128)} %bitcast.33, f32[32,128]{1,0:T(8,128)} %bitcast.27), custom_call_target="tpu_custom_call" | custom-call | flops 6000000000 | bytes 524288 | tf_op jit(solution)/shard_map/species/pallas_call | solution.py:145
  34.4 4.3 %all-to-all-done.3 = f32[16,64,128]{2,1,0:T(8,128)S(1)} async-done(((f32[16,64,128]{2,1,0:T(8,128)}), f32[16,64,128]{2,1,0:T(8,128)S(1)}, u32[]{:S(2)}, u32[]{:S(2)}) %all-to-all-start.3) | async-done | bytes 524320 | tf_op jit(solution)/shard_map/all_to_all | solution.py:196
  38.7 0.0 copy-start
  38.7 1.9 %broadcast_in_dim.13 = f32[4,4,64,128]{3,2,1,0:T(8,128)} broadcast(f32[4,64,128]{2,1,0:T(8,128)} %species.3), dimensions={0,2,3} | broadcast | bytes 655360 | tf_op jit(solution)/shard_map/broadcast_in_dim | solution.py:201
  40.6 3.6 %all-to-all-start.2 = ((f32[16,64,128]{2,1,0:T(8,128)}), f32[16,64,128]{2,1,0:T(8,128)S(1)}, u32[]{:S(2)}, u32[]{:S(2)}) async-start(f32[16,64,128]{2,1,0:T(8,128)} %bitcast.10), calls=%async_computation.2 | async-start | bytes 1048576 | tf_op jit(solution)/shard_map/all_to_all | solution.py:196
  44.2 4.9 %species.2 = f32[4,64,128]{2,1,0:T(8,128)} custom-call(s32[1]{0:T(128)} %bitcast.1.x_ref, f32[1,64,128]{2,1,0:T(8,128)} %newton.1.lam_ref, f32[1,4,64,128]{3,2,1,0:T(8,128)} %bitcast.34, f32[32,128]{1,0:T(8,128)} %bitcast.28), custom_call_target="tpu_custom_call" | custom-call | flops 6000000000 | bytes 524288 | tf_op jit(solution)/shard_map/species/pallas_call | solution.py:145
  49.1 4.0 %all-to-all-done.2 = f32[16,64,128]{2,1,0:T(8,128)S(1)} async-done(((f32[16,64,128]{2,1,0:T(8,128)}), f32[16,64,128]{2,1,0:T(8,128)S(1)}, u32[]{:S(2)}, u32[]{:S(2)}) %all-to-all-start.2) | async-done | bytes 524320 | tf_op jit(solution)/shard_map/all_to_all | solution.py:196
  53.1 0.0 copy-start.1
  53.1 1.9 %broadcast_in_dim.12 = f32[4,4,64,128]{3,2,1,0:T(8,128)} broadcast(f32[4,64,128]{2,1,0:T(8,128)} %species.2), dimensions={0,2,3} | broadcast | bytes 655360 | tf_op jit(solution)/shard_map/broadcast_in_dim | solution.py:201
  55.0 3.6 %all-to-all-start.1 = ((f32[16,64,128]{2,1,0:T(8,128)}), f32[16,64,128]{2,1,0:T(8,128)S(1)}, u32[]{:S(2)}, u32[]{:S(2)}) async-start(f32[16,64,128]{2,1,0:T(8,128)} %bitcast.8), calls=%async_computation.1 | async-start | bytes 1048576 | tf_op jit(solution)/shard_map/all_to_all | solution.py:196
  58.5 0.0 copy-done
  58.6 4.5 %collective-permute-start.2 = (f32[4,4,64,128]{3,2,1,0:T(8,128)S(1)}, f32[4,4,64,128]{3,2,1,0:T(8,128)S(1)}, u32[]{:S(2)}, u32[]{:S(2)}) collective-permute-start(f32[4,4,64,128]{3,2,1,0:T(8,128)S(1)} %bitcast.20), channel_id=1, source_target_pairs={{0,1},{1,0},{2,3},{3,2},{4,5},{5,4},{6,7},{7,6},{8,9},{9,8},{10,11... | collective-permute-start | bytes 1572872 | tf_op jit(solution)/shard_map/ppermute | solution.py:203
  63.0 0.1 collective-permute-start.1
  63.1 4.4 %all-to-all-done.1 = f32[16,64,128]{2,1,0:T(8,128)S(1)} async-done(((f32[16,64,128]{2,1,0:T(8,128)}), f32[16,64,128]{2,1,0:T(8,128)S(1)}, u32[]{:S(2)}, u32[]{:S(2)}) %all-to-all-start.1) | async-done | bytes 524320 | tf_op jit(solution)/shard_map/all_to_all | solution.py:196
  67.5 0.0 copy-start.2
  67.5 5.5 %collective-permute-start = (f32[4,4,64,128]{3,2,1,0:T(8,128)S(1)}, f32[4,4,64,128]{3,2,1,0:T(8,128)S(1)}, u32[]{:S(2)}, u32[]{:S(2)}) collective-permute-start(f32[4,4,64,128]{3,2,1,0:T(8,128)S(1)} %bitcast.24), channel_id=1, source_target_pairs={{0,1},{1,0},{2,3},{3,2},{4,5},{5,4},{6,7},{7,6},{8,9},{9,8},{10,11... | collective-permute-start | bytes 1572872 | tf_op jit(solution)/shard_map/ppermute | solution.py:203
  73.0 0.0 collective-permute-done.2.refs_1_
  73.0 0.0 copy-start.5
  73.0 0.8 %copy-done.5 = f32[4,4,64,128]{3,2,1,0:T(8,128)} copy-done((f32[4,4,64,128]{3,2,1,0:T(8,128)}, f32[4,4,64,128]{3,2,1,0:T(8,128)S(1)}, u32[]{:S(2)}) %copy-start.5) | copy-done | bytes 524312
  73.8 2.2 %lay.3 = f32[4,2,4,1,64,128]{5,4,3,2,1,0:T(8,128)} custom-call(s32[1]{0:T(128)} %bitcast.core_ref, f32[4,4,64,128]{3,2,1,0:T(8,128)} %bitcast.21, f32[4,4,64,128]{3,2,1,0:T(8,128)} %copy-done.5), custom_call_target="tpu_custom_call" | custom-call | flops 2000000000 | bytes 2097152 | tf_op jit(solution)/shard_map/lay/pallas_call | solution.py:183
  76.0 0.0 copy-done.1
  76.0 0.0 copy-done.2
  76.0 0.0 collective-permute-done.1.refs_3_
  76.1 0.0 copy-start.4
  76.1 0.0 collective-permute-done.refs_1_
  76.1 0.8 copy-done.4
  76.9 0.0 copy-start.6
  76.9 0.8 %copy-done.6 = f32[4,4,64,128]{3,2,1,0:T(8,128)} copy-done((f32[4,4,64,128]{3,2,1,0:T(8,128)}, f32[4,4,64,128]{3,2,1,0:T(8,128)S(1)}, u32[]{:S(2)}) %copy-start.6) | copy-done | bytes 524312
  77.7 3.0 %lay.2 = f32[4,2,4,2,64,128]{5,4,3,2,1,0:T(8,128)} custom-call(s32[1]{0:T(128)} %bitcast.core_ref, f32[4,4,64,128]{3,2,1,0:T(8,128)} %bitcast.25, f32[4,4,64,128]{3,2,1,0:T(8,128)} %copy-done.6, f32[4,4,64,128]{3,2,1,0:T(8,128)} %bitcast.23, f32[4,4,64,128]{3,2,1,0:T(8,128)} %copy-done.4), custom_call_target="tpu_custom_call" | custom-call | flops 2000000000 | bytes 2097152 | tf_op jit(solution)/shard_map/lay/pallas_call | solution.py:183
Async XLA Ops:
  2.1 20.4 %all-to-all-start = ((f32[32,1,128]{2,1,0:T(1,128)}), f32[32,1,128]{2,1,0:T(1,128)S(1)}, u32[]{:S(2)}, u32[]{:S(2)}) async-start(f32[32,1,128]{2,1,0:T(1,128)} %bitcast.6), calls=%async_computation | async-start | bytes 32768 | tf_op jit(solution)/shard_map/all_to_all | solution.py:196
  22.5 7.0 %copy-start.3 = (f32[32,1,128]{2,1,0:T(1,128)}, f32[32,1,128]{2,1,0:T(1,128)S(1)}, u32[]{:S(2)}) copy-start(f32[32,1,128]{2,1,0:T(1,128)S(1)} %all-to-all-done) | copy-start | bytes 49156
  24.1 14.6 %all-to-all-start.3 = ((f32[16,64,128]{2,1,0:T(8,128)}), f32[16,64,128]{2,1,0:T(8,128)S(1)}, u32[]{:S(2)}, u32[]{:S(2)}) async-start(f32[16,64,128]{2,1,0:T(8,128)} %reshape.70), calls=%async_computation.3 | async-start | bytes 1048576 | tf_op jit(solution)/shard_map/all_to_all | solution.py:196
  38.7 19.8 %copy-start = (f32[16,64,128]{2,1,0:T(8,128)}, f32[16,64,128]{2,1,0:T(8,128)S(1)}, u32[]{:S(2)}) copy-start(f32[16,64,128]{2,1,0:T(8,128)S(1)} %all-to-all-done.3) | copy-start | bytes 1572868
  40.6 12.5 %all-to-all-start.2 = ((f32[16,64,128]{2,1,0:T(8,128)}), f32[16,64,128]{2,1,0:T(8,128)S(1)}, u32[]{:S(2)}, u32[]{:S(2)}) async-start(f32[16,64,128]{2,1,0:T(8,128)} %bitcast.10), calls=%async_computation.2 | async-start | bytes 1048576 | tf_op jit(solution)/shard_map/all_to_all | solution.py:196
  53.1 22.9 %copy-start.1 = (f32[16,64,128]{2,1,0:T(8,128)}, f32[16,64,128]{2,1,0:T(8,128)S(1)}, u32[]{:S(2)}) copy-start(f32[16,64,128]{2,1,0:T(8,128)S(1)} %all-to-all-done.2) | copy-start | bytes 1572868
  55.0 12.5 %all-to-all-start.1 = ((f32[16,64,128]{2,1,0:T(8,128)}), f32[16,64,128]{2,1,0:T(8,128)S(1)}, u32[]{:S(2)}, u32[]{:S(2)}) async-start(f32[16,64,128]{2,1,0:T(8,128)} %bitcast.8), calls=%async_computation.1 | async-start | bytes 1048576 | tf_op jit(solution)/shard_map/all_to_all | solution.py:196
  58.6 14.4 %collective-permute-start.2 = (f32[4,4,64,128]{3,2,1,0:T(8,128)S(1)}, f32[4,4,64,128]{3,2,1,0:T(8,128)S(1)}, u32[]{:S(2)}, u32[]{:S(2)}) collective-permute-start(f32[4,4,64,128]{3,2,1,0:T(8,128)S(1)} %bitcast.20), channel_id=1, source_target_pairs={{0,1},{1,0},{2,3},{3,2},{4,5},{5,4},{6,7},{7,6},{8,9},{9,8},{10,11... | collective-permute-start | bytes 1572872 | tf_op jit(solution)/shard_map/ppermute | solution.py:203
  63.0 13.0 %collective-permute-start.1 = (f32[4,4,64,128]{3,2,1,0:T(8,128)S(1)}, f32[4,4,64,128]{3,2,1,0:T(8,128)S(1)}, u32[]{:S(2)}, u32[]{:S(2)}) collective-permute-start(f32[4,4,64,128]{3,2,1,0:T(8,128)S(1)} %bitcast.22), channel_id=1, source_target_pairs={{0,1},{1,0},{2,3},{3,2},{4,5},{5,4},{6,7},{7,6},{8,9},{9,8},{10,11... | collective-permute-start | bytes 1572872 | tf_op jit(solution)/shard_map/ppermute | solution.py:203
  67.5 8.6 %copy-start.2 = (f32[16,64,128]{2,1,0:T(8,128)}, f32[16,64,128]{2,1,0:T(8,128)S(1)}, u32[]{:S(2)}) copy-start(f32[16,64,128]{2,1,0:T(8,128)S(1)} %all-to-all-done.1) | copy-start | bytes 1572868
  67.5 8.6 %collective-permute-start = (f32[4,4,64,128]{3,2,1,0:T(8,128)S(1)}, f32[4,4,64,128]{3,2,1,0:T(8,128)S(1)}, u32[]{:S(2)}, u32[]{:S(2)}) collective-permute-start(f32[4,4,64,128]{3,2,1,0:T(8,128)S(1)} %bitcast.24), channel_id=1, source_target_pairs={{0,1},{1,0},{2,3},{3,2},{4,5},{5,4},{6,7},{7,6},{8,9},{9,8},{10,11... | collective-permute-start | bytes 1572872 | tf_op jit(solution)/shard_map/ppermute | solution.py:203
  73.0 0.8 %copy-start.5 = (f32[4,4,64,128]{3,2,1,0:T(8,128)}, f32[4,4,64,128]{3,2,1,0:T(8,128)S(1)}, u32[]{:S(2)}) copy-start(f32[4,4,64,128]{3,2,1,0:T(8,128)S(1)} %collective-permute-done.2.refs_1_) | copy-start | bytes 1572868
  76.1 0.8 %copy-start.4 = (f32[4,4,64,128]{3,2,1,0:T(8,128)}, f32[4,4,64,128]{3,2,1,0:T(8,128)S(1)}, u32[]{:S(2)}) copy-start(f32[4,4,64,128]{3,2,1,0:T(8,128)S(1)} %collective-permute-done.1.refs_3_) | copy-start | bytes 1572868
  76.9 0.8 %copy-start.6 = (f32[4,4,64,128]{3,2,1,0:T(8,128)}, f32[4,4,64,128]{3,2,1,0:T(8,128)S(1)}, u32[]{:S(2)}) copy-start(f32[4,4,64,128]{3,2,1,0:T(8,128)S(1)} %collective-permute-done.refs_1_) | copy-start | bytes 1572868

commit v4 on v2

--- a/solution.py
+++ b/solution.py
@@ -1,3 +1,5 @@
+import functools
+
 import jax
 import jax.numpy as jnp
 import numpy as np
@@ -81,7 +83,7 @@
             num_scalar_prefetch=1,
             grid=(1,),
             in_specs=[mine] * 4,
-            out_specs=pl.BlockSpec((CHUNKS, rows, LANES), lambda g, x: (0, 0, 0)),
+            out_specs=pl.BlockSpec(memory_space=pltpu.VMEM),
             scratch_shapes=[
                 pltpu.VMEM((COARSE * FINE, 8, LANES), jnp.float32),
                 pltpu.VMEM((COARSE * FINE, 8, LANES), jnp.float32),
@@ -93,7 +95,7 @@
     )(x, slope, curve, mean, var)
 
 
-def species_kernel(x_ref, lam_ref, curve_ref, table_ref, out_ref, turned_ref):
+def species_kernel(x_ref, lam_ref, curve_ref, table_ref, sent_ref, turned_ref, out_ref, sems):
     turned_ref[...] = jnp.transpose(table_ref[...])
     table = jnp.concatenate([turned_ref[pl.ds(p, 8, stride=16), :] for p in range(16)], axis=1)
     high = table.astype(jnp.bfloat16).astype(jnp.float32)
@@ -137,40 +139,50 @@
         return 0
 
     rows = lam_ref.shape[1]
-    lax.fori_loop(0, rows // 4, body, 0)
     for x in range(4):
         out_ref[x, 2 * rows :, :] = lam_ref[0]
+    lax.fori_loop(0, rows // 4, body, 0)
+    copies = [pltpu.make_async_copy(out_ref, sent_ref.at[:, y], sems.at[y]) for y in range(4)]
+    for copy in copies:
+        copy.start()
+    for copy in copies:
+        copy.wait()
 
 
 def species(x, lam, curve, table):
     rows = lam.shape[1]
     return pl.pallas_call(
         species_kernel,
-        out_shape=jax.ShapeDtypeStruct((4, 3 * rows, LANES), jnp.float32),
+        out_shape=jax.ShapeDtypeStruct((4, 4, 3 * rows, LANES), jnp.float32),
         grid_spec=pltpu.PrefetchScalarGridSpec(
             num_scalar_prefetch=1,
             grid=(1,),
             in_specs=[
-                pl.BlockSpec((1, rows, LANES), lambda g, x: (0, 0, 0)),
+                pl.BlockSpec(memory_space=pltpu.VMEM),
                 pl.BlockSpec((1, 1, rows, LANES), lambda g, x: (0, x[0], 0, 0)),
-                pl.BlockSpec((32, LANES), lambda g, x: (0, 0)),
+                pl.BlockSpec(memory_space=pltpu.VMEM),
             ],
-            out_specs=pl.BlockSpec((4, 3 * rows, LANES), lambda g, x: (0, 0, 0)),
-            scratch_shapes=[pltpu.VMEM((LANES, 32), jnp.float32)],
+            out_specs=pl.BlockSpec(memory_space=pl.ANY),
+            scratch_shapes=[
+                pltpu.VMEM((LANES, 32), jnp.float32),
+                pltpu.VMEM((4, 3 * rows, LANES), jnp.float32),
+                pltpu.SemaphoreType.DMA((4,)),
+            ],
         ),
         cost_estimate=pl.CostEstimate(flops=6 * 10**9, bytes_accessed=1 << 19, transcendentals=0),
+        compiler_params=pltpu.CompilerParams(vmem_limit_bytes=16 << 20),
         name="species",
     )(x, lam, curve, table)
 
 
-def lay_kernel(core_ref, own_ref, other_ref, species_ref, lam_ref, sems):
+def lay_kernel(flip, core_ref, blocks_ref, *refs):
+    species_ref, lam_ref, sems = refs[-3:]
     rows = lam_ref.shape[3]
+    core = core_ref[0] ^ flip
     copies = []
-    for flip, blocks in ((0, own_ref), (1, other_ref)):
-        core = core_ref[0] ^ flip
-        for y in range(4):
-            copies.append((blocks.at[y, :, pl.ds(0, 2 * rows), :], species_ref.at[y, core]))
-            copies.append((blocks.at[y, :, pl.ds(2 * rows, rows), :], lam_ref.at[y, core]))
+    for y in range(4):
+        copies.append((blocks_ref.at[:, y, pl.ds(0, 2 * rows), :], species_ref.at[y, core]))
+        copies.append((blocks_ref.at[:, y, pl.ds(2 * rows, rows), :], lam_ref.at[y, core]))
     started = [pltpu.make_async_copy(a, b, sems.at[i]) for i, (a, b) in enumerate(copies)]
     for copy in started:
         copy.start()
@@ -178,20 +190,24 @@
         copy.wait()
 
 
-def lay(core, own, other):
+def lay(core, blocks, flip, laid=()):
     anywhere = pl.BlockSpec(memory_space=pl.ANY)
-    rows = own.shape[2] // 3
+    rows = blocks.shape[2] // 3
     return pl.pallas_call(
-        lay_kernel,
+        functools.partial(lay_kernel, flip),
         out_shape=[
             jax.ShapeDtypeStruct((4, 2, 4, 2 * rows, LANES), jnp.float32),
             jax.ShapeDtypeStruct((4, 2, 4, rows, LANES), jnp.float32),
         ],
-        in_specs=[pl.BlockSpec(memory_space=pltpu.SMEM), anywhere, anywhere],
+        in_specs=[pl.BlockSpec(memory_space=pltpu.SMEM), pl.BlockSpec(memory_space=pltpu.VMEM)]
+        + [anywhere] * len(laid),
         out_specs=[anywhere] * 2,
-        scratch_shapes=[pltpu.SemaphoreType.DMA((16,))],
+        input_output_aliases={2: 0, 3: 1} if laid else {},
+        scratch_shapes=[pltpu.SemaphoreType.DMA((8,))],
+        cost_estimate=pl.CostEstimate(flops=2 * 10**9, bytes_accessed=3 << 20, transcendentals=0),
+        compiler_params=pltpu.CompilerParams(vmem_limit_bytes=4 << 20),
         name="lay",
-    )(core, own, other)
+    )(core, blocks, *laid)
 
 
 def exchange(array, axes):
@@ -209,10 +225,9 @@
     args = [a.reshape(1, 4, rows, LANES) for a in (slope, curvature, target_mean, target_var)]
     lam = newton(x, *args)
     sent = species(x, lam, args[1], points)
-    ring = exchange(sent, "x")
-    own = exchange(jnp.broadcast_to(ring[None], (4, *ring.shape)), "y")
+    own = exchange(sent.reshape(16, *sent.shape[2:]), ("x", "y")).reshape(sent.shape)
     other = lax.ppermute(own, "core", [(0, 1), (1, 0)])
-    values, final_slope = lay(core, own, other)
+    values, final_slope = lay(core, other, 1, lay(core, own, 0))
     values = jnp.transpose(values.reshape(-1, 2, LANES), (1, 0, 2)).reshape(2, -1)
     return values, final_slope.reshape(-1)
 

time: 168 us -> 63.8 us (0.38)
  Pallas kernels: 112 us -> 16.7 us
  blocking collectives: 30.6 us -> 25.8 us
    pallas_call x2 -> x3, Pallas kernels: 105 us -> 9.51 us  [the longest x1 7.12 us: species(): pl.pallas_call(species_kernel, out_shape=jax.ShapeDtypeStruct((4, 4, 3 *...]
    all_to_all x2 -> x1, blocking collectives: 30.6 us -> 25.8 us  [exchange(): return lax.all_to_all(array, axes, split_axis=0, concat_axis=0, tiled=True)]
  transfers between devices with their start and end apart: 2 -> 2, of which waited for: 2 -> 2; matrix products, arithmetic and copies ran while one was open for 0% -> 0% of each run, Pallas kernels for 4% -> 13%
where the time goes in v4:
time: 63.8 us; the launch traced here: 63.6 us
  blocking collectives  25.8 us (40%)
  Pallas kernels  16.7 us (26%)
  starting transfers between devices  15 us (24%)
  waiting for transfers between devices  3.12 us (5%)
  local copies, waits for them, and re-layouts  2.24 us (4%)
  between operations  0.67 us (1%)
    all_to_all x1, blocking collectives, exchange(): return lax.all_to_all(array, axes, split_axis=0, concat_axis=0, tiled=True)  25.8 us
    all_to_all x1, starting transfers between devices, exchange(): return lax.all_to_all(array, axes, split_axis=0, concat_axis=0, tiled=True)  11.9 us
    pallas_call x1, Pallas kernels, newton(): pl.pallas_call(newton_kernel, out_shape=jax.ShapeDtypeStruct((CHUNKS, row...  7.21 us
    pallas_call x1, Pallas kernels, species(): pl.pallas_call(species_kernel, out_shape=jax.ShapeDtypeStruct((4, 4, 3 *...  7.12 us
    ppermute x1, starting transfers between devices, per_device(): other = lax.ppermute(own, 'core', [(0, 1), (1, 0)])  3.17 us
    pallas_call x2, Pallas kernels, lay(): pl.pallas_call(functools.partial(lay_kernel, flip), out_shape=[jax.ShapeD...  2.39 us
    ppermute x1, waiting for transfers between devices, per_device(): other = lax.ppermute(own, 'core', [(0, 1), (1, 0)])  1.83 us
    unnamed x5, local copies, waits for them, and re-layouts  1.54 us
  transfers between devices with their start and end apart: 2, of which 2 were waited for; matrix products, arithmetic and copies ran while one was open for 0% of the time, Pallas kernels for 13%

profile of v4, /device:TPU:1, one launch (start us, length us, event | category | flops | bytes accessed | tf_op | source)
XLA Modules:
  0.0 63.6 jit_solution(17322629557716111208)
XLA Ops:
  0.6 0.8 %copy.12 = f32[64,16]{1,0:T(8,128)S(1)} copy(f32[64,16]{0,1:T(8,128)} %param.9) | data formatting | bytes 8192 | tf_op args[4]
  1.4 0.1 broadcast_in_dim.7
  1.5 0.6 broadcast_in_dim.8
  2.1 11.9 %all-to-all-start = ((f32[32,1,128]{2,1,0:T(1,128)}), f32[32,1,128]{2,1,0:T(1,128)S(1)}, u32[]{:S(2)}, u32[]{:S(2)}) async-start(f32[32,1,128]{2,1,0:T(1,128)} %bitcast.6), calls=%async_computation | async-start | bytes 32768 | tf_op jit(solution)/shard_map/all_to_all | solution.py:214
  14.0 0.0 copy-start
  14.0 7.2 %newton.1.lam_ref = f32[1,64,128]{2,1,0:T(8,128)} custom-call(s32[1]{0:T(128)} %bitcast.1.x_ref, f32[1,4,64,128]{3,2,1,0:T(8,128)} %bitcast.22, f32[1,4,64,128]{3,2,1,0:T(8,128)} %bitcast.20, f32[1,4,64,128]{3,2,1,0:T(8,128)} %bitcast.23, f32[1,4,64,128]{3,2,1,0:T(8,128)} %bitcast.24), custom_call_target="tpu_custom_call" | custom-call | flops 12000000000 | bytes 262144 | tf_op jit(solution)/shard_map/newton/pallas_call | solution.py:79
  21.2 1.3 %all-to-all-done = f32[32,1,128]{2,1,0:T(1,128)S(1)} async-done(((f32[32,1,128]{2,1,0:T(1,128)}), f32[32,1,128]{2,1,0:T(1,128)S(1)}, u32[]{:S(2)}, u32[]{:S(2)}) %all-to-all-start) | async-done | bytes 16416 | tf_op jit(solution)/shard_map/all_to_all | solution.py:214
  22.5 0.0 copy-done
  22.5 0.0 copy-start.1
  22.5 0.8 %copy-done.1 = f32[1,64,128]{2,1,0:T(8,128)S(1)} copy-done((f32[1,64,128]{2,1,0:T(8,128)S(1)}, f32[1,64,128]{2,1,0:T(8,128)}, u32[]{:S(2)}) %copy-start.1) | copy-done | bytes 32792
  23.2 7.1 %species.1 = f32[4,4,192,128]{3,2,1,0:T(8,128)S(1)} custom-call(s32[1]{0:T(128)} %bitcast.1.x_ref, f32[1,64,128]{2,1,0:T(8,128)S(1)} %copy-done.1, f32[1,4,64,128]{3,2,1,0:T(8,128)S(1)} %bitcast.21, f32[32,128]{1,0:T(8,128)S(1)} %bitcast.19), custom_call_target="tpu_custom_call" | custom-call | flops 6000000000 | bytes 524288 | tf_op jit(solution)/shard_map/species/pallas_call | solution.py:154
  30.4 25.8 %all_to_all.16 = f32[16,192,128]{2,1,0:T(8,128)S(1)} all-to-all(f32[16,192,128]{2,1,0:T(8,128)S(1)} %bitcast.18), channel_id=1, replica_groups=mesh['z'=8,'x'=4,'y'=4,'core'=2] {'x','y'}, dimensions={0} | all-to-all | bytes 3145728 | tf_op jit(solution)/shard_map/all_to_all | solution.py:214
  56.1 3.2 %collective-permute-start = (f32[4,4,192,128]{3,2,1,0:T(8,128)S(1)}, f32[4,4,192,128]{3,2,1,0:T(8,128)S(1)}, u32[]{:S(2)}, u32[]{:S(2)}) collective-permute-start(f32[4,4,192,128]{3,2,1,0:T(8,128)S(1)} %bitcast.16), channel_id=1, source_target_pairs={{0,1},{1,0},{2,3},{3,2},{4,5},{5,4},{6,7},{7,6},{8,9},{9,8},{10,11... | collective-permute-start | bytes 4718600 | tf_op jit(solution)/shard_map/ppermute | solution.py:229
  59.3 1.2 %lay.2 = (f32[4,2,4,128,128]{4,3,2,1,0:T(8,128)}, f32[4,2,4,64,128]{4,3,2,1,0:T(8,128)}) custom-call(s32[1]{0:T(128)} %bitcast.core_ref, f32[4,4,192,128]{3,2,1,0:T(8,128)S(1)} %bitcast.17), custom_call_target="tpu_custom_call" | custom-call | flops 2000000000 | bytes 3145728 | tf_op jit(solution)/shard_map/lay/pallas_call | solution.py:196
  60.5 1.8 %collective-permute-done.blocks_ref = f32[4,4,192,128]{3,2,1,0:T(8,128)S(1)} collective-permute-done((f32[4,4,192,128]{3,2,1,0:T(8,128)S(1)}, f32[4,4,192,128]{3,2,1,0:T(8,128)S(1)}, u32[]{:S(2)}, u32[]{:S(2)}) %collective-permute-start) | collective-permute-done | bytes 1572896 | tf_op jit(solution)/shard_map/ppermute | solution.py:229
  62.4 1.2 %lay.3 = (f32[4,2,4,128,128]{4,3,2,1,0:T(8,128)}, f32[4,2,4,64,128]{4,3,2,1,0:T(8,128)}) custom-call(s32[1]{0:T(128)} %bitcast.core_ref, f32[4,4,192,128]{3,2,1,0:T(8,128)S(1)} %collective-permute-done.blocks_ref, f32[4,2,4,128,128]{4,3,2,1,0:T(8,128)} %get-tuple-element.6.refs_0_, ...), custom_call_target="tpu_custom_call", output_to_operand_aliasing={{0}: (2, {}), {1}: (3, {})} | custom-call | flops 2000000000 | bytes 3145728 | tf_op jit(solution)/shard_map/lay/pallas_call | solution.py:196
Async XLA Ops:
  2.1 20.4 %all-to-all-start = ((f32[32,1,128]{2,1,0:T(1,128)}), f32[32,1,128]{2,1,0:T(1,128)S(1)}, u32[]{:S(2)}, u32[]{:S(2)}) async-start(f32[32,1,128]{2,1,0:T(1,128)} %bitcast.6), calls=%async_computation | async-start | bytes 32768 | tf_op jit(solution)/shard_map/all_to_all | solution.py:214
  14.0 8.5 %copy-start = (f32[32768]{0:T(1024)S(1)}, f32[32768]{0:T(1024)}, u32[]{:S(2)}) copy-start(f32[32768]{0:T(1024)} %param.6) | copy-start | bytes 393220
  22.5 0.8 %copy-start.1 = (f32[1,64,128]{2,1,0:T(8,128)S(1)}, f32[1,64,128]{2,1,0:T(8,128)}, u32[]{:S(2)}) copy-start(f32[1,64,128]{2,1,0:T(8,128)} %newton.1.lam_ref) | copy-start | bytes 98308
  56.1 6.2 %collective-permute-start = (f32[4,4,192,128]{3,2,1,0:T(8,128)S(1)}, f32[4,4,192,128]{3,2,1,0:T(8,128)S(1)}, u32[]{:S(2)}, u32[]{:S(2)}) collective-permute-start(f32[4,4,192,128]{3,2,1,0:T(8,128)S(1)} %bitcast.16), channel_id=1, source_target_pairs={{0,1},{1,0},{2,3},{3,2},{4,5},{5,4},{6,7},{7,6},{8,9},{9,8},{10,11... | collective-permute-start | bytes 4718600 | tf_op jit(solution)/shard_map/ppermute | solution.py:229

commit v5 on v4

--- a/solution.py
+++ b/solution.py
@@ -9,21 +9,26 @@
 from jax.sharding import PartitionSpec as P
 
 ITERS = 3
-CHUNKS = 1
 LANES = 128
 COARSE = 8
 FINE = 16
 
 
-def newton_kernel(x_ref, slope_ref, curve_ref, mean_ref, var_ref, lam_ref, ch_ref, sh_ref, g_ref):
-    per_chunk = lam_ref.shape[1] // 8
+def newton_kernel(x_ref, *refs):
+    whole, (lam_ref, curve_ref, slope_ref, mean_ref, var_ref) = refs[:4], refs[4:9]
+    ch_ref, sh_ref, g_ref, sems = refs[9:]
+    mine = zip(whole, (slope_ref, curve_ref, mean_ref, var_ref))
+    copies = [pltpu.make_async_copy(a.at[x_ref[0]], b, sems.at[i]) for i, (a, b) in enumerate(mine)]
+    for copy in copies:
+        copy.start()
+    for copy in copies:
+        copy.wait()
 
     def body(v, _):
-        chunk = v // per_chunk
-        rows = pl.ds(pl.multiple_of((v % per_chunk) * 8, 8), 8)
-        curve = curve_ref[chunk, 0, rows, :]
-        mean = mean_ref[chunk, 0, rows, :]
-        inverse = 1.0 / var_ref[chunk, 0, rows, :]
+        rows = pl.ds(pl.multiple_of(v * 8, 8), 8)
+        curve = curve_ref[rows, :]
+        mean = mean_ref[rows, :]
+        inverse = 1.0 / var_ref[rows, :]
         for j in range(FINE):
             angle = curve * ((2 * j + 1) / 16384.0)
             up, down = jnp.exp(angle), jnp.exp(-angle)
@@ -67,35 +72,30 @@
                     up, down = up * up2, down * down2
             return lam + (mean - (0.5 + moment / partition)) * inverse
 
-        lam_ref[chunk, rows, :] = lax.fori_loop(0, ITERS, newton, slope_ref[chunk, 0, rows, :])
+        lam_ref[rows, :] = lax.fori_loop(0, ITERS, newton, slope_ref[rows, :])
         return 0
 
-    lax.fori_loop(0, CHUNKS * per_chunk, body, 0)
+    lax.fori_loop(0, lam_ref.shape[0] // 8, body, 0)
 
 
 def newton(x, slope, curve, mean, var):
-    rows = slope.shape[2]
-    mine = pl.BlockSpec((CHUNKS, 1, rows, LANES), lambda g, x: (0, x[0], 0, 0))
+    rows = slope.shape[1]
+    part = jax.ShapeDtypeStruct((rows, LANES), jnp.float32)
     return pl.pallas_call(
         newton_kernel,
-        out_shape=jax.ShapeDtypeStruct((CHUNKS, rows, LANES), jnp.float32),
-        grid_spec=pltpu.PrefetchScalarGridSpec(
-            num_scalar_prefetch=1,
-            grid=(1,),
-            in_specs=[mine] * 4,
-            out_specs=pl.BlockSpec(memory_space=pltpu.VMEM),
-            scratch_shapes=[
-                pltpu.VMEM((COARSE * FINE, 8, LANES), jnp.float32),
-                pltpu.VMEM((COARSE * FINE, 8, LANES), jnp.float32),
-                pltpu.VMEM((COARSE + FINE, 8, LANES), jnp.float32),
-            ],
-        ),
+        out_shape=[part, part],
+        in_specs=[pl.BlockSpec(memory_space=pltpu.SMEM)] + [pl.BlockSpec(memory_space=pltpu.HBM)] * 4,
+        out_specs=[pl.BlockSpec(memory_space=pltpu.VMEM)] * 2,
+        scratch_shapes=[pltpu.VMEM((rows, LANES), jnp.float32)] * 3
+        + [pltpu.VMEM((COARSE * FINE, 8, LANES), jnp.float32)] * 2
+        + [pltpu.VMEM((COARSE + FINE, 8, LANES), jnp.float32), pltpu.SemaphoreType.DMA((4,))],
         cost_estimate=pl.CostEstimate(flops=12 * 10**9, bytes_accessed=1 << 18, transcendentals=0),
+        compiler_params=pltpu.CompilerParams(vmem_limit_bytes=8 << 20),
         name="newton",
     )(x, slope, curve, mean, var)
 
 
-def species_kernel(x_ref, lam_ref, curve_ref, table_ref, sent_ref, turned_ref, out_ref, sems):
+def species_kernel(lam_ref, curve_ref, table_ref, sent_ref, turned_ref):
     turned_ref[...] = jnp.transpose(table_ref[...])
     table = jnp.concatenate([turned_ref[pl.ds(p, 8, stride=16), :] for p in range(16)], axis=1)
     high = table.astype(jnp.bfloat16).astype(jnp.float32)
@@ -104,8 +104,8 @@
     sub = lax.broadcasted_iota(jnp.int32, (8, LANES), 0).astype(jnp.float32)
 
     def tile(row):
-        lam = jnp.broadcast_to(lam_ref[0, pl.ds(row, 1), :], (8, LANES))
-        curve = jnp.broadcast_to(curve_ref[0, 0, pl.ds(row, 1), :], (8, LANES))
+        lam = jnp.broadcast_to(lam_ref[pl.ds(row, 1), :], (8, LANES))
+        curve = jnp.broadcast_to(curve_ref[pl.ds(row, 1), :], (8, LANES))
         mu = lam + curve
         ratio2 = jnp.exp(curve * (2.0 / (512.0 * 512.0)))
         columns = []
@@ -135,44 +135,50 @@
         values = pair(4 * t) + pair(4 * t + 2)
         rows = pl.ds(pl.multiple_of(8 * t, 8), 8)
         for x in range(4):
-            out_ref[x, rows, :] = jnp.concatenate([v[2 * x : 2 * x + 2] for v in values], axis=0)
+            block = jnp.concatenate([v[2 * x : 2 * x + 2] for v in values], axis=0)
+            for y in range(4):
+                sent_ref[x, y, rows, :] = block
         return 0
 
-    rows = lam_ref.shape[1]
+    rows = lam_ref.shape[0]
     for x in range(4):
-        out_ref[x, 2 * rows :, :] = lam_ref[0]
-    lax.fori_loop(0, rows // 4, body, 0)
-    copies = [pltpu.make_async_copy(out_ref, sent_ref.at[:, y], sems.at[y]) for y in range(4)]
-    for copy in copies:
-        copy.start()
-    for copy in copies:
-        copy.wait()
-
-
-def species(x, lam, curve, table):
-    rows = lam.shape[1]
+        for y in range(4):
+            sent_ref[x, y, 2 * rows :, :] = lam_ref[...]
+    lax.fori_loop(0, rows // 4, body, 0, unroll=4)
+
+
+def species(lam, curve, table):
+    rows = lam.shape[0]
     return pl.pallas_call(
         species_kernel,
         out_shape=jax.ShapeDtypeStruct((4, 4, 3 * rows, LANES), jnp.float32),
-        grid_spec=pltpu.PrefetchScalarGridSpec(
-            num_scalar_prefetch=1,
-            grid=(1,),
-            in_specs=[
-                pl.BlockSpec(memory_space=pltpu.VMEM),
-                pl.BlockSpec((1, 1, rows, LANES), lambda g, x: (0, x[0], 0, 0)),
-                pl.BlockSpec(memory_space=pltpu.VMEM),
-            ],
-            out_specs=pl.BlockSpec(memory_space=pl.ANY),
-            scratch_shapes=[
-                pltpu.VMEM((LANES, 32), jnp.float32),
-                pltpu.VMEM((4, 3 * rows, LANES), jnp.float32),
-                pltpu.SemaphoreType.DMA((4,)),
-            ],
-        ),
+        in_specs=[pl.BlockSpec(memory_space=pltpu.VMEM)] * 3,
+        out_specs=pl.BlockSpec(memory_space=pltpu.VMEM),
+        scratch_shapes=[pltpu.VMEM((LANES, 32), jnp.float32)],
         cost_estimate=pl.CostEstimate(flops=6 * 10**9, bytes_accessed=1 << 19, transcendentals=0),
         compiler_params=pltpu.CompilerParams(vmem_limit_bytes=16 << 20),
         name="species",
-    )(x, lam, curve, table)
+    )(lam, curve, table)
+
+
+def blocks_kernel(table_ref, out_ref, turned_ref):
+    points = table_ref.shape[0]
+    turned_ref[:, :points] = jnp.transpose(table_ref[...])
+    block = [turned_ref[pl.ds(q, 8, stride=8), :points] for q in range(8)]
+    block = jnp.concatenate(block, axis=1)
+    out_ref[...] = jnp.broadcast_to(block[:, None, :], out_ref.shape)
+
+
+def blocks(table):
+    return pl.pallas_call(
+        blocks_kernel,
+        out_shape=jax.ShapeDtypeStruct((8, 4, LANES), jnp.float32),
+        in_specs=[pl.BlockSpec(memory_space=pltpu.VMEM)],
+        out_specs=pl.BlockSpec(memory_space=pltpu.VMEM),
+        scratch_shapes=[pltpu.VMEM((64, LANES), jnp.float32)],
+        compiler_params=pltpu.CompilerParams(vmem_limit_bytes=4 << 20),
+        name="blocks",
+    )(table)
 
 
 def lay_kernel(flip, core_ref, blocks_ref, *refs):
@@ -217,14 +223,13 @@
 def per_device(slope, curvature, target_mean, target_var, table):
     x = jnp.reshape(lax.axis_index("x"), (1,)).astype(jnp.int32)
     core = jnp.reshape(lax.axis_index("core"), (1,)).astype(jnp.int32)
-    sent = jnp.broadcast_to(table.reshape(8, 1, 8 * 16), (8, 4, 8 * 16)).reshape(32, 8 * 16)
-    points = exchange(sent, ("z", "x"))
+    points = exchange(blocks(table.T).reshape(32, LANES), ("z", "x"))
 
     bins = slope.shape[0]
     rows = bins // (4 * LANES)
-    args = [a.reshape(1, 4, rows, LANES) for a in (slope, curvature, target_mean, target_var)]
-    lam = newton(x, *args)
-    sent = species(x, lam, args[1], points)
+    args = [a.reshape(4, rows, LANES) for a in (slope, curvature, target_mean, target_var)]
+    lam, curve = newton(x, *args)
+    sent = species(lam, curve, points)
     own = exchange(sent.reshape(16, *sent.shape[2:]), ("x", "y")).reshape(sent.shape)
     other = lax.ppermute(own, "core", [(0, 1), (1, 0)])
     values, final_slope = lay(core, other, 1, lay(core, own, 0))

time: 63.8 us -> 63.1 us (0.989)
  Pallas kernels: 16.7 us -> 13.9 us
  local copies, waits for them, and re-layouts: 2.24 us -> 4.3 us
  waiting for transfers between devices: 3.12 us -> 1.84 us
  blocking collectives: 25.8 us -> 26.7 us
    unnamed x5 -> x10, local copies, waits for them, and re-layouts: 1.54 us -> 4.3 us
    pallas_call x1, Pallas kernels: 7.12 us -> 4.8 us  [species(): pl.pallas_call(species_kernel, out_shape=jax.ShapeDtypeStruct((4, 4, 3 *...]
    all_to_all x1, waiting for transfers between devices: 1.28 us -> 0.01 us  [exchange(): return lax.all_to_all(array, axes, split_axis=0, concat_axis=0, tiled=True)]
    all_to_all x1, blocking collectives: 25.8 us -> 26.7 us  [exchange(): return lax.all_to_all(array, axes, split_axis=0, concat_axis=0, tiled=True)]
    broadcast_in_dim x2 -> x0, local copies, waits for them, and re-layouts: 0.69 us -> none  [per_device(): jnp.broadcast_to(table.reshape(8, 1, 8 * 16), (8, 4, 8 * 16))]
    pallas_call x1 -> x2, Pallas kernels: 7.21 us -> 6.69 us  [the longest x1 5.91 us: newton(): pl.pallas_call(newton_kernel, out_shape=[part, part], in_specs=[pl.BlockS...]
  transfers between devices with their start and end apart: 2 -> 2, of which waited for: 2 -> 1; matrix products, arithmetic and copies ran while one was open for 0% -> 0% of each run, Pallas kernels for 13% -> 11%
where the time goes in v5:
time: 63.1 us; the launch traced here: 62.8 us
  blocking collectives  26.7 us (42%)
  starting transfers between devices  15.4 us (24%)
  Pallas kernels  13.9 us (22%)
  local copies, waits for them, and re-layouts  4.3 us (7%)
  waiting for transfers between devices  1.84 us (3%)
  between operations  0.7 us (1%)
    all_to_all x1, blocking collectives, exchange(): return lax.all_to_all(array, axes, split_axis=0, concat_axis=0, tiled=True)  26.7 us
    all_to_all x1, starting transfers between devices, exchange(): return lax.all_to_all(array, axes, split_axis=0, concat_axis=0, tiled=True)  11.9 us
    pallas_call x1, Pallas kernels, newton(): pl.pallas_call(newton_kernel, out_shape=[part, part], in_specs=[pl.BlockS...  5.91 us
    pallas_call x1, Pallas kernels, species(): pl.pallas_call(species_kernel, out_shape=jax.ShapeDtypeStruct((4, 4, 3 *...  4.8 us
    unnamed x10, local copies, waits for them, and re-layouts  4.3 us
    ppermute x1, starting transfers between devices, per_device(): other = lax.ppermute(own, 'core', [(0, 1), (1, 0)])  3.53 us
    pallas_call x2, Pallas kernels, lay(): pl.pallas_call(functools.partial(lay_kernel, flip), out_shape=[jax.ShapeD...  2.39 us
    ppermute x1, waiting for transfers between devices, per_device(): other = lax.ppermute(own, 'core', [(0, 1), (1, 0)])  1.83 us
  transfers between devices with their start and end apart: 2, of which 1 were waited for; matrix products, arithmetic and copies ran while one was open for 0% of the time, Pallas kernels for 11%

profile of v5, /device:TPU:1, one launch (start us, length us, event | category | flops | bytes accessed | tf_op | source)
XLA Modules:
  0.0 62.8 jit_solution(11456786948572858349)
XLA Ops:
  0.6 0.0 copy-start
  0.6 0.7 %copy-done = f32[64,16]{0,1:T(8,128)S(1)} copy-done((f32[64,16]{0,1:T(8,128)S(1)}, f32[64,16]{0,1:T(8,128)}, u32[]{:S(2)}) %copy-start) | copy-done | bytes 4120
  1.3 0.8 %blocks.1 = f32[8,4,128]{2,1,0:T(4,128)} custom-call(f32[16,64]{1,0:T(8,128)S(1)} %bitcast.23), custom_call_target="tpu_custom_call" | custom-call | tf_op jit(solution)/shard_map/blocks/pallas_call | solution.py:173
  2.1 11.9 %all-to-all-start = ((f32[32,1,128]{2,1,0:T(1,128)}), f32[32,1,128]{2,1,0:T(1,128)S(1)}, u32[]{:S(2)}, u32[]{:S(2)}) async-start(f32[32,1,128]{2,1,0:T(1,128)} %bitcast.8), calls=%async_computation | async-start | bytes 32768 | tf_op jit(solution)/shard_map/all_to_all | solution.py:220
  14.0 0.0 copy-start.1
  14.0 0.9 %copy-done.1 = f32[32768]{0:T(1024)S(1)} copy-done((f32[32768]{0:T(1024)S(1)}, f32[32768]{0:T(1024)}, u32[]{:S(2)}) %copy-start.1) | copy-done | bytes 131096
  14.9 0.0 copy-start.2
  14.9 0.9 %copy-done.2 = f32[32768]{0:T(1024)S(1)} copy-done((f32[32768]{0:T(1024)S(1)}, f32[32768]{0:T(1024)}, u32[]{:S(2)}) %copy-start.2) | copy-done | bytes 131096
  15.8 0.0 copy-start.3
  15.8 0.9 %copy-done.3 = f32[32768]{0:T(1024)S(1)} copy-done((f32[32768]{0:T(1024)S(1)}, f32[32768]{0:T(1024)}, u32[]{:S(2)}) %copy-start.3) | copy-done | bytes 131096
  16.7 0.0 copy-start.4
  16.7 0.9 %copy-done.4 = f32[32768]{0:T(1024)S(1)} copy-done((f32[32768]{0:T(1024)S(1)}, f32[32768]{0:T(1024)}, u32[]{:S(2)}) %copy-start.4) | copy-done | bytes 131096
  17.6 5.9 %newton.1 = (f32[64,128]{1,0:T(8,128)S(1)}, f32[64,128]{1,0:T(8,128)S(1)}) custom-call(s32[1]{0:T(128)} %bitcast.1.x_ref, f32[4,64,128]{2,1,0:T(8,128)S(1)} %bitcast.24, f32[4,64,128]{2,1,0:T(8,128)S(1)} %bitcast.25, f32[4,64,128]{2,1,0:T(8,128)S(1)} %bitcast.26, f32[4,64,128]{2,1,0:T(8,128)S(1)} %bitcast.27), custom_call_target="tpu_custom_call" | custom-call | flops 12000000000 | bytes 262144 | tf_op jit(solution)/shard_map/newton/pallas_call | solution.py:84
  23.5 0.0 all-to-all-done
  23.5 4.8 %species.1 = f32[4,4,192,128]{3,2,1,0:T(8,128)S(1)} custom-call(f32[64,128]{1,0:T(8,128)S(1)} %get-tuple-element.8.lam_ref, f32[64,128]{1,0:T(8,128)S(1)} %get-tuple-element.9.curve_ref, f32[32,128]{1,0:T(8,128)S(1)} %bitcast.22), custom_call_target="tpu_custom_call" | custom-call | flops 6000000000 | bytes 524288 | tf_op jit(solution)/shard_map/species/pallas_call | solution.py:152
  28.3 26.7 %all_to_all.16 = f32[16,192,128]{2,1,0:T(8,128)S(1)} all-to-all(f32[16,192,128]{2,1,0:T(8,128)S(1)} %bitcast.21), channel_id=1, replica_groups=mesh['z'=8,'x'=4,'y'=4,'core'=2] {'x','y'}, dimensions={0} | all-to-all | bytes 3145728 | tf_op jit(solution)/shard_map/all_to_all | solution.py:220
  55.0 3.5 %collective-permute-start = (f32[4,4,192,128]{3,2,1,0:T(8,128)S(1)}, f32[4,4,192,128]{3,2,1,0:T(8,128)S(1)}, u32[]{:S(2)}, u32[]{:S(2)}) collective-permute-start(f32[4,4,192,128]{3,2,1,0:T(8,128)S(1)} %bitcast.19), channel_id=1, source_target_pairs={{0,1},{1,0},{2,3},{3,2},{4,5},{5,4},{6,7},{7,6},{8,9},{9,8},{10,11... | collective-permute-start | bytes 4718600 | tf_op jit(solution)/shard_map/ppermute | solution.py:234
  58.6 1.2 %lay.2 = (f32[4,2,4,128,128]{4,3,2,1,0:T(8,128)}, f32[4,2,4,64,128]{4,3,2,1,0:T(8,128)}) custom-call(s32[1]{0:T(128)} %bitcast.core_ref, f32[4,4,192,128]{3,2,1,0:T(8,128)S(1)} %bitcast.20), custom_call_target="tpu_custom_call" | custom-call | flops 2000000000 | bytes 3145728 | tf_op jit(solution)/shard_map/lay/pallas_call | solution.py:202
  59.8 1.8 %collective-permute-done.blocks_ref = f32[4,4,192,128]{3,2,1,0:T(8,128)S(1)} collective-permute-done((f32[4,4,192,128]{3,2,1,0:T(8,128)S(1)}, f32[4,4,192,128]{3,2,1,0:T(8,128)S(1)}, u32[]{:S(2)}, u32[]{:S(2)}) %collective-permute-start) | collective-permute-done | bytes 1572896 | tf_op jit(solution)/shard_map/ppermute | solution.py:234
  61.6 1.2 %lay.3 = (f32[4,2,4,128,128]{4,3,2,1,0:T(8,128)}, f32[4,2,4,64,128]{4,3,2,1,0:T(8,128)}) custom-call(s32[1]{0:T(128)} %bitcast.core_ref, f32[4,4,192,128]{3,2,1,0:T(8,128)S(1)} %collective-permute-done.blocks_ref, f32[4,2,4,128,128]{4,3,2,1,0:T(8,128)} %get-tuple-element.10.refs_0_, ...), custom_call_target="tpu_custom_call", output_to_operand_aliasing={{0}: (2, {}), {1}: (3, {})} | custom-call | flops 2000000000 | bytes 3145728 | tf_op jit(solution)/shard_map/lay/pallas_call | solution.py:202
Async XLA Ops:
  0.6 0.7 %copy-start = (f32[64,16]{0,1:T(8,128)S(1)}, f32[64,16]{0,1:T(8,128)}, u32[]{:S(2)}) copy-start(f32[64,16]{0,1:T(8,128)} %param.9) | copy-start | bytes 12292
  2.1 21.4 %all-to-all-start = ((f32[32,1,128]{2,1,0:T(1,128)}), f32[32,1,128]{2,1,0:T(1,128)S(1)}, u32[]{:S(2)}, u32[]{:S(2)}) async-start(f32[32,1,128]{2,1,0:T(1,128)} %bitcast.8), calls=%async_computation | async-start | bytes 32768 | tf_op jit(solution)/shard_map/all_to_all | solution.py:220
  14.0 0.9 %copy-start.1 = (f32[32768]{0:T(1024)S(1)}, f32[32768]{0:T(1024)}, u32[]{:S(2)}) copy-start(f32[32768]{0:T(1024)} %param.5) | copy-start | bytes 393220
  14.9 0.9 %copy-start.2 = (f32[32768]{0:T(1024)S(1)}, f32[32768]{0:T(1024)}, u32[]{:S(2)}) copy-start(f32[32768]{0:T(1024)} %param.6) | copy-start | bytes 393220
  15.8 0.9 %copy-start.3 = (f32[32768]{0:T(1024)S(1)}, f32[32768]{0:T(1024)}, u32[]{:S(2)}) copy-start(f32[32768]{0:T(1024)} %param.7) | copy-start | bytes 393220
  16.7 0.9 %copy-start.4 = (f32[32768]{0:T(1024)S(1)}, f32[32768]{0:T(1024)}, u32[]{:S(2)}) copy-start(f32[32768]{0:T(1024)} %param.8) | copy-start | bytes 393220
  55.0 6.6 %collective-permute-start = (f32[4,4,192,128]{3,2,1,0:T(8,128)S(1)}, f32[4,4,192,128]{3,2,1,0:T(8,128)S(1)}, u32[]{:S(2)}, u32[]{:S(2)}) collective-permute-start(f32[4,4,192,128]{3,2,1,0:T(8,128)S(1)} %bitcast.19), channel_id=1, source_target_pairs={{0,1},{1,0},{2,3},{3,2},{4,5},{5,4},{6,7},{7,6},{8,9},{9,8},{10,11... | collective-permute-start | bytes 4718600 | tf_op jit(solution)/shard_map/ppermute | solution.py:234

commit v6 on v5

--- a/solution.py
+++ b/solution.py
@@ -14,16 +14,7 @@
 FINE = 16
 
 
-def newton_kernel(x_ref, *refs):
-    whole, (lam_ref, curve_ref, slope_ref, mean_ref, var_ref) = refs[:4], refs[4:9]
-    ch_ref, sh_ref, g_ref, sems = refs[9:]
-    mine = zip(whole, (slope_ref, curve_ref, mean_ref, var_ref))
-    copies = [pltpu.make_async_copy(a.at[x_ref[0]], b, sems.at[i]) for i, (a, b) in enumerate(mine)]
-    for copy in copies:
-        copy.start()
-    for copy in copies:
-        copy.wait()
-
+def newton_kernel(slope_ref, curve_ref, mean_ref, var_ref, lam_ref, ch_ref, sh_ref, g_ref):
     def body(v, _):
         rows = pl.ds(pl.multiple_of(v * 8, 8), 8)
         curve = curve_ref[rows, :]
@@ -78,21 +69,18 @@
     lax.fori_loop(0, lam_ref.shape[0] // 8, body, 0)
 
 
-def newton(x, slope, curve, mean, var):
-    rows = slope.shape[1]
-    part = jax.ShapeDtypeStruct((rows, LANES), jnp.float32)
+def newton(slope, curve, mean, var):
     return pl.pallas_call(
         newton_kernel,
-        out_shape=[part, part],
-        in_specs=[pl.BlockSpec(memory_space=pltpu.SMEM)] + [pl.BlockSpec(memory_space=pltpu.HBM)] * 4,
-        out_specs=[pl.BlockSpec(memory_space=pltpu.VMEM)] * 2,
-        scratch_shapes=[pltpu.VMEM((rows, LANES), jnp.float32)] * 3
-        + [pltpu.VMEM((COARSE * FINE, 8, LANES), jnp.float32)] * 2
-        + [pltpu.VMEM((COARSE + FINE, 8, LANES), jnp.float32), pltpu.SemaphoreType.DMA((4,))],
+        out_shape=jax.ShapeDtypeStruct(slope.shape, jnp.float32),
+        in_specs=[pl.BlockSpec(memory_space=pltpu.VMEM)] * 4,
+        out_specs=pl.BlockSpec(memory_space=pltpu.VMEM),
+        scratch_shapes=[pltpu.VMEM((COARSE * FINE, 8, LANES), jnp.float32)] * 2
+        + [pltpu.VMEM((COARSE + FINE, 8, LANES), jnp.float32)],
         cost_estimate=pl.CostEstimate(flops=12 * 10**9, bytes_accessed=1 << 18, transcendentals=0),
         compiler_params=pltpu.CompilerParams(vmem_limit_bytes=8 << 20),
         name="newton",
-    )(x, slope, curve, mean, var)
+    )(slope, curve, mean, var)
 
 
 def species_kernel(lam_ref, curve_ref, table_ref, sent_ref, turned_ref):
@@ -221,15 +209,17 @@
 
 
 def per_device(slope, curvature, target_mean, target_var, table):
-    x = jnp.reshape(lax.axis_index("x"), (1,)).astype(jnp.int32)
+    x = lax.axis_index("x")
     core = jnp.reshape(lax.axis_index("core"), (1,)).astype(jnp.int32)
     points = exchange(blocks(table.T).reshape(32, LANES), ("z", "x"))
 
-    bins = slope.shape[0]
-    rows = bins // (4 * LANES)
-    args = [a.reshape(4, rows, LANES) for a in (slope, curvature, target_mean, target_var)]
-    lam, curve = newton(x, *args)
-    sent = species(lam, curve, points)
+    size = slope.shape[0] // 4
+    mine = [
+        lax.dynamic_slice_in_dim(a, x * size, size, 0).reshape(-1, LANES)
+        for a in (slope, curvature, target_mean, target_var)
+    ]
+    lam = newton(*mine)
+    sent = species(lam, mine[1], points)
     own = exchange(sent.reshape(16, *sent.shape[2:]), ("x", "y")).reshape(sent.shape)
     other = lax.ppermute(own, "core", [(0, 1), (1, 0)])
     values, final_slope = lay(core, other, 1, lay(core, own, 0))

time: 63.1 us -> 60.9 us (0.965)
  local copies, waits for them, and re-layouts: 4.3 us -> 2.25 us
  waiting for transfers between devices: 1.84 us -> 3.03 us
  blocking collectives: 26.7 us -> 25.8 us
    unnamed x10 -> x2, local copies, waits for them, and re-layouts: 4.3 us -> 0.69 us
    reshape x0 -> x2, local copies, waits for them, and re-layouts: none -> 1.56 us  [per_device(): lax.dynamic_slice_in_dim(a, x * size, size, 0).reshape(-1, LANES)]
    all_to_all x1, waiting for transfers between devices: 0.01 us -> 1.2 us  [exchange(): return lax.all_to_all(array, axes, split_axis=0, concat_axis=0, tiled=True)]
    all_to_all x1, blocking collectives: 26.7 us -> 25.8 us  [exchange(): return lax.all_to_all(array, axes, split_axis=0, concat_axis=0, tiled=True)]
  transfers between devices with their start and end apart: 2 -> 2, of which waited for: 1 -> 2; matrix products, arithmetic and copies ran while one was open for 0% -> 3% of each run, Pallas kernels for 11% -> 11%
where the time goes in v6:
time: 60.9 us; the launch traced here: 60.6 us
  blocking collectives  25.8 us (42%)
  starting transfers between devices  15.1 us (25%)
  Pallas kernels  13.7 us (22%)
  waiting for transfers between devices  3.03 us (5%)
  local copies, waits for them, and re-layouts  2.25 us (4%)
  between operations  0.68 us (1%)
    all_to_all x1, blocking collectives, exchange(): return lax.all_to_all(array, axes, split_axis=0, concat_axis=0, tiled=True)  25.8 us
    all_to_all x1, starting transfers between devices, exchange(): return lax.all_to_all(array, axes, split_axis=0, concat_axis=0, tiled=True)  11.9 us
    pallas_call x1, Pallas kernels, newton(): pl.pallas_call(newton_kernel, out_shape=jax.ShapeDtypeStruct(slope.shape,...  5.73 us
    pallas_call x1, Pallas kernels, species(): pl.pallas_call(species_kernel, out_shape=jax.ShapeDtypeStruct((4, 4, 3 *...  4.79 us
    ppermute x1, starting transfers between devices, per_device(): other = lax.ppermute(own, 'core', [(0, 1), (1, 0)])  3.26 us
    pallas_call x2, Pallas kernels, lay(): pl.pallas_call(functools.partial(lay_kernel, flip), out_shape=[jax.ShapeD...  2.39 us
    ppermute x1, waiting for transfers between devices, per_device(): other = lax.ppermute(own, 'core', [(0, 1), (1, 0)])  1.83 us
    reshape x2, local copies, waits for them, and re-layouts, per_device(): lax.dynamic_slice_in_dim(a, x * size, size, 0).reshape(-1, LANES)  1.56 us
  transfers between devices with their start and end apart: 2, of which 2 were waited for; matrix products, arithmetic and copies ran while one was open for 3% of the time, Pallas kernels for 11%

profile of v6, /device:TPU:1, one launch (start us, length us, event | category | flops | bytes accessed | tf_op | source)
XLA Modules:
  0.0 60.6 jit_solution(11538476986927668909)
XLA Ops:
  0.6 0.0 copy-start
  0.6 0.7 %copy-done = f32[64,16]{0,1:T(8,128)S(1)} copy-done((f32[64,16]{0,1:T(8,128)S(1)}, f32[64,16]{0,1:T(8,128)}, u32[]{:S(2)}) %copy-start) | copy-done | bytes 4120
  1.3 0.8 %blocks.1 = f32[8,4,128]{2,1,0:T(4,128)} custom-call(f32[16,64]{1,0:T(8,128)S(1)} %bitcast.26), custom_call_target="tpu_custom_call" | custom-call | tf_op jit(solution)/shard_map/blocks/pallas_call | solution.py:161
  2.1 11.9 %all-to-all-start = ((f32[32,1,128]{2,1,0:T(1,128)}), f32[32,1,128]{2,1,0:T(1,128)S(1)}, u32[]{:S(2)}, u32[]{:S(2)}) async-start(f32[32,1,128]{2,1,0:T(1,128)} %bitcast.7), calls=%async_computation | async-start | bytes 32768 | tf_op jit(solution)/shard_map/all_to_all | solution.py:208
  14.0 0.8 %dynamic-slice_bitcast_fusion.2 = (f32[64,128]{1,0:T(8,128)S(1)}, f32[64,128]{1,0:T(8,128)S(1)}) fusion(f32[32768]{0:T(1024)} %param.6, s32[]{:T(128)S(6)} %select_n.2, f32[32768]{0:T(1024)} %param.5), kind=kLoop, calls=%fused_computation.2 | loop fusion | bytes 131076 | tf_op jit(solution)/shard_map/reshape | solution.py:218
  14.8 0.8 %dynamic-slice_bitcast_fusion = (f32[64,128]{1,0:T(8,128)S(1)}, f32[64,128]{1,0:T(8,128)S(1)}) fusion(f32[32768]{0:T(1024)} %param.8, s32[]{:T(128)S(6)} %select_n.2, f32[32768]{0:T(1024)} %param.7), kind=kLoop, calls=%fused_computation | loop fusion | bytes 131076 | tf_op jit(solution)/shard_map/reshape | solution.py:218
  15.6 5.7 %newton.1.lam_ref = f32[64,128]{1,0:T(8,128)S(1)} custom-call(f32[64,128]{1,0:T(8,128)S(1)} %get-tuple-element.13.slope_ref, f32[64,128]{1,0:T(8,128)S(1)} %get-tuple-element.12.curve_ref, f32[64,128]{1,0:T(8,128)S(1)} %get-tuple-element.11.mean_ref, f32[64,128]{1,0:T(8,128)S(1)} %get-tuple-element.10.var_ref), custom_call_target="tpu_custom_call" | custom-call | flops 12000000000 | bytes 262144 | tf_op jit(solution)/shard_map/newton/pallas_call | solution.py:73
  21.3 1.2 %all-to-all-done = f32[32,1,128]{2,1,0:T(1,128)S(1)} async-done(((f32[32,1,128]{2,1,0:T(1,128)}), f32[32,1,128]{2,1,0:T(1,128)S(1)}, u32[]{:S(2)}, u32[]{:S(2)}) %all-to-all-start) | async-done | bytes 16416 | tf_op jit(solution)/shard_map/all_to_all | solution.py:208
  22.5 4.8 %species.1 = f32[4,4,192,128]{3,2,1,0:T(8,128)S(1)} custom-call(f32[64,128]{1,0:T(8,128)S(1)} %newton.1.lam_ref, f32[64,128]{1,0:T(8,128)S(1)} %get-tuple-element.12.curve_ref, f32[32,128]{1,0:T(8,128)S(1)} %bitcast.25), custom_call_target="tpu_custom_call" | custom-call | flops 6000000000 | bytes 524288 | tf_op jit(solution)/shard_map/species/pallas_call | solution.py:140
  27.3 25.8 %all_to_all.16 = f32[16,192,128]{2,1,0:T(8,128)S(1)} all-to-all(f32[16,192,128]{2,1,0:T(8,128)S(1)} %bitcast.24), channel_id=1, replica_groups=mesh['z'=8,'x'=4,'y'=4,'core'=2] {'x','y'}, dimensions={0} | all-to-all | bytes 3145728 | tf_op jit(solution)/shard_map/all_to_all | solution.py:208
  53.1 3.3 %collective-permute-start = (f32[4,4,192,128]{3,2,1,0:T(8,128)S(1)}, f32[4,4,192,128]{3,2,1,0:T(8,128)S(1)}, u32[]{:S(2)}, u32[]{:S(2)}) collective-permute-start(f32[4,4,192,128]{3,2,1,0:T(8,128)S(1)} %bitcast.22), channel_id=1, source_target_pairs={{0,1},{1,0},{2,3},{3,2},{4,5},{5,4},{6,7},{7,6},{8,9},{9,8},{10,11... | collective-permute-start | bytes 4718600 | tf_op jit(solution)/shard_map/ppermute | solution.py:224
  56.3 1.2 %lay.2 = (f32[4,2,4,128,128]{4,3,2,1,0:T(8,128)}, f32[4,2,4,64,128]{4,3,2,1,0:T(8,128)}) custom-call(s32[1]{0:T(128)} %bitcast.core_ref, f32[4,4,192,128]{3,2,1,0:T(8,128)S(1)} %bitcast.23), custom_call_target="tpu_custom_call" | custom-call | flops 2000000000 | bytes 3145728 | tf_op jit(solution)/shard_map/lay/pallas_call | solution.py:190
  57.5 1.8 %collective-permute-done.blocks_ref = f32[4,4,192,128]{3,2,1,0:T(8,128)S(1)} collective-permute-done((f32[4,4,192,128]{3,2,1,0:T(8,128)S(1)}, f32[4,4,192,128]{3,2,1,0:T(8,128)S(1)}, u32[]{:S(2)}, u32[]{:S(2)}) %collective-permute-start) | collective-permute-done | bytes 1572896 | tf_op jit(solution)/shard_map/ppermute | solution.py:224
  59.4 1.2 %lay.3 = (f32[4,2,4,128,128]{4,3,2,1,0:T(8,128)}, f32[4,2,4,64,128]{4,3,2,1,0:T(8,128)}) custom-call(s32[1]{0:T(128)} %bitcast.core_ref, f32[4,4,192,128]{3,2,1,0:T(8,128)S(1)} %collective-permute-done.blocks_ref, f32[4,2,4,128,128]{4,3,2,1,0:T(8,128)} %get-tuple-element.6.refs_0_, ...), custom_call_target="tpu_custom_call", output_to_operand_aliasing={{0}: (2, {}), {1}: (3, {})} | custom-call | flops 2000000000 | bytes 3145728 | tf_op jit(solution)/shard_map/lay/pallas_call | solution.py:190
Async XLA Ops:
  0.6 0.7 %copy-start = (f32[64,16]{0,1:T(8,128)S(1)}, f32[64,16]{0,1:T(8,128)}, u32[]{:S(2)}) copy-start(f32[64,16]{0,1:T(8,128)} %param.9) | copy-start | bytes 12292
  2.1 20.4 %all-to-all-start = ((f32[32,1,128]{2,1,0:T(1,128)}), f32[32,1,128]{2,1,0:T(1,128)S(1)}, u32[]{:S(2)}, u32[]{:S(2)}) async-start(f32[32,1,128]{2,1,0:T(1,128)} %bitcast.7), calls=%async_computation | async-start | bytes 32768 | tf_op jit(solution)/shard_map/all_to_all | solution.py:208
  53.1 6.3 %collective-permute-start = (f32[4,4,192,128]{3,2,1,0:T(8,128)S(1)}, f32[4,4,192,128]{3,2,1,0:T(8,128)S(1)}, u32[]{:S(2)}, u32[]{:S(2)}) collective-permute-start(f32[4,4,192,128]{3,2,1,0:T(8,128)S(1)} %bitcast.22), channel_id=1, source_target_pairs={{0,1},{1,0},{2,3},{3,2},{4,5},{5,4},{6,7},{7,6},{8,9},{9,8},{10,11... | collective-permute-start | bytes 4718600 | tf_op jit(solution)/shard_map/ppermute | solution.py:224

commit v7 on v6

--- a/solution.py
+++ b/solution.py
@@ -10,11 +10,41 @@
 
 ITERS = 3
 LANES = 128
+EARLY = 6
 COARSE = 8
 FINE = 16
 
 
-def newton_kernel(slope_ref, curve_ref, mean_ref, var_ref, lam_ref, ch_ref, sh_ref, g_ref):
+def weights(lam_ref, curve_ref, t):
+    sub = lax.broadcasted_iota(jnp.int32, (8, LANES), 0).astype(jnp.float32)
+
+    def tile(row):
+        lam = jnp.broadcast_to(lam_ref[pl.ds(row, 1), :], (8, LANES))
+        curve = jnp.broadcast_to(curve_ref[pl.ds(row, 1), :], (8, LANES))
+        mu = lam + curve
+        ratio2 = jnp.exp(curve * (2.0 / (512.0 * 512.0)))
+        columns = []
+        for g in range(4):
+            s = ((sub + 8.0 * g) * 16.0 + 0.5) * (1 / 512.0) - 0.5
+            e = jnp.exp(mu * s + curve * (s * s))
+            ratio = jnp.exp(mu * (1 / 512.0) + curve * ((2.0 * s + 1 / 512.0) * (1 / 512.0)))
+            column = []
+            for p in range(16):
+                column.append(e)
+                if p < 15:
+                    e = e * ratio
+                    ratio = ratio * ratio2
+            columns.append(column)
+        return jnp.concatenate([columns[g][p] for p in range(16) for g in range(4)], axis=0)
+
+    e = jnp.concatenate([tile(2 * t), tile(2 * t + 1)], axis=1)
+    high = e.astype(jnp.bfloat16)
+    return high, (e - high.astype(jnp.float32)).astype(jnp.bfloat16)
+
+
+def newton_kernel(
+    slope_ref, curve_ref, mean_ref, var_ref, lam_ref, high_ref, low_ref, ch_ref, sh_ref, g_ref
+):
     def body(v, _):
         rows = pl.ds(pl.multiple_of(v * 8, 8), 8)
         curve = curve_ref[rows, :]
@@ -68,85 +98,78 @@
 
     lax.fori_loop(0, lam_ref.shape[0] // 8, body, 0)
 
+    def early(t, _):
+        high_ref[t], low_ref[t] = weights(lam_ref, curve_ref, t)
+        return 0
+
+    lax.fori_loop(0, EARLY, early, 0, unroll=EARLY // 2)
+
 
 def newton(slope, curve, mean, var):
+    part = jax.ShapeDtypeStruct((EARLY, 512, 2 * LANES), jnp.bfloat16)
     return pl.pallas_call(
         newton_kernel,
-        out_shape=jax.ShapeDtypeStruct(slope.shape, jnp.float32),
+        out_shape=[jax.ShapeDtypeStruct(slope.shape, jnp.float32), part, part],
         in_specs=[pl.BlockSpec(memory_space=pltpu.VMEM)] * 4,
-        out_specs=pl.BlockSpec(memory_space=pltpu.VMEM),
+        out_specs=[pl.BlockSpec(memory_space=pltpu.VMEM)] * 3,
         scratch_shapes=[pltpu.VMEM((COARSE * FINE, 8, LANES), jnp.float32)] * 2
         + [pltpu.VMEM((COARSE + FINE, 8, LANES), jnp.float32)],
         cost_estimate=pl.CostEstimate(flops=12 * 10**9, bytes_accessed=1 << 18, transcendentals=0),
-        compiler_params=pltpu.CompilerParams(vmem_limit_bytes=8 << 20),
+        compiler_params=pltpu.CompilerParams(vmem_limit_bytes=12 << 20),
         name="newton",
     )(slope, curve, mean, var)
 
 
-def species_kernel(lam_ref, curve_ref, table_ref, sent_ref, turned_ref):
+def species_kernel(lam_ref, curve_ref, high_ref, low_ref, table_ref, sent_ref, turned_ref):
     turned_ref[...] = jnp.transpose(table_ref[...])
     table = jnp.concatenate([turned_ref[pl.ds(p, 8, stride=16), :] for p in range(16)], axis=1)
     high = table.astype(jnp.bfloat16).astype(jnp.float32)
     ones = jnp.ones((16, table.shape[1]), jnp.float32)
     left = jnp.concatenate([high, table - high, ones], axis=0).astype(jnp.bfloat16)
-    sub = lax.broadcasted_iota(jnp.int32, (8, LANES), 0).astype(jnp.float32)
-
-    def tile(row):
-        lam = jnp.broadcast_to(lam_ref[pl.ds(row, 1), :], (8, LANES))
-        curve = jnp.broadcast_to(curve_ref[pl.ds(row, 1), :], (8, LANES))
-        mu = lam + curve
-        ratio2 = jnp.exp(curve * (2.0 / (512.0 * 512.0)))
-        columns = []
-        for g in range(4):
-            s = ((sub + 8.0 * g) * 16.0 + 0.5) * (1 / 512.0) - 0.5
-            e = jnp.exp(mu * s + curve * (s * s))
-            ratio = jnp.exp(mu * (1 / 512.0) + curve * ((2.0 * s + 1 / 512.0) * (1 / 512.0)))
-            column = []
-            for p in range(16):
-                column.append(e)
-                if p < 15:
-                    e = e * ratio
-                    ratio = ratio * ratio2
-            columns.append(column)
-        return jnp.concatenate([columns[g][p] for p in range(16) for g in range(4)], axis=0)
-
-    def pair(row):
-        e = jnp.concatenate([tile(row), tile(row + 1)], axis=1)
-        e_high = e.astype(jnp.bfloat16)
-        e_low = (e - e_high.astype(jnp.float32)).astype(jnp.bfloat16)
-        sums = jnp.dot(left, e_high, preferred_element_type=jnp.float32)
-        sums = sums + jnp.dot(left, e_low, preferred_element_type=jnp.float32)
+    def pair(high, low):
+        sums = jnp.dot(left, high, preferred_element_type=jnp.float32)
+        sums = sums + jnp.dot(left, low, preferred_element_type=jnp.float32)
         values = (sums[0:8] + sums[8:16]) / sums[16:24]
         return [values[:, :LANES], values[:, LANES:]]
 
-    def body(t, _):
-        values = pair(4 * t) + pair(4 * t + 2)
+    def store(t, values):
         rows = pl.ds(pl.multiple_of(8 * t, 8), 8)
         for x in range(4):
             block = jnp.concatenate([v[2 * x : 2 * x + 2] for v in values], axis=0)
             for y in range(4):
                 sent_ref[x, y, rows, :] = block
+
+    def early(t, _):
+        store(t, [v for n in (2 * t, 2 * t + 1) for v in pair(high_ref[n], low_ref[n])])
+        return 0
+
+    def late(t, _):
+        pairs = (weights(lam_ref, curve_ref, 2 * t + n) for n in range(2))
+        store(t, [v for p in pairs for v in pair(*p)])
         return 0
 
     rows = lam_ref.shape[0]
     for x in range(4):
         for y in range(4):
             sent_ref[x, y, 2 * rows :, :] = lam_ref[...]
-    lax.fori_loop(0, rows // 4, body, 0, unroll=4)
-
-
-def species(lam, curve, table):
+    first = EARLY // 2
+    lax.fori_loop(0, first, early, 0, unroll=first)
+    late(first, 0)
+    lax.fori_loop(first + 1, rows // 4, late, 0, unroll=4)
+
+
+def species(lam, curve, early, table):
     rows = lam.shape[0]
     return pl.pallas_call(
         species_kernel,
         out_shape=jax.ShapeDtypeStruct((4, 4, 3 * rows, LANES), jnp.float32),
-        in_specs=[pl.BlockSpec(memory_space=pltpu.VMEM)] * 3,
+        in_specs=[pl.BlockSpec(memory_space=pltpu.VMEM)] * 5,
         out_specs=pl.BlockSpec(memory_space=pltpu.VMEM),
         scratch_shapes=[pltpu.VMEM((LANES, 32), jnp.float32)],
         cost_estimate=pl.CostEstimate(flops=6 * 10**9, bytes_accessed=1 << 19, transcendentals=0),
         compiler_params=pltpu.CompilerParams(vmem_limit_bytes=16 << 20),
         name="species",
-    )(lam, curve, table)
+    )(lam, curve, *early, table)
 
 
 def blocks_kernel(table_ref, out_ref, turned_ref):
@@ -164,7 +187,6 @@
         in_specs=[pl.BlockSpec(memory_space=pltpu.VMEM)],
         out_specs=pl.BlockSpec(memory_space=pltpu.VMEM),
         scratch_shapes=[pltpu.VMEM((64, LANES), jnp.float32)],
-        compiler_params=pltpu.CompilerParams(vmem_limit_bytes=4 << 20),
         name="blocks",
     )(table)
 
@@ -218,8 +240,8 @@
         lax.dynamic_slice_in_dim(a, x * size, size, 0).reshape(-1, LANES)
         for a in (slope, curvature, target_mean, target_var)
     ]
-    lam = newton(*mine)
-    sent = species(lam, mine[1], points)
+    lam, *early = newton(*mine)
+    sent = species(lam, mine[1], early, points)
     own = exchange(sent.reshape(16, *sent.shape[2:]), ("x", "y")).reshape(sent.shape)
     other = lax.ppermute(own, "core", [(0, 1), (1, 0)])
     values, final_slope = lay(core, other, 1, lay(core, own, 0))

time: 60.9 us -> 61.3 us (level)
  Pallas kernels: 13.7 us -> 14.8 us
  waiting for transfers between devices: 3.03 us -> 2.34 us
  local copies, waits for them, and re-layouts: 2.25 us -> 1.57 us
    pallas_call x1, Pallas kernels: 0.78 us -> 1.51 us  [blocks(): pl.pallas_call(blocks_kernel, out_shape=jax.ShapeDtypeStruct((8, 4, LANES...]
    all_to_all x1, waiting for transfers between devices: 1.2 us -> 0.51 us  [exchange(): return lax.all_to_all(array, axes, split_axis=0, concat_axis=0, tiled=True)]
    pallas_call x1, Pallas kernels: 5.73 us -> 6.41 us  [newton(): pl.pallas_call(newton_kernel, out_shape=[jax.ShapeDtypeStruct(slope.shape...]
    unnamed x2, local copies, waits for them, and re-layouts: 0.69 us -> 0.01 us
    reshape x2 -> x3, local copies, waits for them, and re-layouts: 1.56 us -> 1.56 us  [per_device(): lax.dynamic_slice_in_dim(a, x * size, size, 0).reshape(-1, LANES)]
  transfers between devices with their start and end apart: 2 -> 2, of which waited for: 2 -> 2; matrix products, arithmetic and copies ran while one was open for 3% -> 3% of each run, Pallas kernels for 11% -> 12%
where the time goes in v7:
time: 61.3 us; the launch traced here: 61 us
  blocking collectives  26.2 us (43%)
  starting transfers between devices  15.4 us (25%)
  Pallas kernels  14.8 us (24%)
  waiting for transfers between devices  2.34 us (4%)
  local copies, waits for them, and re-layouts  1.57 us (3%)
  between operations  0.7 us (1%)
    all_to_all x1, blocking collectives, exchange(): return lax.all_to_all(array, axes, split_axis=0, concat_axis=0, tiled=True)  26.2 us
    all_to_all x1, starting transfers between devices, exchange(): return lax.all_to_all(array, axes, split_axis=0, concat_axis=0, tiled=True)  11.9 us
    pallas_call x1, Pallas kernels, newton(): pl.pallas_call(newton_kernel, out_shape=[jax.ShapeDtypeStruct(slope.shape...  6.41 us
    pallas_call x1, Pallas kernels, species(): pl.pallas_call(species_kernel, out_shape=jax.ShapeDtypeStruct((4, 4, 3 *...  4.51 us
    ppermute x1, starting transfers between devices, per_device(): other = lax.ppermute(own, 'core', [(0, 1), (1, 0)])  3.53 us
    pallas_call x2, Pallas kernels, lay(): pl.pallas_call(functools.partial(lay_kernel, flip), out_shape=[jax.ShapeD...  2.39 us
    ppermute x1, waiting for transfers between devices, per_device(): other = lax.ppermute(own, 'core', [(0, 1), (1, 0)])  1.83 us
    reshape x3, local copies, waits for them, and re-layouts, per_device(): lax.dynamic_slice_in_dim(a, x * size, size, 0).reshape(-1, LANES)  1.56 us
  transfers between devices with their start and end apart: 2, of which 2 were waited for; matrix products, arithmetic and copies ran while one was open for 3% of the time, Pallas kernels for 12%

profile of v7, /device:TPU:1, one launch (start us, length us, event | category | flops | bytes accessed | tf_op | source)
XLA Modules:
  0.0 61.0 jit_solution(14161289110283399030)
XLA Ops:
  0.6 0.0 copy-start
  0.6 1.5 %blocks.1 = f32[8,4,128]{2,1,0:T(4,128)} custom-call(f32[16,64]{1,0:T(8,128)} %bitcast.27), custom_call_target="tpu_custom_call" | custom-call | tf_op jit(solution)/shard_map/blocks/pallas_call | solution.py:184
  2.2 11.9 %all-to-all-start = ((f32[32,1,128]{2,1,0:T(1,128)}), f32[32,1,128]{2,1,0:T(1,128)S(1)}, u32[]{:S(2)}, u32[]{:S(2)}) async-start(f32[32,1,128]{2,1,0:T(1,128)} %bitcast.26), calls=%async_computation | async-start | bytes 32768 | tf_op jit(solution)/shard_map/all_to_all | solution.py:230
  14.0 0.0 copy-done
  14.1 0.8 %dynamic-slice_bitcast_fusion.3.slope_ref = f32[64,128]{1,0:T(8,128)S(1)} fusion(f32[32768]{0:T(1024)} %param.5, s32[]{:T(128)S(6)} %select_n.2), kind=kLoop, calls=%fused_computation.3 | loop fusion | bytes 65540 | tf_op jit(solution)/shard_map/reshape | solution.py:240
  14.8 0.8 %dynamic-slice_bitcast_fusion = (f32[64,128]{1,0:T(8,128)S(1)}, f32[64,128]{1,0:T(8,128)S(1)}) fusion(f32[32768]{0:T(1024)} %param.8, s32[]{:T(128)S(6)} %select_n.2, f32[32768]{0:T(1024)} %param.7), kind=kLoop, calls=%fused_computation | loop fusion | bytes 131076 | tf_op jit(solution)/shard_map/reshape | solution.py:240
  15.6 6.4 %newton.1 = (f32[64,128]{1,0:T(8,128)S(1)}, bf16[6,512,256]{2,1,0:T(8,128)(2,1)S(1)}, bf16[6,512,256]{2,1,0:T(8,128)(2,1)S(1)}) custom-call(f32[64,128]{1,0:T(8,128)S(1)} %dynamic-slice_bitcast_fusion.3.slope_ref, f32[64,128]{1,0:T(8,128)S(1)} %dynamic-slice_bitcast_fusion.2.curve_ref, f32[64,128]{1,0:T(8,128)S(1)} %get-tuple-element.17.mean_ref, ...), custom_call_target="tpu_custom_call" | custom-call | flops 12000000000 | bytes 262144 | tf_op jit(solution)/shard_map/newton/pallas_call | solution.py:110
  22.0 0.5 all-to-all-done
  22.5 4.5 %species.1 = f32[4,4,192,128]{3,2,1,0:T(8,128)S(1)} custom-call(f32[64,128]{1,0:T(8,128)S(1)} %get-tuple-element.9.lam_ref, f32[64,128]{1,0:T(8,128)S(1)} %dynamic-slice_bitcast_fusion.2.curve_ref, bf16[6,512,256]{2,1,0:T(8,128)(2,1)S(1)} %get-tuple-element.10.high_ref, bf16[6,512,256]{2,1,0:T(8,128)(2,1)S(1)} %get-tuple-element.11.low_ref, ...), custom_call_target="tpu_custom_call" | custom-call | flops 6000000000 | bytes 524288 | tf_op jit(solution)/shard_map/species/pallas_call | solution.py:163
  27.1 26.2 %all_to_all.16 = f32[16,192,128]{2,1,0:T(8,128)S(1)} all-to-all(f32[16,192,128]{2,1,0:T(8,128)S(1)} %bitcast.24), channel_id=1, replica_groups=mesh['z'=8,'x'=4,'y'=4,'core'=2] {'x','y'}, dimensions={0} | all-to-all | bytes 3145728 | tf_op jit(solution)/shard_map/all_to_all | solution.py:230
  53.2 3.5 %collective-permute-start = (f32[4,4,192,128]{3,2,1,0:T(8,128)S(1)}, f32[4,4,192,128]{3,2,1,0:T(8,128)S(1)}, u32[]{:S(2)}, u32[]{:S(2)}) collective-permute-start(f32[4,4,192,128]{3,2,1,0:T(8,128)S(1)} %bitcast.22), channel_id=1, source_target_pairs={{0,1},{1,0},{2,3},{3,2},{4,5},{5,4},{6,7},{7,6},{8,9},{9,8},{10,11... | collective-permute-start | bytes 4718600 | tf_op jit(solution)/shard_map/ppermute | solution.py:246
  56.8 1.2 %lay.2 = (f32[4,2,4,128,128]{4,3,2,1,0:T(8,128)}, f32[4,2,4,64,128]{4,3,2,1,0:T(8,128)}) custom-call(s32[1]{0:T(128)} %bitcast.core_ref, f32[4,4,192,128]{3,2,1,0:T(8,128)S(1)} %bitcast.23), custom_call_target="tpu_custom_call" | custom-call | flops 2000000000 | bytes 3145728 | tf_op jit(solution)/shard_map/lay/pallas_call | solution.py:212
  58.0 1.8 %collective-permute-done.blocks_ref = f32[4,4,192,128]{3,2,1,0:T(8,128)S(1)} collective-permute-done((f32[4,4,192,128]{3,2,1,0:T(8,128)S(1)}, f32[4,4,192,128]{3,2,1,0:T(8,128)S(1)}, u32[]{:S(2)}, u32[]{:S(2)}) %collective-permute-start) | collective-permute-done | bytes 1572896 | tf_op jit(solution)/shard_map/ppermute | solution.py:246
  59.8 1.2 %lay.3 = (f32[4,2,4,128,128]{4,3,2,1,0:T(8,128)}, f32[4,2,4,64,128]{4,3,2,1,0:T(8,128)}) custom-call(s32[1]{0:T(128)} %bitcast.core_ref, f32[4,4,192,128]{3,2,1,0:T(8,128)S(1)} %collective-permute-done.blocks_ref, f32[4,2,4,128,128]{4,3,2,1,0:T(8,128)} %get-tuple-element.12.refs_0_, ...), custom_call_target="tpu_custom_call", output_to_operand_aliasing={{0}: (2, {}), {1}: (3, {})} | custom-call | flops 2000000000 | bytes 3145728 | tf_op jit(solution)/shard_map/lay/pallas_call | solution.py:212
  (1 shorter events, 0.0 us)
Async XLA Ops:
  0.6 13.4 %copy-start = (f32[32768]{0:T(1024)S(1)}, f32[32768]{0:T(1024)}, u32[]{:S(2)}) copy-start(f32[32768]{0:T(1024)} %param.6) | copy-start | bytes 393220
  2.2 20.4 %all-to-all-start = ((f32[32,1,128]{2,1,0:T(1,128)}), f32[32,1,128]{2,1,0:T(1,128)S(1)}, u32[]{:S(2)}, u32[]{:S(2)}) async-start(f32[32,1,128]{2,1,0:T(1,128)} %bitcast.26), calls=%async_computation | async-start | bytes 32768 | tf_op jit(solution)/shard_map/all_to_all | solution.py:230
  53.2 6.6 %collective-permute-start = (f32[4,4,192,128]{3,2,1,0:T(8,128)S(1)}, f32[4,4,192,128]{3,2,1,0:T(8,128)S(1)}, u32[]{:S(2)}, u32[]{:S(2)}) collective-permute-start(f32[4,4,192,128]{3,2,1,0:T(8,128)S(1)} %bitcast.22), channel_id=1, source_target_pairs={{0,1},{1,0},{2,3},{3,2},{4,5},{5,4},{6,7},{7,6},{8,9},{9,8},{10,11... | collective-permute-start | bytes 4718600 | tf_op jit(solution)/shard_map/ppermute | solution.py:246

commit v8 on v6

--- a/solution.py
+++ b/solution.py
@@ -83,7 +83,7 @@
     )(slope, curve, mean, var)
 
 
-def species_kernel(lam_ref, curve_ref, table_ref, sent_ref, turned_ref):
+def species_kernel(lam_ref, curve_ref, table_ref, sent_ref, done_ref, turned_ref):
     turned_ref[...] = jnp.transpose(table_ref[...])
     table = jnp.concatenate([turned_ref[pl.ds(p, 8, stride=16), :] for p in range(16)], axis=1)
     high = table.astype(jnp.bfloat16).astype(jnp.float32)
@@ -129,9 +129,7 @@
         return 0
 
     rows = lam_ref.shape[0]
-    for x in range(4):
-        for y in range(4):
-            sent_ref[x, y, 2 * rows :, :] = lam_ref[...]
+    done_ref[...] = lam_ref[...]
     lax.fori_loop(0, rows // 4, body, 0, unroll=4)
 
 
@@ -139,9 +137,12 @@
     rows = lam.shape[0]
     return pl.pallas_call(
         species_kernel,
-        out_shape=jax.ShapeDtypeStruct((4, 4, 3 * rows, LANES), jnp.float32),
+        out_shape=[
+            jax.ShapeDtypeStruct((4, 4, 2 * rows, LANES), jnp.float32),
+            jax.ShapeDtypeStruct(lam.shape, jnp.float32),
+        ],
         in_specs=[pl.BlockSpec(memory_space=pltpu.VMEM)] * 3,
-        out_specs=pl.BlockSpec(memory_space=pltpu.VMEM),
+        out_specs=[pl.BlockSpec(memory_space=pltpu.VMEM)] * 2,
         scratch_shapes=[pltpu.VMEM((LANES, 32), jnp.float32)],
         cost_estimate=pl.CostEstimate(flops=6 * 10**9, bytes_accessed=1 << 19, transcendentals=0),
         compiler_params=pltpu.CompilerParams(vmem_limit_bytes=16 << 20),
@@ -169,39 +170,48 @@
     )(table)
 
 
-def lay_kernel(flip, core_ref, blocks_ref, *refs):
-    species_ref, lam_ref, sems = refs[-3:]
-    rows = lam_ref.shape[3]
-    core = core_ref[0] ^ flip
-    copies = []
-    for y in range(4):
-        copies.append((blocks_ref.at[:, y, pl.ds(0, 2 * rows), :], species_ref.at[y, core]))
-        copies.append((blocks_ref.at[:, y, pl.ds(2 * rows, rows), :], lam_ref.at[y, core]))
-    started = [pltpu.make_async_copy(a, b, sems.at[i]) for i, (a, b) in enumerate(copies)]
+def lay_kernel(flip, by_xor, place_ref, blocks_ref, *refs):
+    out_ref, sems = refs[-2:]
+    x, y, core = place_ref[0], place_ref[1], place_ref[2] ^ flip
+    started = []
+    for e in range(4):
+        if by_xor:
+            pairs = [(blocks_ref.at[e, d], out_ref.at[y ^ e, core, x ^ d]) for d in range(4)]
+        else:
+            pairs = [(blocks_ref.at[:, e], out_ref.at[e, core])]
+        started += [pltpu.make_async_copy(a, b, sems.at[e, d]) for d, (a, b) in enumerate(pairs)]
     for copy in started:
         copy.start()
     for copy in started:
         copy.wait()
 
 
-def lay(core, blocks, flip, laid=()):
+def lay(place, blocks, flip, by_xor, laid=()):
     anywhere = pl.BlockSpec(memory_space=pl.ANY)
-    rows = blocks.shape[2] // 3
-    return pl.pallas_call(
-        functools.partial(lay_kernel, flip),
-        out_shape=[
-            jax.ShapeDtypeStruct((4, 2, 4, 2 * rows, LANES), jnp.float32),
-            jax.ShapeDtypeStruct((4, 2, 4, rows, LANES), jnp.float32),
-        ],
+    return pl.pallas_call(
+        functools.partial(lay_kernel, flip, by_xor),
+        out_shape=jax.ShapeDtypeStruct((4, 2, 4, *blocks.shape[2:]), jnp.float32),
         in_specs=[pl.BlockSpec(memory_space=pltpu.SMEM), pl.BlockSpec(memory_space=pltpu.VMEM)]
         + [anywhere] * len(laid),
-        out_specs=[anywhere] * 2,
-        input_output_aliases={2: 0, 3: 1} if laid else {},
-        scratch_shapes=[pltpu.SemaphoreType.DMA((8,))],
-        cost_estimate=pl.CostEstimate(flops=2 * 10**9, bytes_accessed=3 << 20, transcendentals=0),
+        out_specs=anywhere,
+        input_output_aliases={2: 0} if laid else {},
+        scratch_shapes=[pltpu.SemaphoreType.DMA((4, 4))],
+        cost_estimate=pl.CostEstimate(
+            flops=10**6 if by_xor else 2 * 10**9, bytes_accessed=1 << 10 if by_xor else 3 << 20, transcendentals=0
+        ),
         compiler_params=pltpu.CompilerParams(vmem_limit_bytes=4 << 20),
         name="lay",
-    )(core, blocks, *laid)
+    )(place, blocks, *laid)
+
+
+def with_partners(block, axis):
+    others = [lax.ppermute(block, axis, [(i, i ^ d) for i in range(4)]) for d in (1, 2, 3)]
+    return jnp.stack([block, *others])
+
+
+def swap_and_lay(place, own, by_xor):
+    other = lax.ppermute(own, "core", [(0, 1), (1, 0)])
+    return lay(place, other, 1, by_xor, (lay(place, own, 0, by_xor),))
 
 
 def exchange(array, axes):
@@ -210,7 +220,7 @@
 
 def per_device(slope, curvature, target_mean, target_var, table):
     x = lax.axis_index("x")
-    core = jnp.reshape(lax.axis_index("core"), (1,)).astype(jnp.int32)
+    place = jnp.stack([x, lax.axis_index("y"), lax.axis_index("core")]).astype(jnp.int32)
     points = exchange(blocks(table.T).reshape(32, LANES), ("z", "x"))
 
     size = slope.shape[0] // 4
@@ -219,10 +229,11 @@
         for a in (slope, curvature, target_mean, target_var)
     ]
     lam = newton(*mine)
-    sent = species(lam, mine[1], points)
+    sent, lam = species(lam, mine[1], points)
     own = exchange(sent.reshape(16, *sent.shape[2:]), ("x", "y")).reshape(sent.shape)
-    other = lax.ppermute(own, "core", [(0, 1), (1, 0)])
-    values, final_slope = lay(core, other, 1, lay(core, own, 0))
+    final_slope = swap_and_lay(place, with_partners(with_partners(lam, "x"), "y"), True)
+    own, final_slope = lax.optimization_barrier((own, final_slope))
+    values = swap_and_lay(place, own, False)
     values = jnp.transpose(values.reshape(-1, 2, LANES), (1, 0, 2)).reshape(2, -1)
     return values, final_slope.reshape(-1)
 

time: 60.9 us -> 68.7 us (1.13)
  blocking collectives: 25.8 us -> 0 us
  waiting for transfers between devices: 3.03 us -> 18.7 us
  starting transfers between devices: 15.1 us -> 28 us
  Pallas kernels: 13.7 us -> 18.5 us
    all_to_all x1 -> x0, blocking collectives: 25.8 us -> none  [exchange(): return lax.all_to_all(array, axes, split_axis=0, concat_axis=0, tiled=True)]
    ppermute x1 -> x8, waiting for transfers between devices: 1.83 us -> 17.5 us  [the longest x6 16.9 us: with_partners(): lax.ppermute(block, axis, [(i, i ^ d) for i in range(4)])]
    ppermute x1 -> x8, starting transfers between devices: 3.26 us -> 10.6 us  [the longest x6 6.73 us: with_partners(): lax.ppermute(block, axis, [(i, i ^ d) for i in range(4)])]
    all_to_all x1 -> x2, starting transfers between devices: 11.9 us -> 17.4 us  [exchange(): return lax.all_to_all(array, axes, split_axis=0, concat_axis=0, tiled=True)]
    pallas_call x3 -> x5, Pallas kernels: 7.19 us -> 12 us  [the longest x4 6.22 us: lay(): pl.pallas_call(functools.partial(lay_kernel, flip, by_xor), out_shape=jax...]
  transfers between devices with their start and end apart: 2 -> 10, of which waited for: 2 -> 7; matrix products, arithmetic and copies ran while one was open for 3% -> 2% of each run, Pallas kernels for 11% -> 15%
where the time goes in v8:
time: 68.7 us; the launch traced here: 68.3 us
  starting transfers between devices  28 us (41%)
  waiting for transfers between devices  18.7 us (27%)
  Pallas kernels  18.5 us (27%)
  local copies, waits for them, and re-layouts  2.25 us (3%)
  between operations  0.73 us (1%)
    all_to_all x2, starting transfers between devices, exchange(): return lax.all_to_all(array, axes, split_axis=0, concat_axis=0, tiled=True)  17.4 us
    ppermute x6, waiting for transfers between devices, with_partners(): lax.ppermute(block, axis, [(i, i ^ d) for i in range(4)])  16.9 us
    ppermute x6, starting transfers between devices, with_partners(): lax.ppermute(block, axis, [(i, i ^ d) for i in range(4)])  6.73 us
    pallas_call x4, Pallas kernels, lay(): pl.pallas_call(functools.partial(lay_kernel, flip, by_xor), out_shape=jax...  6.22 us
    pallas_call x1, Pallas kernels, species(): pl.pallas_call(species_kernel, out_shape=[jax.ShapeDtypeStruct((4, 4, 2 *...  5.78 us
    pallas_call x1, Pallas kernels, newton(): pl.pallas_call(newton_kernel, out_shape=jax.ShapeDtypeStruct(slope.shape,...  5.73 us
    ppermute x2, starting transfers between devices, swap_and_lay(): other = lax.ppermute(own, 'core', [(0, 1), (1, 0)])  3.84 us
    reshape x2, local copies, waits for them, and re-layouts, per_device(): lax.dynamic_slice_in_dim(a, x * size, size, 0).reshape(-1, LANES)  1.56 us
  transfers between devices with their start and end apart: 10, of which 7 were waited for; matrix products, arithmetic and copies ran while one was open for 2% of the time, Pallas kernels for 15%

profile of v8, /device:TPU:1, one launch (start us, length us, event | category | flops | bytes accessed | tf_op | source)
XLA Modules:
  0.0 68.3 jit_solution(17091815477866644657)
XLA Ops:
  0.6 0.0 copy-start
  0.6 0.7 %copy-done = f32[64,16]{0,1:T(8,128)S(1)} copy-done((f32[64,16]{0,1:T(8,128)S(1)}, f32[64,16]{0,1:T(8,128)}, u32[]{:S(2)}) %copy-start) | copy-done | bytes 4120
  1.3 0.8 %blocks.1 = f32[8,4,128]{2,1,0:T(4,128)} custom-call(f32[16,64]{1,0:T(8,128)S(1)} %bitcast.37), custom_call_target="tpu_custom_call" | custom-call | tf_op jit(solution)/shard_map/blocks/pallas_call | solution.py:162
  2.1 11.9 %all-to-all-start = ((f32[32,1,128]{2,1,0:T(1,128)}), f32[32,1,128]{2,1,0:T(1,128)S(1)}, u32[]{:S(2)}, u32[]{:S(2)}) async-start(f32[32,1,128]{2,1,0:T(1,128)} %bitcast.9), calls=%async_computation | async-start | bytes 32768 | tf_op jit(solution)/shard_map/all_to_all | solution.py:218
  14.0 0.8 %dynamic-slice_bitcast_fusion.2 = (f32[64,128]{1,0:T(8,128)S(1)}, f32[64,128]{1,0:T(8,128)S(1)}) fusion(f32[32768]{0:T(1024)} %param.6, s32[]{:T(128)S(6)} %select_n.2, f32[32768]{0:T(1024)} %param.5), kind=kLoop, calls=%fused_computation.4 | loop fusion | bytes 131076 | tf_op jit(solution)/shard_map/reshape | solution.py:228
  14.8 0.8 %dynamic-slice_bitcast_fusion = (f32[64,128]{1,0:T(8,128)S(1)}, f32[64,128]{1,0:T(8,128)S(1)}) fusion(f32[32768]{0:T(1024)} %param.8, s32[]{:T(128)S(6)} %select_n.2, f32[32768]{0:T(1024)} %param.7), kind=kLoop, calls=%fused_computation.2 | loop fusion | bytes 131076 | tf_op jit(solution)/shard_map/reshape | solution.py:228
  15.6 5.7 %newton.1.lam_ref = f32[64,128]{1,0:T(8,128)S(1)} custom-call(f32[64,128]{1,0:T(8,128)S(1)} %get-tuple-element.15.slope_ref, f32[64,128]{1,0:T(8,128)S(1)} %get-tuple-element.14.curve_ref, f32[64,128]{1,0:T(8,128)S(1)} %get-tuple-element.13.mean_ref, f32[64,128]{1,0:T(8,128)S(1)} %get-tuple-element.12.var_ref), custom_call_target="tpu_custom_call" | custom-call | flops 12000000000 | bytes 262144 | tf_op jit(solution)/shard_map/newton/pallas_call | solution.py:73
  21.3 1.2 %all-to-all-done = f32[32,1,128]{2,1,0:T(1,128)S(1)} async-done(((f32[32,1,128]{2,1,0:T(1,128)}), f32[32,1,128]{2,1,0:T(1,128)S(1)}, u32[]{:S(2)}, u32[]{:S(2)}) %all-to-all-start) | async-done | bytes 16416 | tf_op jit(solution)/shard_map/all_to_all | solution.py:218
  22.5 5.8 %species.1 = (f32[4,4,128,128]{3,2,1,0:T(8,128)}, f32[64,128]{1,0:T(8,128)S(1)}) custom-call(f32[64,128]{1,0:T(8,128)S(1)} %newton.1.lam_ref, f32[64,128]{1,0:T(8,128)S(1)} %get-tuple-element.14.curve_ref, f32[32,128]{1,0:T(8,128)S(1)} %bitcast.36), custom_call_target="tpu_custom_call" | custom-call | flops 6000000000 | bytes 524288 | tf_op jit(solution)/shard_map/species/pallas_call | solution.py:138
  28.3 5.6 %all-to-all-start.1 = ((f32[16,128,128]{2,1,0:T(8,128)}), f32[16,128,128]{2,1,0:T(8,128)S(1)}, u32[]{:S(2)}, u32[]{:S(2)}) async-start(f32[16,128,128]{2,1,0:T(8,128)} %bitcast.11), calls=%async_computation.1 | async-start | bytes 2097152 | tf_op jit(solution)/shard_map/all_to_all | solution.py:218
  33.8 2.6 %collective-permute-start.2 = (f32[64,128]{1,0:T(8,128)S(1)}, f32[64,128]{1,0:T(8,128)S(1)}, u32[]{:S(2)}, u32[]{:S(2)}) collective-permute-start(f32[64,128]{1,0:T(8,128)S(1)} %get-tuple-element.7), channel_id=1, source_target_pairs={{0,24},{8,16},{16,8},{24,0},{1,25},{9,17},{17,9},{25,1},{2,26},{10... | collective-permute-start | bytes 98312 | tf_op jit(solution)/shard_map/ppermute | solution.py:208
  36.4 0.6 collective-permute-start.1
  37.0 0.2 collective-permute-start
  37.2 7.0 %collective-permute-done.2 = f32[64,128]{1,0:T(8,128)S(1)} collective-permute-done((f32[64,128]{1,0:T(8,128)S(1)}, f32[64,128]{1,0:T(8,128)S(1)}, u32[]{:S(2)}, u32[]{:S(2)}) %collective-permute-start.2) | collective-permute-done | bytes 32800 | tf_op jit(solution)/shard_map/ppermute | solution.py:208
  44.2 3.7 %collective-permute-done.1 = f32[64,128]{1,0:T(8,128)S(1)} collective-permute-done((f32[64,128]{1,0:T(8,128)S(1)}, f32[64,128]{1,0:T(8,128)S(1)}, u32[]{:S(2)}, u32[]{:S(2)}) %collective-permute-start.1) | collective-permute-done | bytes 32800 | tf_op jit(solution)/shard_map/ppermute | solution.py:208
  47.8 0.0 collective-permute-done
  47.9 2.9 %collective-permute-start.4 = (f32[4,64,128]{2,1,0:T(8,128)S(1)}, f32[4,64,128]{2,1,0:T(8,128)S(1)}, u32[]{:S(2)}, u32[]{:S(2)}) collective-permute-start(f32[4,64,128]{2,1,0:T(8,128)S(1)} %get-tuple-element.11), channel_id=1, source_target_pairs={{0,4},{2,6},{4,0},{6,2},{1,5},{3,7},{5,1},{7,3},{8,12},{10,14},{12... | collective-permute-start | bytes 393224 | tf_op jit(solution)/shard_map/ppermute | solution.py:208
  50.7 0.3 collective-permute-start.3
  51.0 0.2 collective-permute-start.5
  51.2 2.2 %collective-permute-done.4 = f32[4,64,128]{2,1,0:T(8,128)S(1)} collective-permute-done((f32[4,64,128]{2,1,0:T(8,128)S(1)}, f32[4,64,128]{2,1,0:T(8,128)S(1)}, u32[]{:S(2)}, u32[]{:S(2)}) %collective-permute-start.4) | collective-permute-done | bytes 131104 | tf_op jit(solution)/shard_map/ppermute | solution.py:208
  53.4 1.4 %collective-permute-done.3 = f32[4,64,128]{2,1,0:T(8,128)S(1)} collective-permute-done((f32[4,64,128]{2,1,0:T(8,128)S(1)}, f32[4,64,128]{2,1,0:T(8,128)S(1)}, u32[]{:S(2)}, u32[]{:S(2)}) %collective-permute-start.3) | collective-permute-done | bytes 131104 | tf_op jit(solution)/shard_map/ppermute | solution.py:208
  54.8 2.7 %collective-permute-done.5 = f32[4,64,128]{2,1,0:T(8,128)S(1)} collective-permute-done((f32[4,64,128]{2,1,0:T(8,128)S(1)}, f32[4,64,128]{2,1,0:T(8,128)S(1)}, u32[]{:S(2)}, u32[]{:S(2)}) %collective-permute-start.5) | collective-permute-done | bytes 131104 | tf_op jit(solution)/shard_map/ppermute | solution.py:208
  57.5 3.4 %collective-permute-start.6 = (f32[4,4,64,128]{3,2,1,0:T(8,128)S(1)}, f32[4,4,64,128]{3,2,1,0:T(8,128)S(1)}, u32[]{:S(2)}, u32[]{:S(2)}) collective-permute-start(f32[4,4,64,128]{3,2,1,0:T(8,128)S(1)} %pad_maximum_fusion.blocks_ref), channel_id=1, source_target_pairs={{0,1},{1,0},{2,3},{3,2},{4,5},{5,4},{6,7},{7,6},{8,9},{9,8},{10,11... | collective-permute-start | bytes 1572872 | tf_op jit(solution)/shard_map/ppermute | solution.py:213
  60.9 0.1 pad_add_fusion.place_ref
  61.0 1.5 %lay.4.refs_0_ = f32[4,2,4,64,128]{4,3,2,1,0:T(8,128)} custom-call(s32[3]{0:T(128)S(1)} %pad_add_fusion.place_ref, f32[4,4,64,128]{3,2,1,0:T(8,128)S(1)} %pad_maximum_fusion.blocks_ref), custom_call_target="tpu_custom_call" | custom-call | flops 1000000 | bytes 1024 | tf_op jit(solution)/shard_map/lay/pallas_call | solution.py:191
  62.5 0.0 collective-permute-done.6.blocks_ref
  62.5 1.5 %lay.5 = f32[4,2,4,64,128]{4,3,2,1,0:T(8,128)} custom-call(s32[3]{0:T(128)S(1)} %pad_add_fusion.place_ref, f32[4,4,64,128]{3,2,1,0:T(8,128)S(1)} %collective-permute-done.6.blocks_ref, f32[4,2,4,64,128]{4,3,2,1,0:T(8,128)} %lay.4.refs_0_), custom_call_target="tpu_custom_call", output_to_operand_aliasing={{}: (2, {})} | custom-call | flops 1000000 | bytes 1024 | tf_op jit(solution)/shard_map/lay/pallas_call | solution.py:191
  63.9 0.0 all-to-all-done.1
  63.9 0.4 collective-permute-start.7
  64.4 1.6 %lay.6.refs_0_ = f32[4,2,4,128,128]{4,3,2,1,0:T(8,128)} custom-call(s32[3]{0:T(128)S(1)} %pad_add_fusion.place_ref, f32[4,4,128,128]{3,2,1,0:T(8,128)S(1)} %bitcast.34), custom_call_target="tpu_custom_call" | custom-call | flops 2000000000 | bytes 3145728 | tf_op jit(solution)/shard_map/lay/pallas_call | solution.py:191
  66.0 0.7 collective-permute-done.7.blocks_ref
  66.7 1.6 %lay.7 = f32[4,2,4,128,128]{4,3,2,1,0:T(8,128)} custom-call(s32[3]{0:T(128)S(1)} %pad_add_fusion.place_ref, f32[4,4,128,128]{3,2,1,0:T(8,128)S(1)} %collective-permute-done.7.blocks_ref, f32[4,2,4,128,128]{4,3,2,1,0:T(8,128)} %lay.6.refs_0_), custom_call_target="tpu_custom_call", output_to_operand_aliasing={{}: (2, {})} | custom-call | flops 2000000000 | bytes 3145728 | tf_op jit(solution)/shard_map/lay/pallas_call | solution.py:191
  (2 shorter events, 0.1 us)
Async XLA Ops:
  0.6 0.7 %copy-start = (f32[64,16]{0,1:T(8,128)S(1)}, f32[64,16]{0,1:T(8,128)}, u32[]{:S(2)}) copy-start(f32[64,16]{0,1:T(8,128)} %param.9) | copy-start | bytes 12292
  2.1 20.4 %all-to-all-start = ((f32[32,1,128]{2,1,0:T(1,128)}), f32[32,1,128]{2,1,0:T(1,128)S(1)}, u32[]{:S(2)}, u32[]{:S(2)}) async-start(f32[32,1,128]{2,1,0:T(1,128)} %bitcast.9), calls=%async_computation | async-start | bytes 32768 | tf_op jit(solution)/shard_map/all_to_all | solution.py:218
  28.3 35.7 %all-to-all-start.1 = ((f32[16,128,128]{2,1,0:T(8,128)}), f32[16,128,128]{2,1,0:T(8,128)S(1)}, u32[]{:S(2)}, u32[]{:S(2)}) async-start(f32[16,128,128]{2,1,0:T(8,128)} %bitcast.11), calls=%async_computation.1 | async-start | bytes 2097152 | tf_op jit(solution)/shard_map/all_to_all | solution.py:218
  33.8 10.3 %collective-permute-start.2 = (f32[64,128]{1,0:T(8,128)S(1)}, f32[64,128]{1,0:T(8,128)S(1)}, u32[]{:S(2)}, u32[]{:S(2)}) collective-permute-start(f32[64,128]{1,0:T(8,128)S(1)} %get-tuple-element.7), channel_id=1, source_target_pairs={{0,24},{8,16},{16,8},{24,0},{1,25},{9,17},{17,9},{25,1},{2,26},{10... | collective-permute-start | bytes 98312 | tf_op jit(solution)/shard_map/ppermute | solution.py:208
  36.4 11.4 %collective-permute-start.1 = (f32[64,128]{1,0:T(8,128)S(1)}, f32[64,128]{1,0:T(8,128)S(1)}, u32[]{:S(2)}, u32[]{:S(2)}) collective-permute-start(f32[64,128]{1,0:T(8,128)S(1)} %get-tuple-element.7), channel_id=1, source_target_pairs={{0,16},{8,24},{16,0},{24,8},{1,17},{9,25},{17,1},{25,9},{2,18},{10... | collective-permute-start | bytes 98312 | tf_op jit(solution)/shard_map/ppermute | solution.py:208
  37.0 10.8 %collective-permute-start = (f32[64,128]{1,0:T(8,128)S(1)}, f32[64,128]{1,0:T(8,128)S(1)}, u32[]{:S(2)}, u32[]{:S(2)}) collective-permute-start(f32[64,128]{1,0:T(8,128)S(1)} %get-tuple-element.7), channel_id=1, source_target_pairs={{0,8},{8,0},{16,24},{24,16},{1,9},{9,1},{17,25},{25,17},{2,10},{10... | collective-permute-start | bytes 98312 | tf_op jit(solution)/shard_map/ppermute | solution.py:208
  47.9 5.5 %collective-permute-start.4 = (f32[4,64,128]{2,1,0:T(8,128)S(1)}, f32[4,64,128]{2,1,0:T(8,128)S(1)}, u32[]{:S(2)}, u32[]{:S(2)}) collective-permute-start(f32[4,64,128]{2,1,0:T(8,128)S(1)} %get-tuple-element.11), channel_id=1, source_target_pairs={{0,4},{2,6},{4,0},{6,2},{1,5},{3,7},{5,1},{7,3},{8,12},{10,14},{12... | collective-permute-start | bytes 393224 | tf_op jit(solution)/shard_map/ppermute | solution.py:208
  50.7 4.0 %collective-permute-start.3 = (f32[4,64,128]{2,1,0:T(8,128)S(1)}, f32[4,64,128]{2,1,0:T(8,128)S(1)}, u32[]{:S(2)}, u32[]{:S(2)}) collective-permute-start(f32[4,64,128]{2,1,0:T(8,128)S(1)} %get-tuple-element.11), channel_id=1, source_target_pairs={{0,2},{2,0},{4,6},{6,4},{1,3},{3,1},{5,7},{7,5},{8,10},{10,8},{12,... | collective-permute-start | bytes 393224 | tf_op jit(solution)/shard_map/ppermute | solution.py:208
  51.0 6.4 %collective-permute-start.5 = (f32[4,64,128]{2,1,0:T(8,128)S(1)}, f32[4,64,128]{2,1,0:T(8,128)S(1)}, u32[]{:S(2)}, u32[]{:S(2)}) collective-permute-start(f32[4,64,128]{2,1,0:T(8,128)S(1)} %get-tuple-element.11), channel_id=1, source_target_pairs={{0,6},{2,4},{4,2},{6,0},{1,7},{3,5},{5,3},{7,1},{8,14},{10,12},{12... | collective-permute-start | bytes 393224 | tf_op jit(solution)/shard_map/ppermute | solution.py:208
  57.5 4.9 %collective-permute-start.6 = (f32[4,4,64,128]{3,2,1,0:T(8,128)S(1)}, f32[4,4,64,128]{3,2,1,0:T(8,128)S(1)}, u32[]{:S(2)}, u32[]{:S(2)}) collective-permute-start(f32[4,4,64,128]{3,2,1,0:T(8,128)S(1)} %pad_maximum_fusion.blocks_ref), channel_id=1, source_target_pairs={{0,1},{1,0},{2,3},{3,2},{4,5},{5,4},{6,7},{7,6},{8,9},{9,8},{10,11... | collective-permute-start | bytes 1572872 | tf_op jit(solution)/shard_map/ppermute | solution.py:213
  63.9 2.7 %collective-permute-start.7 = (f32[4,4,128,128]{3,2,1,0:T(8,128)S(1)}, f32[4,4,128,128]{3,2,1,0:T(8,128)S(1)}, u32[]{:S(2)}, u32[]{:S(2)}) collective-permute-start(f32[4,4,128,128]{3,2,1,0:T(8,128)S(1)} %bitcast.33), channel_id=1, source_target_pairs={{0,1},{1,0},{2,3},{3,2},{4,5},{5,4},{6,7},{7,6},{8,9},{9,8},{10,11... | collective-permute-start | bytes 3145736 | tf_op jit(solution)/shard_map/ppermute | solution.py:213

commit v9 on v6

--- a/solution.py
+++ b/solution.py
@@ -87,8 +87,9 @@
     turned_ref[...] = jnp.transpose(table_ref[...])
     table = jnp.concatenate([turned_ref[pl.ds(p, 8, stride=16), :] for p in range(16)], axis=1)
     high = table.astype(jnp.bfloat16).astype(jnp.float32)
-    ones = jnp.ones((16, table.shape[1]), jnp.float32)
-    left = jnp.concatenate([high, table - high, ones], axis=0).astype(jnp.bfloat16)
+    ones = jnp.ones((8, table.shape[1]), jnp.float32)
+    for_high = jnp.concatenate([high, ones, table - high], axis=0).astype(jnp.bfloat16)
+    for_low = jnp.concatenate([high, ones], axis=0).astype(jnp.bfloat16)
     sub = lax.broadcasted_iota(jnp.int32, (8, LANES), 0).astype(jnp.float32)
 
     def tile(row):
@@ -114,9 +115,9 @@
         e = jnp.concatenate([tile(row), tile(row + 1)], axis=1)
         e_high = e.astype(jnp.bfloat16)
         e_low = (e - e_high.astype(jnp.float32)).astype(jnp.bfloat16)
-        sums = jnp.dot(left, e_high, preferred_element_type=jnp.float32)
-        sums = sums + jnp.dot(left, e_low, preferred_element_type=jnp.float32)
-        values = (sums[0:8] + sums[8:16]) / sums[16:24]
+        sums = jnp.dot(for_high, e_high, preferred_element_type=jnp.float32)
+        more = jnp.dot(for_low, e_low, preferred_element_type=jnp.float32)
+        values = (sums[0:8] + sums[16:24] + more[0:8]) / (sums[8:16] + more[8:16])
         return [values[:, :LANES], values[:, LANES:]]
 
     def body(t, _):
@@ -132,7 +133,7 @@
     for x in range(4):
         for y in range(4):
             sent_ref[x, y, 2 * rows :, :] = lam_ref[...]
-    lax.fori_loop(0, rows // 4, body, 0, unroll=4)
+    lax.fori_loop(0, rows // 4, body, 0, unroll=16)
 
 
 def species(lam, curve, table):

time: 60.9 us -> 59.5 us (0.977)
  Pallas kernels: 13.7 us -> 12.3 us
    pallas_call x1, Pallas kernels: 4.79 us -> 3.4 us  [species(): pl.pallas_call(species_kernel, out_shape=jax.ShapeDtypeStruct((4, 4, 3 *...]
  transfers between devices with their start and end apart: 2 -> 2, of which waited for: 2 -> 2; matrix products, arithmetic and copies ran while one was open for 3% -> 3% of each run, Pallas kernels for 11% -> 12%
where the time goes in v9:
time: 59.5 us; the launch traced here: 59.2 us
  blocking collectives  25.8 us (43%)
  starting transfers between devices  15.1 us (25%)
  Pallas kernels  12.3 us (21%)
  waiting for transfers between devices  3.03 us (5%)
  local copies, waits for them, and re-layouts  2.25 us (4%)
  between operations  0.68 us (1%)
    all_to_all x1, blocking collectives, exchange(): return lax.all_to_all(array, axes, split_axis=0, concat_axis=0, tiled=True)  25.8 us
    all_to_all x1, starting transfers between devices, exchange(): return lax.all_to_all(array, axes, split_axis=0, concat_axis=0, tiled=True)  11.9 us
    pallas_call x1, Pallas kernels, newton(): pl.pallas_call(newton_kernel, out_shape=jax.ShapeDtypeStruct(slope.shape,...  5.73 us
    pallas_call x1, Pallas kernels, species(): pl.pallas_call(species_kernel, out_shape=jax.ShapeDtypeStruct((4, 4, 3 *...  3.4 us
    ppermute x1, starting transfers between devices, per_device(): other = lax.ppermute(own, 'core', [(0, 1), (1, 0)])  3.26 us
    pallas_call x2, Pallas kernels, lay(): pl.pallas_call(functools.partial(lay_kernel, flip), out_shape=[jax.ShapeD...  2.39 us
    ppermute x1, waiting for transfers between devices, per_device(): other = lax.ppermute(own, 'core', [(0, 1), (1, 0)])  1.83 us
    reshape x2, local copies, waits for them, and re-layouts, per_device(): lax.dynamic_slice_in_dim(a, x * size, size, 0).reshape(-1, LANES)  1.56 us
  transfers between devices with their start and end apart: 2, of which 2 were waited for; matrix products, arithmetic and copies ran while one was open for 3% of the time, Pallas kernels for 12%

profile of v9, /device:TPU:1, one launch (start us, length us, event | category | flops | bytes accessed | tf_op | source)
XLA Modules:
  0.0 59.2 jit_solution(15971398226649885270)
XLA Ops:
  0.6 0.0 copy-start
  0.6 0.7 %copy-done = f32[64,16]{0,1:T(8,128)S(1)} copy-done((f32[64,16]{0,1:T(8,128)S(1)}, f32[64,16]{0,1:T(8,128)}, u32[]{:S(2)}) %copy-start) | copy-done | bytes 4120
  1.3 0.8 %blocks.1 = f32[8,4,128]{2,1,0:T(4,128)} custom-call(f32[16,64]{1,0:T(8,128)S(1)} %bitcast.26), custom_call_target="tpu_custom_call" | custom-call | tf_op jit(solution)/shard_map/blocks/pallas_call | solution.py:162
  2.1 11.9 %all-to-all-start = ((f32[32,1,128]{2,1,0:T(1,128)}), f32[32,1,128]{2,1,0:T(1,128)S(1)}, u32[]{:S(2)}, u32[]{:S(2)}) async-start(f32[32,1,128]{2,1,0:T(1,128)} %bitcast.7), calls=%async_computation | async-start | bytes 32768 | tf_op jit(solution)/shard_map/all_to_all | solution.py:209
  14.0 0.8 %dynamic-slice_bitcast_fusion.2 = (f32[64,128]{1,0:T(8,128)S(1)}, f32[64,128]{1,0:T(8,128)S(1)}) fusion(f32[32768]{0:T(1024)} %param.6, s32[]{:T(128)S(6)} %select_n.2, f32[32768]{0:T(1024)} %param.5), kind=kLoop, calls=%fused_computation.2 | loop fusion | bytes 131076 | tf_op jit(solution)/shard_map/reshape | solution.py:219
  14.8 0.8 %dynamic-slice_bitcast_fusion = (f32[64,128]{1,0:T(8,128)S(1)}, f32[64,128]{1,0:T(8,128)S(1)}) fusion(f32[32768]{0:T(1024)} %param.8, s32[]{:T(128)S(6)} %select_n.2, f32[32768]{0:T(1024)} %param.7), kind=kLoop, calls=%fused_computation | loop fusion | bytes 131076 | tf_op jit(solution)/shard_map/reshape | solution.py:219
  15.6 5.7 %newton.1.lam_ref = f32[64,128]{1,0:T(8,128)S(1)} custom-call(f32[64,128]{1,0:T(8,128)S(1)} %get-tuple-element.13.slope_ref, f32[64,128]{1,0:T(8,128)S(1)} %get-tuple-element.12.curve_ref, f32[64,128]{1,0:T(8,128)S(1)} %get-tuple-element.11.mean_ref, f32[64,128]{1,0:T(8,128)S(1)} %get-tuple-element.10.var_ref), custom_call_target="tpu_custom_call" | custom-call | flops 12000000000 | bytes 262144 | tf_op jit(solution)/shard_map/newton/pallas_call | solution.py:73
  21.3 1.2 %all-to-all-done = f32[32,1,128]{2,1,0:T(1,128)S(1)} async-done(((f32[32,1,128]{2,1,0:T(1,128)}), f32[32,1,128]{2,1,0:T(1,128)S(1)}, u32[]{:S(2)}, u32[]{:S(2)}) %all-to-all-start) | async-done | bytes 16416 | tf_op jit(solution)/shard_map/all_to_all | solution.py:209
  22.5 3.4 %species.1 = f32[4,4,192,128]{3,2,1,0:T(8,128)S(1)} custom-call(f32[64,128]{1,0:T(8,128)S(1)} %newton.1.lam_ref, f32[64,128]{1,0:T(8,128)S(1)} %get-tuple-element.12.curve_ref, f32[32,128]{1,0:T(8,128)S(1)} %bitcast.25), custom_call_target="tpu_custom_call" | custom-call | flops 6000000000 | bytes 524288 | tf_op jit(solution)/shard_map/species/pallas_call | solution.py:141
  25.9 25.8 %all_to_all.16 = f32[16,192,128]{2,1,0:T(8,128)S(1)} all-to-all(f32[16,192,128]{2,1,0:T(8,128)S(1)} %bitcast.24), channel_id=1, replica_groups=mesh['z'=8,'x'=4,'y'=4,'core'=2] {'x','y'}, dimensions={0} | all-to-all | bytes 3145728 | tf_op jit(solution)/shard_map/all_to_all | solution.py:209
  51.7 3.3 %collective-permute-start = (f32[4,4,192,128]{3,2,1,0:T(8,128)S(1)}, f32[4,4,192,128]{3,2,1,0:T(8,128)S(1)}, u32[]{:S(2)}, u32[]{:S(2)}) collective-permute-start(f32[4,4,192,128]{3,2,1,0:T(8,128)S(1)} %bitcast.22), channel_id=1, source_target_pairs={{0,1},{1,0},{2,3},{3,2},{4,5},{5,4},{6,7},{7,6},{8,9},{9,8},{10,11... | collective-permute-start | bytes 4718600 | tf_op jit(solution)/shard_map/ppermute | solution.py:225
  54.9 1.2 %lay.2 = (f32[4,2,4,128,128]{4,3,2,1,0:T(8,128)}, f32[4,2,4,64,128]{4,3,2,1,0:T(8,128)}) custom-call(s32[1]{0:T(128)} %bitcast.core_ref, f32[4,4,192,128]{3,2,1,0:T(8,128)S(1)} %bitcast.23), custom_call_target="tpu_custom_call" | custom-call | flops 2000000000 | bytes 3145728 | tf_op jit(solution)/shard_map/lay/pallas_call | solution.py:191
  56.1 1.8 %collective-permute-done.blocks_ref = f32[4,4,192,128]{3,2,1,0:T(8,128)S(1)} collective-permute-done((f32[4,4,192,128]{3,2,1,0:T(8,128)S(1)}, f32[4,4,192,128]{3,2,1,0:T(8,128)S(1)}, u32[]{:S(2)}, u32[]{:S(2)}) %collective-permute-start) | collective-permute-done | bytes 1572896 | tf_op jit(solution)/shard_map/ppermute | solution.py:225
  58.0 1.2 %lay.3 = (f32[4,2,4,128,128]{4,3,2,1,0:T(8,128)}, f32[4,2,4,64,128]{4,3,2,1,0:T(8,128)}) custom-call(s32[1]{0:T(128)} %bitcast.core_ref, f32[4,4,192,128]{3,2,1,0:T(8,128)S(1)} %collective-permute-done.blocks_ref, f32[4,2,4,128,128]{4,3,2,1,0:T(8,128)} %get-tuple-element.6.refs_0_, ...), custom_call_target="tpu_custom_call", output_to_operand_aliasing={{0}: (2, {}), {1}: (3, {})} | custom-call | flops 2000000000 | bytes 3145728 | tf_op jit(solution)/shard_map/lay/pallas_call | solution.py:191
Async XLA Ops:
  0.6 0.7 %copy-start = (f32[64,16]{0,1:T(8,128)S(1)}, f32[64,16]{0,1:T(8,128)}, u32[]{:S(2)}) copy-start(f32[64,16]{0,1:T(8,128)} %param.9) | copy-start | bytes 12292
  2.1 20.4 %all-to-all-start = ((f32[32,1,128]{2,1,0:T(1,128)}), f32[32,1,128]{2,1,0:T(1,128)S(1)}, u32[]{:S(2)}, u32[]{:S(2)}) async-start(f32[32,1,128]{2,1,0:T(1,128)} %bitcast.7), calls=%async_computation | async-start | bytes 32768 | tf_op jit(solution)/shard_map/all_to_all | solution.py:209
  51.7 6.3 %collective-permute-start = (f32[4,4,192,128]{3,2,1,0:T(8,128)S(1)}, f32[4,4,192,128]{3,2,1,0:T(8,128)S(1)}, u32[]{:S(2)}, u32[]{:S(2)}) collective-permute-start(f32[4,4,192,128]{3,2,1,0:T(8,128)S(1)} %bitcast.22), channel_id=1, source_target_pairs={{0,1},{1,0},{2,3},{3,2},{4,5},{5,4},{6,7},{7,6},{8,9},{9,8},{10,11... | collective-permute-start | bytes 4718600 | tf_op jit(solution)/shard_map/ppermute | solution.py:225

commit v10 on v9

--- a/solution.py
+++ b/solution.py
@@ -126,13 +126,13 @@
         for x in range(4):
             block = jnp.concatenate([v[2 * x : 2 * x + 2] for v in values], axis=0)
             for y in range(4):
-                sent_ref[x, y, rows, :] = block
+                sent_ref[y, x, rows, :] = block
         return 0
 
     rows = lam_ref.shape[0]
     for x in range(4):
         for y in range(4):
-            sent_ref[x, y, 2 * rows :, :] = lam_ref[...]
+            sent_ref[y, x, 2 * rows :, :] = lam_ref[...]
     lax.fori_loop(0, rows // 4, body, 0, unroll=16)
 
 
@@ -174,10 +174,10 @@
     species_ref, lam_ref, sems = refs[-3:]
     rows = lam_ref.shape[3]
     core = core_ref[0] ^ flip
-    copies = []
-    for y in range(4):
-        copies.append((blocks_ref.at[:, y, pl.ds(0, 2 * rows), :], species_ref.at[y, core]))
-        copies.append((blocks_ref.at[:, y, pl.ds(2 * rows, rows), :], lam_ref.at[y, core]))
+    copies = [
+        (blocks_ref.at[:, :, pl.ds(0, 2 * rows), :], species_ref.at[:, core]),
+        (blocks_ref.at[:, :, pl.ds(2 * rows, rows), :], lam_ref.at[:, core]),
+    ]
     started = [pltpu.make_async_copy(a, b, sems.at[i]) for i, (a, b) in enumerate(copies)]
     for copy in started:
         copy.start()
@@ -198,7 +198,7 @@
         + [anywhere] * len(laid),
         out_specs=[anywhere] * 2,
         input_output_aliases={2: 0, 3: 1} if laid else {},
-        scratch_shapes=[pltpu.SemaphoreType.DMA((8,))],
+        scratch_shapes=[pltpu.SemaphoreType.DMA((2,))],
         cost_estimate=pl.CostEstimate(flops=2 * 10**9, bytes_accessed=3 << 20, transcendentals=0),
         compiler_params=pltpu.CompilerParams(vmem_limit_bytes=4 << 20),
         name="lay",
@@ -221,7 +221,7 @@
     ]
     lam = newton(*mine)
     sent = species(lam, mine[1], points)
-    own = exchange(sent.reshape(16, *sent.shape[2:]), ("x", "y")).reshape(sent.shape)
+    own = exchange(sent.reshape(16, *sent.shape[2:]), ("y", "x")).reshape(sent.shape)
     other = lax.ppermute(own, "core", [(0, 1), (1, 0)])
     values, final_slope = lay(core, other, 1, lay(core, own, 0))
     values = jnp.transpose(values.reshape(-1, 2, LANES), (1, 0, 2)).reshape(2, -1)

time: 59.5 us -> 59.7 us (level)
  blocking collectives: 25.8 us -> 26.6 us
  starting transfers between devices: 15.1 us -> 14.5 us
    all_to_all x1, blocking collectives: 25.8 us -> 26.6 us  [exchange(): return lax.all_to_all(array, axes, split_axis=0, concat_axis=0, tiled=True)]
    ppermute x1, starting transfers between devices: 3.26 us -> 2.66 us  [per_device(): other = lax.ppermute(own, 'core', [(0, 1), (1, 0)])]
where the time goes in v10:
time: 59.7 us; the launch traced here: 59.3 us
  blocking collectives  26.6 us (45%)
  starting transfers between devices  14.5 us (24%)
  Pallas kernels  12.2 us (20%)
  waiting for transfers between devices  3.07 us (5%)
  local copies, waits for them, and re-layouts  2.25 us (4%)
  between operations  0.68 us (1%)
    all_to_all x1, blocking collectives, exchange(): return lax.all_to_all(array, axes, split_axis=0, concat_axis=0, tiled=True)  26.6 us
    all_to_all x1, starting transfers between devices, exchange(): return lax.all_to_all(array, axes, split_axis=0, concat_axis=0, tiled=True)  11.9 us
    pallas_call x1, Pallas kernels, newton(): pl.pallas_call(newton_kernel, out_shape=jax.ShapeDtypeStruct(slope.shape,...  5.73 us
    pallas_call x1, Pallas kernels, species(): pl.pallas_call(species_kernel, out_shape=jax.ShapeDtypeStruct((4, 4, 3 *...  3.4 us
    ppermute x1, starting transfers between devices, per_device(): other = lax.ppermute(own, 'core', [(0, 1), (1, 0)])  2.66 us
    pallas_call x2, Pallas kernels, lay(): pl.pallas_call(functools.partial(lay_kernel, flip), out_shape=[jax.ShapeD...  2.31 us
    ppermute x1, waiting for transfers between devices, per_device(): other = lax.ppermute(own, 'core', [(0, 1), (1, 0)])  1.88 us
    reshape x2, local copies, waits for them, and re-layouts, per_device(): lax.dynamic_slice_in_dim(a, x * size, size, 0).reshape(-1, LANES)  1.56 us
  transfers between devices with their start and end apart: 2, of which 2 were waited for; matrix products, arithmetic and copies ran while one was open for 3% of the time, Pallas kernels for 12%

profile of v10, /device:TPU:1, one launch (start us, length us, event | category | flops | bytes accessed | tf_op | source)
XLA Modules:
  0.0 59.3 jit_solution(6521679257159866749)
XLA Ops:
  0.6 0.0 copy-start
  0.6 0.7 %copy-done = f32[64,16]{0,1:T(8,128)S(1)} copy-done((f32[64,16]{0,1:T(8,128)S(1)}, f32[64,16]{0,1:T(8,128)}, u32[]{:S(2)}) %copy-start) | copy-done | bytes 4120
  1.3 0.8 %blocks.1 = f32[8,4,128]{2,1,0:T(4,128)} custom-call(f32[16,64]{1,0:T(8,128)S(1)} %bitcast.26), custom_call_target="tpu_custom_call" | custom-call | tf_op jit(solution)/shard_map/blocks/pallas_call | solution.py:162
  2.1 11.9 %all-to-all-start = ((f32[32,1,128]{2,1,0:T(1,128)}), f32[32,1,128]{2,1,0:T(1,128)S(1)}, u32[]{:S(2)}, u32[]{:S(2)}) async-start(f32[32,1,128]{2,1,0:T(1,128)} %bitcast.7), calls=%async_computation | async-start | bytes 32768 | tf_op jit(solution)/shard_map/all_to_all | solution.py:209
  14.0 0.8 %dynamic-slice_bitcast_fusion.2 = (f32[64,128]{1,0:T(8,128)S(1)}, f32[64,128]{1,0:T(8,128)S(1)}) fusion(f32[32768]{0:T(1024)} %param.6, s32[]{:T(128)S(6)} %select_n.2, f32[32768]{0:T(1024)} %param.5), kind=kLoop, calls=%fused_computation.2 | loop fusion | bytes 131076 | tf_op jit(solution)/shard_map/reshape | solution.py:219
  14.8 0.8 %dynamic-slice_bitcast_fusion = (f32[64,128]{1,0:T(8,128)S(1)}, f32[64,128]{1,0:T(8,128)S(1)}) fusion(f32[32768]{0:T(1024)} %param.8, s32[]{:T(128)S(6)} %select_n.2, f32[32768]{0:T(1024)} %param.7), kind=kLoop, calls=%fused_computation | loop fusion | bytes 131076 | tf_op jit(solution)/shard_map/reshape | solution.py:219
  15.6 5.7 %newton.1.lam_ref = f32[64,128]{1,0:T(8,128)S(1)} custom-call(f32[64,128]{1,0:T(8,128)S(1)} %get-tuple-element.13.slope_ref, f32[64,128]{1,0:T(8,128)S(1)} %get-tuple-element.12.curve_ref, f32[64,128]{1,0:T(8,128)S(1)} %get-tuple-element.11.mean_ref, f32[64,128]{1,0:T(8,128)S(1)} %get-tuple-element.10.var_ref), custom_call_target="tpu_custom_call" | custom-call | flops 12000000000 | bytes 262144 | tf_op jit(solution)/shard_map/newton/pallas_call | solution.py:73
  21.3 1.2 %all-to-all-done = f32[32,1,128]{2,1,0:T(1,128)S(1)} async-done(((f32[32,1,128]{2,1,0:T(1,128)}), f32[32,1,128]{2,1,0:T(1,128)S(1)}, u32[]{:S(2)}, u32[]{:S(2)}) %all-to-all-start) | async-done | bytes 16416 | tf_op jit(solution)/shard_map/all_to_all | solution.py:209
  22.5 3.4 %species.1 = f32[4,4,192,128]{3,2,1,0:T(8,128)S(1)} custom-call(f32[64,128]{1,0:T(8,128)S(1)} %newton.1.lam_ref, f32[64,128]{1,0:T(8,128)S(1)} %get-tuple-element.12.curve_ref, f32[32,128]{1,0:T(8,128)S(1)} %bitcast.25), custom_call_target="tpu_custom_call" | custom-call | flops 6000000000 | bytes 524288 | tf_op jit(solution)/shard_map/species/pallas_call | solution.py:141
  25.9 26.6 %all_to_all.16 = f32[16,192,128]{2,1,0:T(8,128)S(1)} all-to-all(f32[16,192,128]{2,1,0:T(8,128)S(1)} %bitcast.24), channel_id=1, replica_groups=mesh['z'=8,'x'=4,'y'=4,'core'=2] {'y','x'}, dimensions={0} | all-to-all | bytes 3145728 | tf_op jit(solution)/shard_map/all_to_all | solution.py:209
  52.5 2.7 %collective-permute-start = (f32[4,4,192,128]{3,2,1,0:T(8,128)S(1)}, f32[4,4,192,128]{3,2,1,0:T(8,128)S(1)}, u32[]{:S(2)}, u32[]{:S(2)}) collective-permute-start(f32[4,4,192,128]{3,2,1,0:T(8,128)S(1)} %bitcast.22), channel_id=1, source_target_pairs={{0,1},{1,0},{2,3},{3,2},{4,5},{5,4},{6,7},{7,6},{8,9},{9,8},{10,11... | collective-permute-start | bytes 4718600 | tf_op jit(solution)/shard_map/ppermute | solution.py:225
  55.1 1.2 %lay.2 = (f32[4,2,4,128,128]{4,3,2,1,0:T(8,128)}, f32[4,2,4,64,128]{4,3,2,1,0:T(8,128)}) custom-call(s32[1]{0:T(128)} %bitcast.core_ref, f32[4,4,192,128]{3,2,1,0:T(8,128)S(1)} %bitcast.23), custom_call_target="tpu_custom_call" | custom-call | flops 2000000000 | bytes 3145728 | tf_op jit(solution)/shard_map/lay/pallas_call | solution.py:191
  56.3 1.9 %collective-permute-done.blocks_ref = f32[4,4,192,128]{3,2,1,0:T(8,128)S(1)} collective-permute-done((f32[4,4,192,128]{3,2,1,0:T(8,128)S(1)}, f32[4,4,192,128]{3,2,1,0:T(8,128)S(1)}, u32[]{:S(2)}, u32[]{:S(2)}) %collective-permute-start) | collective-permute-done | bytes 1572896 | tf_op jit(solution)/shard_map/ppermute | solution.py:225
  58.2 1.2 %lay.3 = (f32[4,2,4,128,128]{4,3,2,1,0:T(8,128)}, f32[4,2,4,64,128]{4,3,2,1,0:T(8,128)}) custom-call(s32[1]{0:T(128)} %bitcast.core_ref, f32[4,4,192,128]{3,2,1,0:T(8,128)S(1)} %collective-permute-done.blocks_ref, f32[4,2,4,128,128]{4,3,2,1,0:T(8,128)} %get-tuple-element.6.refs_0_, ...), custom_call_target="tpu_custom_call", output_to_operand_aliasing={{0}: (2, {}), {1}: (3, {})} | custom-call | flops 2000000000 | bytes 3145728 | tf_op jit(solution)/shard_map/lay/pallas_call | solution.py:191
Async XLA Ops:
  0.6 0.7 %copy-start = (f32[64,16]{0,1:T(8,128)S(1)}, f32[64,16]{0,1:T(8,128)}, u32[]{:S(2)}) copy-start(f32[64,16]{0,1:T(8,128)} %param.9) | copy-start | bytes 12292
  2.1 20.4 %all-to-all-start = ((f32[32,1,128]{2,1,0:T(1,128)}), f32[32,1,128]{2,1,0:T(1,128)S(1)}, u32[]{:S(2)}, u32[]{:S(2)}) async-start(f32[32,1,128]{2,1,0:T(1,128)} %bitcast.7), calls=%async_computation | async-start | bytes 32768 | tf_op jit(solution)/shard_map/all_to_all | solution.py:209
  52.5 5.7 %collective-permute-start = (f32[4,4,192,128]{3,2,1,0:T(8,128)S(1)}, f32[4,4,192,128]{3,2,1,0:T(8,128)S(1)}, u32[]{:S(2)}, u32[]{:S(2)}) collective-permute-start(f32[4,4,192,128]{3,2,1,0:T(8,128)S(1)} %bitcast.22), channel_id=1, source_target_pairs={{0,1},{1,0},{2,3},{3,2},{4,5},{5,4},{6,7},{7,6},{8,9},{9,8},{10,11... | collective-permute-start | bytes 4718600 | tf_op jit(solution)/shard_map/ppermute | solution.py:225

commit v11 on v10

--- a/solution.py
+++ b/solution.py
@@ -150,22 +150,32 @@
     )(lam, curve, table)
 
 
-def blocks_kernel(table_ref, out_ref, turned_ref):
+def blocks_kernel(table_ref, out_ref, near_ref, turned_ref, block_ref, sems):
+    fetch = pltpu.make_async_copy(table_ref, near_ref, sems.at[0])
+    fetch.start()
+    fetch.wait()
     points = table_ref.shape[0]
-    turned_ref[:, :points] = jnp.transpose(table_ref[...])
+    turned_ref[:, :points] = jnp.transpose(near_ref[...])
     block = [turned_ref[pl.ds(q, 8, stride=8), :points] for q in range(8)]
     block = jnp.concatenate(block, axis=1)
-    out_ref[...] = jnp.broadcast_to(block[:, None, :], out_ref.shape)
+    block_ref[...] = jnp.broadcast_to(block[:, None, :], block_ref.shape)
+    store = pltpu.make_async_copy(block_ref, out_ref, sems.at[1])
+    store.start()
+    store.wait()
 
 
 def blocks(table):
     return pl.pallas_call(
         blocks_kernel,
         out_shape=jax.ShapeDtypeStruct((8, 4, LANES), jnp.float32),
-        in_specs=[pl.BlockSpec(memory_space=pltpu.VMEM)],
-        out_specs=pl.BlockSpec(memory_space=pltpu.VMEM),
-        scratch_shapes=[pltpu.VMEM((64, LANES), jnp.float32)],
-        compiler_params=pltpu.CompilerParams(vmem_limit_bytes=4 << 20),
+        in_specs=[pl.BlockSpec(memory_space=pl.ANY)],
+        out_specs=pl.BlockSpec(memory_space=pl.ANY),
+        scratch_shapes=[
+            pltpu.VMEM(table.shape, jnp.float32),
+            pltpu.VMEM((64, LANES), jnp.float32),
+            pltpu.VMEM((8, 4, LANES), jnp.float32),
+            pltpu.SemaphoreType.DMA((2,)),
+        ],
         name="blocks",
     )(table)
 

time: 59.7 us -> 59.7 us (level)
  Pallas kernels: 12.2 us -> 12.9 us
  local copies, waits for them, and re-layouts: 2.25 us -> 1.56 us
    pallas_call x1, Pallas kernels: 0.78 us -> 1.49 us  [blocks(): pl.pallas_call(blocks_kernel, out_shape=jax.ShapeDtypeStruct((8, 4, LANES...]
    unnamed x2 -> x0, local copies, waits for them, and re-layouts: 0.69 us -> none
where the time goes in v11:
time: 59.7 us; the launch traced here: 59.3 us
  blocking collectives  26.6 us (45%)
  starting transfers between devices  14.5 us (24%)
  Pallas kernels  12.9 us (22%)
  waiting for transfers between devices  3.07 us (5%)
  local copies, waits for them, and re-layouts  1.56 us (3%)
  between operations  0.68 us (1%)
    all_to_all x1, blocking collectives, exchange(): return lax.all_to_all(array, axes, split_axis=0, concat_axis=0, tiled=True)  26.6 us
    all_to_all x1, starting transfers between devices, exchange(): return lax.all_to_all(array, axes, split_axis=0, concat_axis=0, tiled=True)  11.9 us
    pallas_call x1, Pallas kernels, newton(): pl.pallas_call(newton_kernel, out_shape=jax.ShapeDtypeStruct(slope.shape,...  5.73 us
    pallas_call x1, Pallas kernels, species(): pl.pallas_call(species_kernel, out_shape=jax.ShapeDtypeStruct((4, 4, 3 *...  3.4 us
    ppermute x1, starting transfers between devices, per_device(): other = lax.ppermute(own, 'core', [(0, 1), (1, 0)])  2.66 us
    pallas_call x2, Pallas kernels, lay(): pl.pallas_call(functools.partial(lay_kernel, flip), out_shape=[jax.ShapeD...  2.31 us
    ppermute x1, waiting for transfers between devices, per_device(): other = lax.ppermute(own, 'core', [(0, 1), (1, 0)])  1.88 us
    reshape x2, local copies, waits for them, and re-layouts, per_device(): lax.dynamic_slice_in_dim(a, x * size, size, 0).reshape(-1, LANES)  1.56 us
  transfers between devices with their start and end apart: 2, of which 2 were waited for; matrix products, arithmetic and copies ran while one was open for 3% of the time, Pallas kernels for 12%

profile of v11, /device:TPU:1, one launch (start us, length us, event | category | flops | bytes accessed | tf_op | source)
XLA Modules:
  0.0 59.3 jit_solution(1231116928153289742)
XLA Ops:
  0.6 1.5 %blocks.1 = f32[8,4,128]{2,1,0:T(4,128)} custom-call(f32[16,64]{1,0:T(8,128)} %bitcast.27), custom_call_target="tpu_custom_call" | custom-call | tf_op jit(solution)/shard_map/blocks/pallas_call | solution.py:168
  2.1 11.9 %all-to-all-start = ((f32[32,1,128]{2,1,0:T(1,128)}), f32[32,1,128]{2,1,0:T(1,128)S(1)}, u32[]{:S(2)}, u32[]{:S(2)}) async-start(f32[32,1,128]{2,1,0:T(1,128)} %bitcast.26), calls=%async_computation | async-start | bytes 32768 | tf_op jit(solution)/shard_map/all_to_all | solution.py:219
  14.0 0.8 %dynamic-slice_bitcast_fusion.2 = (f32[64,128]{1,0:T(8,128)S(1)}, f32[64,128]{1,0:T(8,128)S(1)}) fusion(f32[32768]{0:T(1024)} %param.6, s32[]{:T(128)S(6)} %select_n.2, f32[32768]{0:T(1024)} %param.5), kind=kLoop, calls=%fused_computation.2 | loop fusion | bytes 131076 | tf_op jit(solution)/shard_map/reshape | solution.py:229
  14.8 0.8 %dynamic-slice_bitcast_fusion = (f32[64,128]{1,0:T(8,128)S(1)}, f32[64,128]{1,0:T(8,128)S(1)}) fusion(f32[32768]{0:T(1024)} %param.8, s32[]{:T(128)S(6)} %select_n.2, f32[32768]{0:T(1024)} %param.7), kind=kLoop, calls=%fused_computation | loop fusion | bytes 131076 | tf_op jit(solution)/shard_map/reshape | solution.py:229
  15.6 5.7 %newton.1.lam_ref = f32[64,128]{1,0:T(8,128)S(1)} custom-call(f32[64,128]{1,0:T(8,128)S(1)} %get-tuple-element.13.slope_ref, f32[64,128]{1,0:T(8,128)S(1)} %get-tuple-element.12.curve_ref, f32[64,128]{1,0:T(8,128)S(1)} %get-tuple-element.11.mean_ref, f32[64,128]{1,0:T(8,128)S(1)} %get-tuple-element.10.var_ref), custom_call_target="tpu_custom_call" | custom-call | flops 12000000000 | bytes 262144 | tf_op jit(solution)/shard_map/newton/pallas_call | solution.py:73
  21.3 1.2 %all-to-all-done = f32[32,1,128]{2,1,0:T(1,128)S(1)} async-done(((f32[32,1,128]{2,1,0:T(1,128)}), f32[32,1,128]{2,1,0:T(1,128)S(1)}, u32[]{:S(2)}, u32[]{:S(2)}) %all-to-all-start) | async-done | bytes 16416 | tf_op jit(solution)/shard_map/all_to_all | solution.py:219
  22.5 3.4 %species.1 = f32[4,4,192,128]{3,2,1,0:T(8,128)S(1)} custom-call(f32[64,128]{1,0:T(8,128)S(1)} %newton.1.lam_ref, f32[64,128]{1,0:T(8,128)S(1)} %get-tuple-element.12.curve_ref, f32[32,128]{1,0:T(8,128)S(1)} %bitcast.25), custom_call_target="tpu_custom_call" | custom-call | flops 6000000000 | bytes 524288 | tf_op jit(solution)/shard_map/species/pallas_call | solution.py:141
  25.9 26.6 %all_to_all.16 = f32[16,192,128]{2,1,0:T(8,128)S(1)} all-to-all(f32[16,192,128]{2,1,0:T(8,128)S(1)} %bitcast.24), channel_id=1, replica_groups=mesh['z'=8,'x'=4,'y'=4,'core'=2] {'y','x'}, dimensions={0} | all-to-all | bytes 3145728 | tf_op jit(solution)/shard_map/all_to_all | solution.py:219
  52.5 2.7 %collective-permute-start = (f32[4,4,192,128]{3,2,1,0:T(8,128)S(1)}, f32[4,4,192,128]{3,2,1,0:T(8,128)S(1)}, u32[]{:S(2)}, u32[]{:S(2)}) collective-permute-start(f32[4,4,192,128]{3,2,1,0:T(8,128)S(1)} %bitcast.22), channel_id=1, source_target_pairs={{0,1},{1,0},{2,3},{3,2},{4,5},{5,4},{6,7},{7,6},{8,9},{9,8},{10,11... | collective-permute-start | bytes 4718600 | tf_op jit(solution)/shard_map/ppermute | solution.py:235
  55.1 1.2 %lay.2 = (f32[4,2,4,128,128]{4,3,2,1,0:T(8,128)}, f32[4,2,4,64,128]{4,3,2,1,0:T(8,128)}) custom-call(s32[1]{0:T(128)} %bitcast.core_ref, f32[4,4,192,128]{3,2,1,0:T(8,128)S(1)} %bitcast.23), custom_call_target="tpu_custom_call" | custom-call | flops 2000000000 | bytes 3145728 | tf_op jit(solution)/shard_map/lay/pallas_call | solution.py:201
  56.3 1.9 %collective-permute-done.blocks_ref = f32[4,4,192,128]{3,2,1,0:T(8,128)S(1)} collective-permute-done((f32[4,4,192,128]{3,2,1,0:T(8,128)S(1)}, f32[4,4,192,128]{3,2,1,0:T(8,128)S(1)}, u32[]{:S(2)}, u32[]{:S(2)}) %collective-permute-start) | collective-permute-done | bytes 1572896 | tf_op jit(solution)/shard_map/ppermute | solution.py:235
  58.2 1.2 %lay.3 = (f32[4,2,4,128,128]{4,3,2,1,0:T(8,128)}, f32[4,2,4,64,128]{4,3,2,1,0:T(8,128)}) custom-call(s32[1]{0:T(128)} %bitcast.core_ref, f32[4,4,192,128]{3,2,1,0:T(8,128)S(1)} %collective-permute-done.blocks_ref, f32[4,2,4,128,128]{4,3,2,1,0:T(8,128)} %get-tuple-element.6.refs_0_, ...), custom_call_target="tpu_custom_call", output_to_operand_aliasing={{0}: (2, {}), {1}: (3, {})} | custom-call | flops 2000000000 | bytes 3145728 | tf_op jit(solution)/shard_map/lay/pallas_call | solution.py:201
Async XLA Ops:
  2.1 20.4 %all-to-all-start = ((f32[32,1,128]{2,1,0:T(1,128)}), f32[32,1,128]{2,1,0:T(1,128)S(1)}, u32[]{:S(2)}, u32[]{:S(2)}) async-start(f32[32,1,128]{2,1,0:T(1,128)} %bitcast.26), calls=%async_computation | async-start | bytes 32768 | tf_op jit(solution)/shard_map/all_to_all | solution.py:219
  52.5 5.7 %collective-permute-start = (f32[4,4,192,128]{3,2,1,0:T(8,128)S(1)}, f32[4,4,192,128]{3,2,1,0:T(8,128)S(1)}, u32[]{:S(2)}, u32[]{:S(2)}) collective-permute-start(f32[4,4,192,128]{3,2,1,0:T(8,128)S(1)} %bitcast.22), channel_id=1, source_target_pairs={{0,1},{1,0},{2,3},{3,2},{4,5},{5,4},{6,7},{7,6},{8,9},{9,8},{10,11... | collective-permute-start | bytes 4718600 | tf_op jit(solution)/shard_map/ppermute | solution.py:235

commit v12 on v10

--- a/solution.py
+++ b/solution.py
@@ -170,13 +170,14 @@
     )(table)
 
 
-def lay_kernel(flip, core_ref, blocks_ref, *refs):
+def lay_kernel(flip, first, core_ref, blocks_ref, *refs):
     species_ref, lam_ref, sems = refs[-3:]
     rows = lam_ref.shape[3]
     core = core_ref[0] ^ flip
+    here = pl.ds(first, blocks_ref.shape[0])
     copies = [
-        (blocks_ref.at[:, :, pl.ds(0, 2 * rows), :], species_ref.at[:, core]),
-        (blocks_ref.at[:, :, pl.ds(2 * rows, rows), :], lam_ref.at[:, core]),
+        (blocks_ref.at[:, :, pl.ds(0, 2 * rows), :], species_ref.at[here, core]),
+        (blocks_ref.at[:, :, pl.ds(2 * rows, rows), :], lam_ref.at[here, core]),
     ]
     started = [pltpu.make_async_copy(a, b, sems.at[i]) for i, (a, b) in enumerate(copies)]
     for copy in started:
@@ -185,11 +186,11 @@
         copy.wait()
 
 
-def lay(core, blocks, flip, laid=()):
+def lay(core, blocks, flip, first=0, laid=()):
     anywhere = pl.BlockSpec(memory_space=pl.ANY)
     rows = blocks.shape[2] // 3
     return pl.pallas_call(
-        functools.partial(lay_kernel, flip),
+        functools.partial(lay_kernel, flip, first),
         out_shape=[
             jax.ShapeDtypeStruct((4, 2, 4, 2 * rows, LANES), jnp.float32),
             jax.ShapeDtypeStruct((4, 2, 4, rows, LANES), jnp.float32),
@@ -222,8 +223,10 @@
     lam = newton(*mine)
     sent = species(lam, mine[1], points)
     own = exchange(sent.reshape(16, *sent.shape[2:]), ("y", "x")).reshape(sent.shape)
-    other = lax.ppermute(own, "core", [(0, 1), (1, 0)])
-    values, final_slope = lay(core, other, 1, lay(core, own, 0))
+    others = [lax.ppermute(own[y : y + 2], "core", [(0, 1), (1, 0)]) for y in (0, 2)]
+    laid = lay(core, own, 0)
+    laid = lay(core, others[0], 1, 0, laid)
+    values, final_slope = lay(core, others[1], 1, 2, laid)
     values = jnp.transpose(values.reshape(-1, 2, LANES), (1, 0, 2)).reshape(2, -1)
     return values, final_slope.reshape(-1)
 

time: 59.7 us -> 60.9 us (1.020)
  local copies, waits for them, and re-layouts: 2.25 us -> 3.52 us
  waiting for transfers between devices: 3.07 us -> 2.38 us
    slice x0 -> x1, local copies, waits for them, and re-layouts: none -> 1.26 us  [per_device(): own[y:y + 2]]
    ppermute x1 -> x2, waiting for transfers between devices: 1.88 us -> 1.18 us  [per_device(): lax.ppermute(own[y:y + 2], 'core', [(0, 1), (1, 0)])]
    pallas_call x2 -> x3, Pallas kernels: 2.31 us -> 2.94 us  [lay(): pl.pallas_call(functools.partial(lay_kernel, flip, first), out_shape=[jax...]
    ppermute x1 -> x2, starting transfers between devices: 2.66 us -> 2.66 us  [per_device(): lax.ppermute(own[y:y + 2], 'core', [(0, 1), (1, 0)])]
  transfers between devices with their start and end apart: 2 -> 3, of which waited for: 2 -> 3; matrix products, arithmetic and copies ran while one was open for 3% -> 3% of each run, Pallas kernels for 12% -> 13%
where the time goes in v12:
time: 60.9 us; the launch traced here: 60.5 us
  blocking collectives  26.6 us (44%)
  starting transfers between devices  14.5 us (24%)
  Pallas kernels  12.8 us (21%)
  local copies, waits for them, and re-layouts  3.52 us (6%)
  waiting for transfers between devices  2.38 us (4%)
  between operations  0.69 us (1%)
    all_to_all x1, blocking collectives, exchange(): return lax.all_to_all(array, axes, split_axis=0, concat_axis=0, tiled=True)  26.6 us
    all_to_all x1, starting transfers between devices, exchange(): return lax.all_to_all(array, axes, split_axis=0, concat_axis=0, tiled=True)  11.9 us
    pallas_call x1, Pallas kernels, newton(): pl.pallas_call(newton_kernel, out_shape=jax.ShapeDtypeStruct(slope.shape,...  5.73 us
    pallas_call x1, Pallas kernels, species(): pl.pallas_call(species_kernel, out_shape=jax.ShapeDtypeStruct((4, 4, 3 *...  3.4 us
    pallas_call x3, Pallas kernels, lay(): pl.pallas_call(functools.partial(lay_kernel, flip, first), out_shape=[jax...  2.94 us
    ppermute x2, starting transfers between devices, per_device(): lax.ppermute(own[y:y + 2], 'core', [(0, 1), (1, 0)])  2.66 us
    reshape x2, local copies, waits for them, and re-layouts, per_device(): lax.dynamic_slice_in_dim(a, x * size, size, 0).reshape(-1, LANES)  1.56 us
    slice x1, local copies, waits for them, and re-layouts, per_device(): own[y:y + 2]  1.26 us
  transfers between devices with their start and end apart: 3, of which 3 were waited for; matrix products, arithmetic and copies ran while one was open for 3% of the time, Pallas kernels for 13%

profile of v12, /device:TPU:1, one launch (start us, length us, event | category | flops | bytes accessed | tf_op | source)
XLA Modules:
  0.0 60.5 jit_solution(12453583906264601903)
XLA Ops:
  0.6 0.0 copy-start
  0.6 0.7 %copy-done = f32[64,16]{0,1:T(8,128)S(1)} copy-done((f32[64,16]{0,1:T(8,128)S(1)}, f32[64,16]{0,1:T(8,128)}, u32[]{:S(2)}) %copy-start) | copy-done | bytes 4120
  1.3 0.8 %blocks.1 = f32[8,4,128]{2,1,0:T(4,128)} custom-call(f32[16,64]{1,0:T(8,128)S(1)} %bitcast.27), custom_call_target="tpu_custom_call" | custom-call | tf_op jit(solution)/shard_map/blocks/pallas_call | solution.py:162
  2.1 11.9 %all-to-all-start = ((f32[32,1,128]{2,1,0:T(1,128)}), f32[32,1,128]{2,1,0:T(1,128)S(1)}, u32[]{:S(2)}, u32[]{:S(2)}) async-start(f32[32,1,128]{2,1,0:T(1,128)} %bitcast.7), calls=%async_computation | async-start | bytes 32768 | tf_op jit(solution)/shard_map/all_to_all | solution.py:210
  14.0 0.8 %dynamic-slice_bitcast_fusion.2 = (f32[64,128]{1,0:T(8,128)S(1)}, f32[64,128]{1,0:T(8,128)S(1)}) fusion(f32[32768]{0:T(1024)} %param.6, s32[]{:T(128)S(6)} %select_n.2, f32[32768]{0:T(1024)} %param.5), kind=kLoop, calls=%fused_computation.2 | loop fusion | bytes 131076 | tf_op jit(solution)/shard_map/reshape | solution.py:220
  14.8 0.8 %dynamic-slice_bitcast_fusion = (f32[64,128]{1,0:T(8,128)S(1)}, f32[64,128]{1,0:T(8,128)S(1)}) fusion(f32[32768]{0:T(1024)} %param.8, s32[]{:T(128)S(6)} %select_n.2, f32[32768]{0:T(1024)} %param.7), kind=kLoop, calls=%fused_computation | loop fusion | bytes 131076 | tf_op jit(solution)/shard_map/reshape | solution.py:220
  15.6 5.7 %newton.1.lam_ref = f32[64,128]{1,0:T(8,128)S(1)} custom-call(f32[64,128]{1,0:T(8,128)S(1)} %get-tuple-element.19.slope_ref, f32[64,128]{1,0:T(8,128)S(1)} %get-tuple-element.18.curve_ref, f32[64,128]{1,0:T(8,128)S(1)} %get-tuple-element.17.mean_ref, f32[64,128]{1,0:T(8,128)S(1)} %get-tuple-element.16.var_ref), custom_call_target="tpu_custom_call" | custom-call | flops 12000000000 | bytes 262144 | tf_op jit(solution)/shard_map/newton/pallas_call | solution.py:73
  21.3 1.2 %all-to-all-done = f32[32,1,128]{2,1,0:T(1,128)S(1)} async-done(((f32[32,1,128]{2,1,0:T(1,128)}), f32[32,1,128]{2,1,0:T(1,128)S(1)}, u32[]{:S(2)}, u32[]{:S(2)}) %all-to-all-start) | async-done | bytes 16416 | tf_op jit(solution)/shard_map/all_to_all | solution.py:210
  22.5 3.4 %species.1 = f32[4,4,192,128]{3,2,1,0:T(8,128)S(1)} custom-call(f32[64,128]{1,0:T(8,128)S(1)} %newton.1.lam_ref, f32[64,128]{1,0:T(8,128)S(1)} %get-tuple-element.18.curve_ref, f32[32,128]{1,0:T(8,128)S(1)} %bitcast.26), custom_call_target="tpu_custom_call" | custom-call | flops 6000000000 | bytes 524288 | tf_op jit(solution)/shard_map/species/pallas_call | solution.py:141
  25.9 26.6 %all_to_all.16 = f32[16,192,128]{2,1,0:T(8,128)S(1)} all-to-all(f32[16,192,128]{2,1,0:T(8,128)S(1)} %bitcast.25), channel_id=1, replica_groups=mesh['z'=8,'x'=4,'y'=4,'core'=2] {'y','x'}, dimensions={0} | all-to-all | bytes 3145728 | tf_op jit(solution)/shard_map/all_to_all | solution.py:210
  52.5 1.3 %fusion = (f32[8,192,128]{2,1,0:T(8,128)}, f32[8,192,128]{2,1,0:T(8,128)}) fusion(f32[16,192,128]{2,1,0:T(8,128)S(1)} %all_to_all.16), kind=kLoop, calls=%fused_computation.4 | loop fusion | bytes 3145728 | tf_op jit(solution)/shard_map/slice | solution.py:226
  53.7 2.7 %collective-permute-start.1 = (f32[2,4,192,128]{3,2,1,0:T(8,128)}, f32[2,4,192,128]{3,2,1,0:T(8,128)S(1)}, u32[]{:S(2)}, u32[]{:S(2)}) collective-permute-start(f32[2,4,192,128]{3,2,1,0:T(8,128)} %bitcast.11), channel_id=1, source_target_pairs={{0,1},{1,0},{2,3},{3,2},{4,5},{5,4},{6,7},{7,6},{8,9},{9,8},{10,11... | collective-permute-start | bytes 2359304 | tf_op jit(solution)/shard_map/ppermute | solution.py:226
  56.4 0.0 collective-permute-start
  56.4 1.2 %lay.3 = (f32[4,2,4,128,128]{4,3,2,1,0:T(8,128)}, f32[4,2,4,64,128]{4,3,2,1,0:T(8,128)}) custom-call(s32[1]{0:T(128)} %bitcast.core_ref, f32[4,4,192,128]{3,2,1,0:T(8,128)S(1)} %bitcast.24), custom_call_target="tpu_custom_call" | custom-call | flops 2000000000 | bytes 3145728 | tf_op jit(solution)/shard_map/lay/pallas_call | solution.py:192
  57.5 1.0 %collective-permute-done.1.blocks_ref = f32[2,4,192,128]{3,2,1,0:T(8,128)S(1)} collective-permute-done((f32[2,4,192,128]{3,2,1,0:T(8,128)}, f32[2,4,192,128]{3,2,1,0:T(8,128)S(1)}, u32[]{:S(2)}, u32[]{:S(2)}) %collective-permute-start.1) | collective-permute-done | bytes 786464 | tf_op jit(solution)/shard_map/ppermute | solution.py:226
  58.5 0.9 %lay.4 = (f32[4,2,4,128,128]{4,3,2,1,0:T(8,128)}, f32[4,2,4,64,128]{4,3,2,1,0:T(8,128)}) custom-call(s32[1]{0:T(128)} %bitcast.core_ref, f32[2,4,192,128]{3,2,1,0:T(8,128)S(1)} %collective-permute-done.1.blocks_ref, f32[4,2,4,128,128]{4,3,2,1,0:T(8,128)} %get-tuple-element.8.refs_0_, ...), custom_call_target="tpu_custom_call", output_to_operand_aliasing={{0}: (2, {}), {1}: (3, {})} | custom-call | flops 2000000000 | bytes 3145728 | tf_op jit(solution)/shard_map/lay/pallas_call | solution.py:192
  59.4 0.2 collective-permute-done.blocks_ref
  59.6 0.9 %lay.5 = (f32[4,2,4,128,128]{4,3,2,1,0:T(8,128)}, f32[4,2,4,64,128]{4,3,2,1,0:T(8,128)}) custom-call(s32[1]{0:T(128)} %bitcast.core_ref, f32[2,4,192,128]{3,2,1,0:T(8,128)S(1)} %collective-permute-done.blocks_ref, f32[4,2,4,128,128]{4,3,2,1,0:T(8,128)} %get-tuple-element.10.refs_0_, ...), custom_call_target="tpu_custom_call", output_to_operand_aliasing={{0}: (2, {}), {1}: (3, {})} | custom-call | flops 2000000000 | bytes 3145728 | tf_op jit(solution)/shard_map/lay/pallas_call | solution.py:192
Async XLA Ops:
  0.6 0.7 %copy-start = (f32[64,16]{0,1:T(8,128)S(1)}, f32[64,16]{0,1:T(8,128)}, u32[]{:S(2)}) copy-start(f32[64,16]{0,1:T(8,128)} %param.9) | copy-start | bytes 12292
  2.1 20.4 %all-to-all-start = ((f32[32,1,128]{2,1,0:T(1,128)}), f32[32,1,128]{2,1,0:T(1,128)S(1)}, u32[]{:S(2)}, u32[]{:S(2)}) async-start(f32[32,1,128]{2,1,0:T(1,128)} %bitcast.7), calls=%async_computation | async-start | bytes 32768 | tf_op jit(solution)/shard_map/all_to_all | solution.py:210
  53.7 4.8 %collective-permute-start.1 = (f32[2,4,192,128]{3,2,1,0:T(8,128)}, f32[2,4,192,128]{3,2,1,0:T(8,128)S(1)}, u32[]{:S(2)}, u32[]{:S(2)}) collective-permute-start(f32[2,4,192,128]{3,2,1,0:T(8,128)} %bitcast.11), channel_id=1, source_target_pairs={{0,1},{1,0},{2,3},{3,2},{4,5},{5,4},{6,7},{7,6},{8,9},{9,8},{10,11... | collective-permute-start | bytes 2359304 | tf_op jit(solution)/shard_map/ppermute | solution.py:226
  56.4 3.2 %collective-permute-start = (f32[2,4,192,128]{3,2,1,0:T(8,128)}, f32[2,4,192,128]{3,2,1,0:T(8,128)S(1)}, u32[]{:S(2)}, u32[]{:S(2)}) collective-permute-start(f32[2,4,192,128]{3,2,1,0:T(8,128)} %bitcast.10), channel_id=1, source_target_pairs={{0,1},{1,0},{2,3},{3,2},{4,5},{5,4},{6,7},{7,6},{8,9},{9,8},{10,11... | collective-permute-start | bytes 2359304 | tf_op jit(solution)/shard_map/ppermute | solution.py:226

commit v13 on v7

--- a/solution.py
+++ b/solution.py
@@ -102,7 +102,7 @@
         high_ref[t], low_ref[t] = weights(lam_ref, curve_ref, t)
         return 0
 
-    lax.fori_loop(0, EARLY, early, 0, unroll=EARLY // 2)
+    lax.fori_loop(0, EARLY, early, 0, unroll=EARLY)
 
 
 def newton(slope, curve, mean, var):
@@ -124,12 +124,13 @@
     turned_ref[...] = jnp.transpose(table_ref[...])
     table = jnp.concatenate([turned_ref[pl.ds(p, 8, stride=16), :] for p in range(16)], axis=1)
     high = table.astype(jnp.bfloat16).astype(jnp.float32)
-    ones = jnp.ones((16, table.shape[1]), jnp.float32)
-    left = jnp.concatenate([high, table - high, ones], axis=0).astype(jnp.bfloat16)
+    ones = jnp.ones((8, table.shape[1]), jnp.float32)
+    for_high = jnp.concatenate([high, ones, table - high], axis=0).astype(jnp.bfloat16)
+    for_low = jnp.concatenate([high, ones], axis=0).astype(jnp.bfloat16)
     def pair(high, low):
-        sums = jnp.dot(left, high, preferred_element_type=jnp.float32)
-        sums = sums + jnp.dot(left, low, preferred_element_type=jnp.float32)
-        values = (sums[0:8] + sums[8:16]) / sums[16:24]
+        sums = jnp.dot(for_high, high, preferred_element_type=jnp.float32)
+        more = jnp.dot(for_low, low, preferred_element_type=jnp.float32)
+        values = (sums[0:8] + sums[16:24] + more[0:8]) / (sums[8:16] + more[8:16])
         return [values[:, :LANES], values[:, LANES:]]
 
     def store(t, values):
@@ -154,8 +155,7 @@
             sent_ref[x, y, 2 * rows :, :] = lam_ref[...]
     first = EARLY // 2
     lax.fori_loop(0, first, early, 0, unroll=first)
-    late(first, 0)
-    lax.fori_loop(first + 1, rows // 4, late, 0, unroll=4)
+    lax.fori_loop(first, rows // 4, late, 0, unroll=13)
 
 
 def species(lam, curve, early, table):
@@ -187,6 +187,7 @@
         in_specs=[pl.BlockSpec(memory_space=pltpu.VMEM)],
         out_specs=pl.BlockSpec(memory_space=pltpu.VMEM),
         scratch_shapes=[pltpu.VMEM((64, LANES), jnp.float32)],
+        compiler_params=pltpu.CompilerParams(vmem_limit_bytes=4 << 20),
         name="blocks",
     )(table)
 

time: 61.3 us -> 60.1 us (0.980)
  Pallas kernels: 14.8 us -> 12.8 us
  local copies, waits for them, and re-layouts: 1.57 us -> 2.29 us
    pallas_call x1, Pallas kernels: 4.51 us -> 3.24 us  [species(): pl.pallas_call(species_kernel, out_shape=jax.ShapeDtypeStruct((4, 4, 3 *...]
    pallas_call x1, Pallas kernels: 1.51 us -> 0.78 us  [blocks(): pl.pallas_call(blocks_kernel, out_shape=jax.ShapeDtypeStruct((8, 4, LANES...]
    unnamed x2 -> x4, local copies, waits for them, and re-layouts: 0.01 us -> 0.73 us
  transfers between devices with their start and end apart: 2 -> 2, of which waited for: 2 -> 2; matrix products, arithmetic and copies ran while one was open for 3% -> 3% of each run, Pallas kernels for 12% -> 13%
where the time goes in v13:
time: 60.1 us; the launch traced here: 59.7 us
  blocking collectives  26.2 us (44%)
  starting transfers between devices  15.4 us (26%)
  Pallas kernels  12.8 us (21%)
  waiting for transfers between devices  2.35 us (4%)
  local copies, waits for them, and re-layouts  2.29 us (4%)
  between operations  0.7 us (1%)
    all_to_all x1, blocking collectives, exchange(): return lax.all_to_all(array, axes, split_axis=0, concat_axis=0, tiled=True)  26.2 us
    all_to_all x1, starting transfers between devices, exchange(): return lax.all_to_all(array, axes, split_axis=0, concat_axis=0, tiled=True)  11.9 us
    pallas_call x1, Pallas kernels, newton(): pl.pallas_call(newton_kernel, out_shape=[jax.ShapeDtypeStruct(slope.shape...  6.4 us
    ppermute x1, starting transfers between devices, per_device(): other = lax.ppermute(own, 'core', [(0, 1), (1, 0)])  3.53 us
    pallas_call x1, Pallas kernels, species(): pl.pallas_call(species_kernel, out_shape=jax.ShapeDtypeStruct((4, 4, 3 *...  3.24 us
    pallas_call x2, Pallas kernels, lay(): pl.pallas_call(functools.partial(lay_kernel, flip), out_shape=[jax.ShapeD...  2.39 us
    ppermute x1, waiting for transfers between devices, per_device(): other = lax.ppermute(own, 'core', [(0, 1), (1, 0)])  1.83 us
    reshape x3, local copies, waits for them, and re-layouts, per_device(): lax.dynamic_slice_in_dim(a, x * size, size, 0).reshape(-1, LANES)  1.56 us
  transfers between devices with their start and end apart: 2, of which 2 were waited for; matrix products, arithmetic and copies ran while one was open for 3% of the time, Pallas kernels for 13%

profile of v13, /device:TPU:1, one launch (start us, length us, event | category | flops | bytes accessed | tf_op | source)
XLA Modules:
  0.0 59.7 jit_solution(16073777133749374533)
XLA Ops:
  0.6 0.0 copy-start
  0.6 0.0 copy-start.1
  0.7 0.7 %copy-done.1 = f32[64,16]{0,1:T(8,128)S(1)} copy-done((f32[64,16]{0,1:T(8,128)S(1)}, f32[64,16]{0,1:T(8,128)}, u32[]{:S(2)}) %copy-start.1) | copy-done | bytes 4120
  1.4 0.8 %blocks.1 = f32[8,4,128]{2,1,0:T(4,128)} custom-call(f32[16,64]{1,0:T(8,128)S(1)} %bitcast.26), custom_call_target="tpu_custom_call" | custom-call | tf_op jit(solution)/shard_map/blocks/pallas_call | solution.py:184
  2.2 11.9 %all-to-all-start = ((f32[32,1,128]{2,1,0:T(1,128)}), f32[32,1,128]{2,1,0:T(1,128)S(1)}, u32[]{:S(2)}, u32[]{:S(2)}) async-start(f32[32,1,128]{2,1,0:T(1,128)} %bitcast.7), calls=%async_computation | async-start | bytes 32768 | tf_op jit(solution)/shard_map/all_to_all | solution.py:231
  14.0 0.0 copy-done
  14.1 0.8 %dynamic-slice_bitcast_fusion.3.slope_ref = f32[64,128]{1,0:T(8,128)S(1)} fusion(f32[32768]{0:T(1024)} %param.5, s32[]{:T(128)S(6)} %select_n.2), kind=kLoop, calls=%fused_computation.3 | loop fusion | bytes 65540 | tf_op jit(solution)/shard_map/reshape | solution.py:241
  14.8 0.8 %dynamic-slice_bitcast_fusion = (f32[64,128]{1,0:T(8,128)S(1)}, f32[64,128]{1,0:T(8,128)S(1)}) fusion(f32[32768]{0:T(1024)} %param.8, s32[]{:T(128)S(6)} %select_n.2, f32[32768]{0:T(1024)} %param.7), kind=kLoop, calls=%fused_computation | loop fusion | bytes 131076 | tf_op jit(solution)/shard_map/reshape | solution.py:241
  15.6 6.4 %newton.1 = (f32[64,128]{1,0:T(8,128)S(1)}, bf16[6,512,256]{2,1,0:T(8,128)(2,1)S(1)}, bf16[6,512,256]{2,1,0:T(8,128)(2,1)S(1)}) custom-call(f32[64,128]{1,0:T(8,128)S(1)} %dynamic-slice_bitcast_fusion.3.slope_ref, f32[64,128]{1,0:T(8,128)S(1)} %dynamic-slice_bitcast_fusion.2.curve_ref, f32[64,128]{1,0:T(8,128)S(1)} %get-tuple-element.17.mean_ref, ...), custom_call_target="tpu_custom_call" | custom-call | flops 12000000000 | bytes 262144 | tf_op jit(solution)/shard_map/newton/pallas_call | solution.py:110
  22.0 0.5 all-to-all-done
  22.5 3.2 %species.1 = f32[4,4,192,128]{3,2,1,0:T(8,128)S(1)} custom-call(f32[64,128]{1,0:T(8,128)S(1)} %get-tuple-element.9.lam_ref, f32[64,128]{1,0:T(8,128)S(1)} %dynamic-slice_bitcast_fusion.2.curve_ref, bf16[6,512,256]{2,1,0:T(8,128)(2,1)S(1)} %get-tuple-element.10.high_ref, bf16[6,512,256]{2,1,0:T(8,128)(2,1)S(1)} %get-tuple-element.11.low_ref, ...), custom_call_target="tpu_custom_call" | custom-call | flops 6000000000 | bytes 524288 | tf_op jit(solution)/shard_map/species/pallas_call | solution.py:163
  25.8 26.2 %all_to_all.16 = f32[16,192,128]{2,1,0:T(8,128)S(1)} all-to-all(f32[16,192,128]{2,1,0:T(8,128)S(1)} %bitcast.24), channel_id=1, replica_groups=mesh['z'=8,'x'=4,'y'=4,'core'=2] {'x','y'}, dimensions={0} | all-to-all | bytes 3145728 | tf_op jit(solution)/shard_map/all_to_all | solution.py:231
  52.0 3.5 %collective-permute-start = (f32[4,4,192,128]{3,2,1,0:T(8,128)S(1)}, f32[4,4,192,128]{3,2,1,0:T(8,128)S(1)}, u32[]{:S(2)}, u32[]{:S(2)}) collective-permute-start(f32[4,4,192,128]{3,2,1,0:T(8,128)S(1)} %bitcast.22), channel_id=1, source_target_pairs={{0,1},{1,0},{2,3},{3,2},{4,5},{5,4},{6,7},{7,6},{8,9},{9,8},{10,11... | collective-permute-start | bytes 4718600 | tf_op jit(solution)/shard_map/ppermute | solution.py:247
  55.5 1.2 %lay.2 = (f32[4,2,4,128,128]{4,3,2,1,0:T(8,128)}, f32[4,2,4,64,128]{4,3,2,1,0:T(8,128)}) custom-call(s32[1]{0:T(128)} %bitcast.core_ref, f32[4,4,192,128]{3,2,1,0:T(8,128)S(1)} %bitcast.23), custom_call_target="tpu_custom_call" | custom-call | flops 2000000000 | bytes 3145728 | tf_op jit(solution)/shard_map/lay/pallas_call | solution.py:213
  56.7 1.8 %collective-permute-done.blocks_ref = f32[4,4,192,128]{3,2,1,0:T(8,128)S(1)} collective-permute-done((f32[4,4,192,128]{3,2,1,0:T(8,128)S(1)}, f32[4,4,192,128]{3,2,1,0:T(8,128)S(1)}, u32[]{:S(2)}, u32[]{:S(2)}) %collective-permute-start) | collective-permute-done | bytes 1572896 | tf_op jit(solution)/shard_map/ppermute | solution.py:247
  58.5 1.2 %lay.3 = (f32[4,2,4,128,128]{4,3,2,1,0:T(8,128)}, f32[4,2,4,64,128]{4,3,2,1,0:T(8,128)}) custom-call(s32[1]{0:T(128)} %bitcast.core_ref, f32[4,4,192,128]{3,2,1,0:T(8,128)S(1)} %collective-permute-done.blocks_ref, f32[4,2,4,128,128]{4,3,2,1,0:T(8,128)} %get-tuple-element.12.refs_0_, ...), custom_call_target="tpu_custom_call", output_to_operand_aliasing={{0}: (2, {}), {1}: (3, {})} | custom-call | flops 2000000000 | bytes 3145728 | tf_op jit(solution)/shard_map/lay/pallas_call | solution.py:213
  (1 shorter events, 0.0 us)
Async XLA Ops:
  0.6 13.4 %copy-start = (f32[32768]{0:T(1024)S(1)}, f32[32768]{0:T(1024)}, u32[]{:S(2)}) copy-start(f32[32768]{0:T(1024)} %param.6) | copy-start | bytes 393220
  0.6 0.7 %copy-start.1 = (f32[64,16]{0,1:T(8,128)S(1)}, f32[64,16]{0,1:T(8,128)}, u32[]{:S(2)}) copy-start(f32[64,16]{0,1:T(8,128)} %param.9) | copy-start | bytes 12292
  2.2 20.4 %all-to-all-start = ((f32[32,1,128]{2,1,0:T(1,128)}), f32[32,1,128]{2,1,0:T(1,128)S(1)}, u32[]{:S(2)}, u32[]{:S(2)}) async-start(f32[32,1,128]{2,1,0:T(1,128)} %bitcast.7), calls=%async_computation | async-start | bytes 32768 | tf_op jit(solution)/shard_map/all_to_all | solution.py:231
  52.0 6.6 %collective-permute-start = (f32[4,4,192,128]{3,2,1,0:T(8,128)S(1)}, f32[4,4,192,128]{3,2,1,0:T(8,128)S(1)}, u32[]{:S(2)}, u32[]{:S(2)}) collective-permute-start(f32[4,4,192,128]{3,2,1,0:T(8,128)S(1)} %bitcast.22), channel_id=1, source_target_pairs={{0,1},{1,0},{2,3},{3,2},{4,5},{5,4},{6,7},{7,6},{8,9},{9,8},{10,11... | collective-permute-start | bytes 4718600 | tf_op jit(solution)/shard_map/ppermute | solution.py:247

commit v14 on v9

--- a/solution.py
+++ b/solution.py
@@ -63,7 +63,7 @@
                     up, down = up * up2, down * down2
             return lam + (mean - (0.5 + moment / partition)) * inverse
 
-        lam_ref[rows, :] = lax.fori_loop(0, ITERS, newton, slope_ref[rows, :])
+        lam_ref[rows, :] = lax.fori_loop(0, ITERS, newton, slope_ref[rows, :], unroll=ITERS)
         return 0
 
     lax.fori_loop(0, lam_ref.shape[0] // 8, body, 0)

time: 59.5 us -> 60.3 us (1.013)
  Pallas kernels: 12.3 us -> 13.1 us
  waiting for transfers between devices: 3.03 us -> 2.28 us
    pallas_call x1, Pallas kernels: 5.73 us -> 6.48 us  [newton(): pl.pallas_call(newton_kernel, out_shape=jax.ShapeDtypeStruct(slope.shape,...]
    all_to_all x1, waiting for transfers between devices: 1.2 us -> 0.45 us  [exchange(): return lax.all_to_all(array, axes, split_axis=0, concat_axis=0, tiled=True)]
  transfers between devices with their start and end apart: 2 -> 2, of which waited for: 2 -> 2; matrix products, arithmetic and copies ran while one was open for 3% -> 3% of each run, Pallas kernels for 12% -> 13%
where the time goes in v14:
time: 60.3 us; the launch traced here: 59.9 us
  blocking collectives  26.3 us (44%)
  starting transfers between devices  15.4 us (26%)
  Pallas kernels  13.1 us (22%)
  waiting for transfers between devices  2.28 us (4%)
  local copies, waits for them, and re-layouts  2.25 us (4%)
  between operations  0.68 us (1%)
    all_to_all x1, blocking collectives, exchange(): return lax.all_to_all(array, axes, split_axis=0, concat_axis=0, tiled=True)  26.3 us
    all_to_all x1, starting transfers between devices, exchange(): return lax.all_to_all(array, axes, split_axis=0, concat_axis=0, tiled=True)  11.9 us
    pallas_call x1, Pallas kernels, newton(): pl.pallas_call(newton_kernel, out_shape=jax.ShapeDtypeStruct(slope.shape,...  6.48 us
    ppermute x1, starting transfers between devices, per_device(): other = lax.ppermute(own, 'core', [(0, 1), (1, 0)])  3.53 us
    pallas_call x1, Pallas kernels, species(): pl.pallas_call(species_kernel, out_shape=jax.ShapeDtypeStruct((4, 4, 3 *...  3.4 us
    pallas_call x2, Pallas kernels, lay(): pl.pallas_call(functools.partial(lay_kernel, flip), out_shape=[jax.ShapeD...  2.39 us
    ppermute x1, waiting for transfers between devices, per_device(): other = lax.ppermute(own, 'core', [(0, 1), (1, 0)])  1.83 us
    reshape x2, local copies, waits for them, and re-layouts, per_device(): lax.dynamic_slice_in_dim(a, x * size, size, 0).reshape(-1, LANES)  1.56 us
  transfers between devices with their start and end apart: 2, of which 2 were waited for; matrix products, arithmetic and copies ran while one was open for 3% of the time, Pallas kernels for 13%

profile of v14, /device:TPU:1, one launch (start us, length us, event | category | flops | bytes accessed | tf_op | source)
XLA Modules:
  0.0 59.9 jit_solution(3311514583138256327)
XLA Ops:
  0.6 0.0 copy-start
  0.6 0.7 %copy-done = f32[64,16]{0,1:T(8,128)S(1)} copy-done((f32[64,16]{0,1:T(8,128)S(1)}, f32[64,16]{0,1:T(8,128)}, u32[]{:S(2)}) %copy-start) | copy-done | bytes 4120
  1.3 0.8 %blocks.1 = f32[8,4,128]{2,1,0:T(4,128)} custom-call(f32[16,64]{1,0:T(8,128)S(1)} %bitcast.26), custom_call_target="tpu_custom_call" | custom-call | tf_op jit(solution)/shard_map/blocks/pallas_call | solution.py:162
  2.1 11.9 %all-to-all-start = ((f32[32,1,128]{2,1,0:T(1,128)}), f32[32,1,128]{2,1,0:T(1,128)S(1)}, u32[]{:S(2)}, u32[]{:S(2)}) async-start(f32[32,1,128]{2,1,0:T(1,128)} %bitcast.7), calls=%async_computation | async-start | bytes 32768 | tf_op jit(solution)/shard_map/all_to_all | solution.py:209
  14.0 0.8 %dynamic-slice_bitcast_fusion.2 = (f32[64,128]{1,0:T(8,128)S(1)}, f32[64,128]{1,0:T(8,128)S(1)}) fusion(f32[32768]{0:T(1024)} %param.6, s32[]{:T(128)S(6)} %select_n.2, f32[32768]{0:T(1024)} %param.5), kind=kLoop, calls=%fused_computation.2 | loop fusion | bytes 131076 | tf_op jit(solution)/shard_map/reshape | solution.py:219
  14.8 0.8 %dynamic-slice_bitcast_fusion = (f32[64,128]{1,0:T(8,128)S(1)}, f32[64,128]{1,0:T(8,128)S(1)}) fusion(f32[32768]{0:T(1024)} %param.8, s32[]{:T(128)S(6)} %select_n.2, f32[32768]{0:T(1024)} %param.7), kind=kLoop, calls=%fused_computation | loop fusion | bytes 131076 | tf_op jit(solution)/shard_map/reshape | solution.py:219
  15.6 6.5 %newton.1.lam_ref = f32[64,128]{1,0:T(8,128)S(1)} custom-call(f32[64,128]{1,0:T(8,128)S(1)} %get-tuple-element.13.slope_ref, f32[64,128]{1,0:T(8,128)S(1)} %get-tuple-element.12.curve_ref, f32[64,128]{1,0:T(8,128)S(1)} %get-tuple-element.11.mean_ref, f32[64,128]{1,0:T(8,128)S(1)} %get-tuple-element.10.var_ref), custom_call_target="tpu_custom_call" | custom-call | flops 12000000000 | bytes 262144 | tf_op jit(solution)/shard_map/newton/pallas_call | solution.py:73
  22.0 0.4 all-to-all-done
  22.5 3.4 %species.1 = f32[4,4,192,128]{3,2,1,0:T(8,128)S(1)} custom-call(f32[64,128]{1,0:T(8,128)S(1)} %newton.1.lam_ref, f32[64,128]{1,0:T(8,128)S(1)} %get-tuple-element.12.curve_ref, f32[32,128]{1,0:T(8,128)S(1)} %bitcast.25), custom_call_target="tpu_custom_call" | custom-call | flops 6000000000 | bytes 524288 | tf_op jit(solution)/shard_map/species/pallas_call | solution.py:141
  25.9 26.3 %all_to_all.16 = f32[16,192,128]{2,1,0:T(8,128)S(1)} all-to-all(f32[16,192,128]{2,1,0:T(8,128)S(1)} %bitcast.24), channel_id=1, replica_groups=mesh['z'=8,'x'=4,'y'=4,'core'=2] {'x','y'}, dimensions={0} | all-to-all | bytes 3145728 | tf_op jit(solution)/shard_map/all_to_all | solution.py:209
  52.2 3.5 %collective-permute-start = (f32[4,4,192,128]{3,2,1,0:T(8,128)S(1)}, f32[4,4,192,128]{3,2,1,0:T(8,128)S(1)}, u32[]{:S(2)}, u32[]{:S(2)}) collective-permute-start(f32[4,4,192,128]{3,2,1,0:T(8,128)S(1)} %bitcast.22), channel_id=1, source_target_pairs={{0,1},{1,0},{2,3},{3,2},{4,5},{5,4},{6,7},{7,6},{8,9},{9,8},{10,11... | collective-permute-start | bytes 4718600 | tf_op jit(solution)/shard_map/ppermute | solution.py:225
  55.7 1.2 %lay.2 = (f32[4,2,4,128,128]{4,3,2,1,0:T(8,128)}, f32[4,2,4,64,128]{4,3,2,1,0:T(8,128)}) custom-call(s32[1]{0:T(128)} %bitcast.core_ref, f32[4,4,192,128]{3,2,1,0:T(8,128)S(1)} %bitcast.23), custom_call_target="tpu_custom_call" | custom-call | flops 2000000000 | bytes 3145728 | tf_op jit(solution)/shard_map/lay/pallas_call | solution.py:191
  56.9 1.8 %collective-permute-done.blocks_ref = f32[4,4,192,128]{3,2,1,0:T(8,128)S(1)} collective-permute-done((f32[4,4,192,128]{3,2,1,0:T(8,128)S(1)}, f32[4,4,192,128]{3,2,1,0:T(8,128)S(1)}, u32[]{:S(2)}, u32[]{:S(2)}) %collective-permute-start) | collective-permute-done | bytes 1572896 | tf_op jit(solution)/shard_map/ppermute | solution.py:225
  58.7 1.2 %lay.3 = (f32[4,2,4,128,128]{4,3,2,1,0:T(8,128)}, f32[4,2,4,64,128]{4,3,2,1,0:T(8,128)}) custom-call(s32[1]{0:T(128)} %bitcast.core_ref, f32[4,4,192,128]{3,2,1,0:T(8,128)S(1)} %collective-permute-done.blocks_ref, f32[4,2,4,128,128]{4,3,2,1,0:T(8,128)} %get-tuple-element.6.refs_0_, ...), custom_call_target="tpu_custom_call", output_to_operand_aliasing={{0}: (2, {}), {1}: (3, {})} | custom-call | flops 2000000000 | bytes 3145728 | tf_op jit(solution)/shard_map/lay/pallas_call | solution.py:191
Async XLA Ops:
  0.6 0.7 %copy-start = (f32[64,16]{0,1:T(8,128)S(1)}, f32[64,16]{0,1:T(8,128)}, u32[]{:S(2)}) copy-start(f32[64,16]{0,1:T(8,128)} %param.9) | copy-start | bytes 12292
  2.1 20.4 %all-to-all-start = ((f32[32,1,128]{2,1,0:T(1,128)}), f32[32,1,128]{2,1,0:T(1,128)S(1)}, u32[]{:S(2)}, u32[]{:S(2)}) async-start(f32[32,1,128]{2,1,0:T(1,128)} %bitcast.7), calls=%async_computation | async-start | bytes 32768 | tf_op jit(solution)/shard_map/all_to_all | solution.py:209
  52.2 6.6 %collective-permute-start = (f32[4,4,192,128]{3,2,1,0:T(8,128)S(1)}, f32[4,4,192,128]{3,2,1,0:T(8,128)S(1)}, u32[]{:S(2)}, u32[]{:S(2)}) collective-permute-start(f32[4,4,192,128]{3,2,1,0:T(8,128)S(1)} %bitcast.22), channel_id=1, source_target_pairs={{0,1},{1,0},{2,3},{3,2},{4,5},{5,4},{6,7},{7,6},{8,9},{9,8},{10,11... | collective-permute-start | bytes 4718600 | tf_op jit(solution)/shard_map/ppermute | solution.py:225
